TPU v7x, 512 devices: a whole 4x4x16 slice. The times are simulated.
512 devices in a mesh: dp: 64 (over z_lo, x, core), mp: 8 (over z_hi, y).
Axes of the slice: x: 4, y: 4, z: 16 (z_hi: 2, z_lo: 8; z = z_hi * 8 + z_lo), core: 2. Of those that a mesh axis runs over, the one named last changes fastest.
Arguments:
- inputs: bfloat16 [1024, 6144], P('dp', 'mp'), may hold values from -6 to 6
- targets: bfloat16 [1024, 6144], P('dp', 'mp'), may hold values from -6 to 6
- w_in: bfloat16 [6144, 16384], P('mp', 'dp'), may hold values from -6 to 6
- w_out: bfloat16 [16384, 6144], P('dp', 'mp'), may hold values from -6 to 6
- teach_in: float32 [6144, 16384], P('mp', 'dp'), may hold values from -6 to 6
- teach_out: float32 [16384, 6144], P('dp', 'mp'), may hold values from -6 to 6
Outputs:
- grad_in: bfloat16 [6144, 16384], P('mp', 'dp')
- grad_out: bfloat16 [16384, 6144], P('dp', 'mp')
- new_in: float32 [6144, 16384], P('mp', 'dp')
- new_out: float32 [16384, 6144], P('dp', 'mp')
All inputs are finite; a program needn't handle non-finite values.
Results may differ from a plain program's by a relative error of at most 0.017.
Values may be sent and summed in bfloat16 or wider, within the bound.
No kernel may reach another device: no remote copies, remote signals or barrier semaphores. Data moves between devices by JAX's collectives and lax.ppermute only.
A program may use at most 64 MiB of HBM per device.

v0:
```python
import math

import jax
import jax.numpy as jnp
from jax import lax
from jax.sharding import Mesh
from jax.sharding import PartitionSpec as P

D = 6144
FF = 16384
DP = ("dp_0", "dp_1", "dp_2")


decay_rate = 0.99
step_size = 0.5


def from_everyone(value, axis):
    copies = jnp.broadcast_to(value, (lax.axis_size(axis), *value.shape))
    return lax.all_to_all(copies, axis, split_axis=0, concat_axis=0, tiled=True)


def in_order(pieces, dim):
    pieces = jnp.moveaxis(pieces, 0, dim)
    dims = pieces.shape
    return pieces.reshape(*dims[:dim], dims[dim] * dims[dim + 1], *dims[dim + 2 :])


def gather_axes(value, axes, dim):
    far, near = axes
    pieces = from_everyone(from_everyone(value, far), near)
    return in_order(pieces.swapaxes(0, 1).reshape(-1, *value.shape), dim)


def cut_along(value, dim, size):
    before, after = (value.shape[:dim], value.shape[dim + 1 :])
    return jnp.moveaxis(value.reshape(*before, size, -1, *after), dim, 0)


def summed_on_arrival(value, axis, dim):
    pieces = cut_along(value, dim, lax.axis_size(axis))
    arrived = lax.all_to_all(pieces, axis, split_axis=0, concat_axis=0, tiled=True)
    return arrived.sum(axis=0)


def sum_in_two_steps(value, axes, dim):
    far, near = axes
    own = summed_on_arrival(cut_along(value, dim, lax.axis_size(far)), near, dim + 1)
    return jnp.sum(lax.all_to_all(own, far, 0, 0, tiled=True), axis=0)


def gelu_value(value):
    return 0.5 * value * (1.0 + jax.scipy.special.erf(value * (1.0 / math.sqrt(2.0))))


def gelu_slope(value):
    normal_cdf = 0.5 * (1.0 + jax.scipy.special.erf(value * (1.0 / math.sqrt(2.0))))
    return normal_cdf + value * jnp.exp(-0.5 * value * value) * (1.0 / math.sqrt(2.0 * math.pi))


def shards(inputs, targets, w_in, w_out, teach_in, teach_out):
    in_scale = 1.0 / math.sqrt(D)
    out_scale = 1.0 / math.sqrt(FF)
    gathered = gather_axes(inputs, (("dp_0", "dp_1"), "dp_2"), 0)
    partial_pre = jnp.dot(gathered, w_in, preferred_element_type=jnp.float32) * in_scale
    preact = lax.psum(partial_pre, "mp")
    hidden = gelu_value(preact).astype(jnp.bfloat16)
    block = hidden
    summed_rows = sum_in_two_steps(
        jnp.dot(block, w_out, preferred_element_type=jnp.float32) * out_scale,
        (("dp_0", "dp_1"), "dp_2"),
        0,
    )
    slope = (inputs.astype(jnp.float32) + summed_rows - targets.astype(jnp.float32)).astype(
        jnp.bfloat16
    )
    piece = gather_axes(slope, (("dp_0", "dp_1"), "dp_2"), 0)
    block = hidden
    grad_acc = jnp.einsum("tf,td->fd", block, piece, preferred_element_type=jnp.float32) * out_scale
    slope_part = (
        jnp.einsum("td,fd->tf", piece, w_out, preferred_element_type=jnp.float32) * out_scale
    )
    hidden_slope = lax.psum(slope_part.astype(jnp.bfloat16), "mp").astype(jnp.float32)
    pre_slope = (hidden_slope * gelu_slope(preact)).astype(jnp.bfloat16)
    grad_in = (
        jnp.einsum("td,tf->df", gathered, pre_slope, preferred_element_type=jnp.float32) * in_scale
    )
    new_in = decay_rate * teach_in + (1.0 - decay_rate) * (
        w_in.astype(jnp.float32) - step_size * grad_in
    )
    new_out = decay_rate * teach_out + (1.0 - decay_rate) * (
        w_out.astype(jnp.float32) - step_size * grad_acc
    )
    return (grad_in.astype(jnp.bfloat16), grad_acc.astype(jnp.bfloat16), new_in, new_out)


def solution(mesh):
    finer = Mesh(mesh.devices.reshape(8, 4, 2, mesh.shape["mp"]), ("dp_0", "dp_1", "dp_2", "mp"))
    return jax.shard_map(
        shards,
        mesh=finer,
        in_specs=(P(DP, "mp"), P(DP, "mp"), P("mp", DP), P(DP, "mp"), P("mp", DP), P(DP, "mp")),
        out_specs=(P("mp", DP), P(DP, "mp"), P("mp", DP), P(DP, "mp")),
        check_vma=False,
    )
```

profile of v0, /device:TPU:1, one launch (start us, length us, event | category | flops | bytes accessed | tf_op | source)
XLA Modules:
  0.0 553.0 jit_solution(2530100006321149228)
XLA Ops:
  7.2 0.8 broadcast_in_dim.12
  8.0 53.6 %all_to_all.30 = bf16[32,16,768]{2,1,0:T(8,128)(2,1)S(1)} all-to-all(bf16[32,16,768]{2,1,0:T(8,128)(2,1)S(1)} %broadcast_in_dim.12), channel_id=1, replica_groups=mesh['dp_0'=8,'dp_1'=4,'dp_2'=2,'mp'=8] {'dp_0','dp_1'}, dimensions={0} | all-to-all | bytes 1572864 | tf_op jit(solution)/shard_map/all_to_all | solution.py:20
  61.6 0.1 broadcast_in_dim.13
  61.7 8.7 %all_to_all.31 = bf16[2,32,16,768]{3,2,1,0:T(8,128)(2,1)S(1)} all-to-all(bf16[2,32,16,768]{3,2,1,0:T(8,128)(2,1)S(1)} %broadcast_in_dim.13), channel_id=1, replica_groups=mesh['dp_0'=8,'dp_1'=4,'dp_2'=2,'mp'=8] {'dp_2'}, dimensions={0} | all-to-all | bytes 3145728 | tf_op jit(solution)/shard_map/all_to_all | solution.py:20
  70.4 0.2 copy.25
  70.5 0.8 copy-done.1
  71.4 1.6 convolution_multiply_fusion.2
  73.0 0.0 all-reduce.5.cloned.1.call-start
  73.0 167.2 %all-reduce.3.cloned.1.call-done = f32[1024,256]{1,0:T(8,128)} async-done(((f32[1024,256]{1,0:T(8,128)}), f32[1024,256]{1,0:T(8,128)}) %all-reduce.3.cloned.1.call-update) | async-done | bytes 1048592 | tf_op jit(solution)/shard_map/psum | solution.py:66
  240.2 1.4 multiply_convert_fusion
  241.6 0.6 convolution_multiply_fusion
  242.2 0.2 copy-done
  242.4 0.2 copy.33
  242.7 11.2 %all_to_all.32 = f32[2,32,16,768]{3,2,1,0:T(8,128)} all-to-all(f32[2,32,16,768]{3,2,1,0:T(8,128)S(1)} %bitcast.29), channel_id=1, replica_groups=mesh['dp_0'=8,'dp_1'=4,'dp_2'=2,'mp'=8] {'dp_2'}, dimensions={0} | all-to-all | bytes 6291456 | tf_op jit(solution)/shard_map/all_to_all | solution.py:42
  253.9 3.4 reduce_sum.18
  257.3 87.5 %all_to_all.33 = f32[32,16,768]{2,1,0:T(8,128)S(1)} all-to-all(f32[32,16,768]{2,1,0:T(8,128)} %reduce_sum.18), channel_id=1, replica_groups=mesh['dp_0'=8,'dp_1'=4,'dp_2'=2,'mp'=8] {'dp_0','dp_1'}, dimensions={0} | all-to-all | bytes 3145728 | tf_op jit(solution)/shard_map/all_to_all | solution.py:49
  344.8 0.7 reduce_sum.19
  345.5 0.8 subtract_convert_fusion
  346.3 0.1 broadcast_in_dim.14
  346.3 44.4 %all_to_all.34 = bf16[32,16,768]{2,1,0:T(8,128)(2,1)S(1)} all-to-all(bf16[32,16,768]{2,1,0:T(8,128)(2,1)S(1)} %broadcast_in_dim.14), channel_id=1, replica_groups=mesh['dp_0'=8,'dp_1'=4,'dp_2'=2,'mp'=8] {'dp_0','dp_1'}, dimensions={0} | all-to-all | bytes 1572864 | tf_op jit(solution)/shard_map/all_to_all | solution.py:20
  390.7 0.1 broadcast_in_dim.15
  390.8 8.7 %all_to_all.35 = bf16[2,32,16,768]{3,2,1,0:T(8,128)(2,1)S(1)} all-to-all(bf16[2,32,16,768]{3,2,1,0:T(8,128)(2,1)S(1)} %broadcast_in_dim.15), channel_id=1, replica_groups=mesh['dp_0'=8,'dp_1'=4,'dp_2'=2,'mp'=8] {'dp_2'}, dimensions={0} | all-to-all | bytes 3145728 | tf_op jit(solution)/shard_map/all_to_all | solution.py:20
  399.5 0.2 copy.27
  399.7 1.4 fusion
  401.1 1.2 copy.29
  402.3 2.3 copy.28
  404.6 3.1 multiply_add_fusion
  407.7 133.9 %all-reduce.5.cloned.1.call-done = bf16[1024,256]{1,0:T(8,128)(2,1)} async-done(((bf16[1024,256]{1,0:T(8,128)(2,1)}), bf16[1024,256]{1,0:T(8,128)(2,1)}) %all-reduce.5.cloned.1.call-update) | async-done | bytes 524304 | tf_op jit(solution)/shard_map/psum | solution.py:83
  541.6 2.4 fusion.8
  544.1 0.1 fusion.14
  544.1 0.9 copy.30
  545.1 1.1 copy.31
  (7 shorter events, 0.1 us)
Async XLA Ops:
  7.2 233.0 %all-reduce.3.cloned.1.call-start = ((), (), s32[]{:S(2)}) async-start(), calls=%async_computation.6 | async-start | bytes 2097152 | tf_op jit(solution)/shard_map/psum | solution.py:66
  70.4 1.0 copy-start.1
  72.9 168.7 %copy-start.2 = (bf16[256,768]{1,0:T(8,128)(2,1)S(1)}, bf16[256,768]{1,0:T(8,128)(2,1)}, u32[]{:S(2)}) copy-start(bf16[256,768]{1,0:T(8,128)(2,1)} %param.9) | copy-start | bytes 1179652
  73.0 468.7 %all-reduce.5.cloned.1.call-start = ((), (), s32[]{:S(2)}) async-start(), calls=%async_computation.7 | async-start | bytes 1048576 | tf_op jit(solution)/shard_map/psum | solution.py:83
  241.6 0.8 copy-start
Sparse Core Ops, SparseCore 0:
  73.1 167.0 all-reduce.2
  401.2 140.3 all-reduce.4
where the time goes:
time: 559 us; the launch traced here: 553 us
  waiting for transfers between devices  301 us (54%)
  blocking collectives  214 us (38%)
  between operations  14.1 us (3%)
  matrix products  9.1 us (2%)
  local copies, waits for them, and re-layouts  8.2 us (1%)
  other arithmetic  6.4 us (1%)
    psum x1, waiting for transfers between devices, shards(): preact = lax.psum(partial_pre, 'mp')  167 us
    psum x1, waiting for transfers between devices, shards(): lax.psum(slope_part.astype(jnp.bfloat16), 'mp').astype(jnp.float32)  134 us
    all_to_all x4, blocking collectives, from_everyone(): return lax.all_to_all(copies, axis, split_axis=0, concat_axis=0, tiled=True)  115 us
    all_to_all x1, blocking collectives, sum_in_two_steps(): return jnp.sum(lax.all_to_all(own, far, 0, 0, tiled=True), axis=0)  87.5 us
    all_to_all x1, blocking collectives, summed_on_arrival(): lax.all_to_all(pieces, axis, split_axis=0, concat_axis=0, tiled=True)  11.2 us
  transfers between devices with their start and end apart: 2, of which 2 were waited for; matrix products, arithmetic and copies ran while one was open for 1% of the time, Pallas kernels for 0%

commit v1 on v0

v1 whole, which is shorter than its diff:
```python
import math

import jax
import jax.numpy as jnp
from jax import lax
from jax.sharding import Mesh
from jax.sharding import PartitionSpec as P

D = 6144
FF = 16384
DP = ("zl", "x", "c")
MP = ("zh", "y")
BF = jnp.bfloat16
F32 = jnp.float32

decay_rate = 0.99
step_size = 0.5


def exchange(pieces, axis):
    return lax.all_to_all(pieces, axis, split_axis=0, concat_axis=0, tiled=True)


def gather(value, axis):
    return exchange(jnp.broadcast_to(value, (lax.axis_size(axis), *value.shape)), axis)


def gather_tokens(value):
    return gather(gather(gather(value, "zl"), "x"), "c")


def sum_pieces(pieces):
    return pieces.astype(F32).sum(axis=0)


def scatter_tokens(partial):
    own = sum_pieces(exchange(partial.astype(BF), "c"))
    own = sum_pieces(exchange(own.astype(BF), "x"))
    return sum_pieces(exchange(own.astype(BF), "zl"))


def gelu_value(value):
    return 0.5 * value * (1.0 + jax.scipy.special.erf(value * (1.0 / math.sqrt(2.0))))


def gelu_slope(value):
    normal_cdf = 0.5 * (1.0 + jax.scipy.special.erf(value * (1.0 / math.sqrt(2.0))))
    return normal_cdf + value * jnp.exp(-0.5 * value * value) * (1.0 / math.sqrt(2.0 * math.pi))


def shards(inputs, targets, w_in, w_out, teach_in, teach_out):
    in_scale = 1.0 / math.sqrt(D)
    out_scale = 1.0 / math.sqrt(FF)
    rows, d = inputs.shape
    f = w_in.shape[1]
    dims = tuple(lax.axis_size(a) for a in ("c", "x", "zl"))
    tokens = rows * math.prod(dims)
    groups = lax.axis_size("zh") * lax.axis_size("y")

    gathered = gather_tokens(inputs).reshape(tokens, d)
    partial_pre = jnp.dot(gathered, w_in, preferred_element_type=F32) * in_scale
    preact = sum_pieces(exchange(partial_pre.astype(BF).reshape(groups, tokens // groups, f), MP))
    hidden = gather(gelu_value(preact).astype(BF), MP).reshape(tokens, f)

    partial_out = jnp.dot(hidden, w_out, preferred_element_type=F32) * out_scale
    summed_rows = scatter_tokens(partial_out.reshape(*dims, rows, d))
    slope = (inputs.astype(F32) + summed_rows - targets.astype(F32)).astype(BF)
    slopes = gather_tokens(slope).reshape(tokens, d)

    slope_part = jnp.einsum("td,fd->tf", slopes, w_out, preferred_element_type=F32) * out_scale
    hidden_slope = sum_pieces(
        exchange(slope_part.astype(BF).reshape(groups, tokens // groups, f), MP)
    )
    pre_slope = (hidden_slope * gelu_slope(preact)).astype(BF)
    pre_slopes = gather(pre_slope, MP).reshape(tokens, f)

    grad_out = jnp.einsum("tf,td->fd", hidden, slopes, preferred_element_type=F32) * out_scale
    new_out = decay_rate * teach_out + (1.0 - decay_rate) * (
        w_out.astype(F32) - step_size * grad_out
    )
    grad_in = jnp.einsum("td,tf->df", gathered, pre_slopes, preferred_element_type=F32) * in_scale
    new_in = decay_rate * teach_in + (1.0 - decay_rate) * (w_in.astype(F32) - step_size * grad_in)
    return (grad_in.astype(BF), grad_out.astype(BF), new_in, new_out)


def solution(mesh):
    finer = Mesh(mesh.devices.reshape(8, 4, 2, 2, 4), ("zl", "x", "c", "zh", "y"))
    return jax.shard_map(
        shards,
        mesh=finer,
        in_specs=(P(DP, MP), P(DP, MP), P(MP, DP), P(DP, MP), P(MP, DP), P(DP, MP)),
        out_specs=(P(MP, DP), P(DP, MP), P(MP, DP), P(DP, MP)),
        check_vma=False,
    )
```

time: 559 us -> 275 us (0.49)
  the two profiles are of different devices: /device:TPU:1 before, /device:TPU:32 now
where the time goes in v1:
time: 275 us; the launch traced here: 274 us
  blocking collectives  235 us (85%)
  waiting for transfers between devices  16.7 us (6%)
  local copies, waits for them, and re-layouts  8.56 us (3%)
  matrix products  6.81 us (2%)
  starting transfers between devices  4.14 us (2%)
    all_to_all x12, blocking collectives, exchange(): return lax.all_to_all(pieces, axis, split_axis=0, concat_axis=0, tiled=True)  235 us
    all_to_all x1, waiting for transfers between devices, exchange(): return lax.all_to_all(pieces, axis, split_axis=0, concat_axis=0, tiled=True)  16.7 us
    unnamed x18, local copies, waits for them, and re-layouts  6.54 us
  transfers between devices with their start and end apart: 1, of which 1 were waited for; matrix products, arithmetic and copies ran while one was open for 3% of the time, Pallas kernels for 0%

profile of v1, /device:TPU:32, one launch (start us, length us, event | category | flops | bytes accessed | tf_op | source)
XLA Modules:
  0.0 274.3 jit_solution(16152387306656025026)
XLA Ops:
  0.6 0.8 broadcast_in_dim.24
  1.4 26.0 %all_to_all.65 = bf16[8,16,768]{2,1,0:T(8,128)(2,1)S(1)} all-to-all(bf16[8,16,768]{2,1,0:T(8,128)(2,1)S(1)} %broadcast_in_dim.24), channel_id=1, replica_groups=mesh['zl'=8,'x'=4,'c'=2,'zh'=2,'y'=4] {'zl'}, dimensions={0} | all-to-all | bytes 393216 | tf_op jit(solution)/shard_map/all_to_all | solution.py:21
  27.5 13.6 %all_to_all.66 = bf16[4,8,16,768]{3,2,1,0:T(8,128)(2,1)S(1)} all-to-all(bf16[4,8,16,768]{3,2,1,0:T(8,128)(2,1)S(1)} %broadcast_in_dim.25), channel_id=1, replica_groups=mesh['zl'=8,'x'=4,'c'=2,'zh'=2,'y'=4] {'x'}, dimensions={0} | all-to-all | bytes 1572864 | tf_op jit(solution)/shard_map/all_to_all | solution.py:21
  41.1 0.1 broadcast_in_dim.26
  41.2 5.1 %all_to_all.67 = bf16[2,4,8,16,768]{4,3,2,1,0:T(8,128)(2,1)S(1)} all-to-all(bf16[2,4,8,16,768]{4,3,2,1,0:T(8,128)(2,1)S(1)} %broadcast_in_dim.26), channel_id=1, replica_groups=mesh['zl'=8,'x'=4,'c'=2,'zh'=2,'y'=4] {'c'}, dimensions={0} | all-to-all | bytes 3145728 | tf_op jit(solution)/shard_map/all_to_all | solution.py:21
  46.3 0.6 fusion
  46.9 45.3 %all_to_all.68 = bf16[8,128,256]{2,1,0:T(8,128)(2,1)S(1)} all-to-all(bf16[8,128,256]{2,1,0:T(8,128)(2,1)S(1)} %bitcast.32), channel_id=1, replica_groups=mesh['zl'=8,'x'=4,'c'=2,'zh'=2,'y'=4] {'zh','y'}, dimensions={0} | all-to-all | bytes 1048576 | tf_op jit(solution)/shard_map/all_to_all | solution.py:21
  92.2 0.1 convert_reduce_fusion.1
  92.4 28.4 %all_to_all.69 = bf16[8,128,256]{2,1,0:T(8,128)(2,1)S(1)} all-to-all(bf16[8,128,256]{2,1,0:T(8,128)(2,1)S(1)} %broadcast_in_dim.27), channel_id=1, replica_groups=mesh['zl'=8,'x'=4,'c'=2,'zh'=2,'y'=4] {'zh','y'}, dimensions={0} | all-to-all | bytes 1048576 | tf_op jit(solution)/shard_map/all_to_all | solution.py:21
  120.8 0.6 multiply_convert_fusion
  121.4 0.2 copy-done
  121.6 5.0 %all_to_all.70 = bf16[2,4,8,16,768]{4,3,2,1,0:T(8,128)(2,1)S(1)} all-to-all(bf16[2,4,8,16,768]{4,3,2,1,0:T(8,128)(2,1)S(1)} %bitcast.27), channel_id=1, replica_groups=mesh['zl'=8,'x'=4,'c'=2,'zh'=2,'y'=4] {'c'}, dimensions={0} | all-to-all | bytes 3145728 | tf_op jit(solution)/shard_map/all_to_all | solution.py:21
  126.6 1.4 reduce_sum.52
  128.0 16.5 %all_to_all.71 = bf16[4,8,16,768]{3,2,1,0:T(8,128)(2,1)S(1)} all-to-all(bf16[4,8,16,768]{3,2,1,0:T(8,128)(2,1)} %reduce_sum.52), channel_id=1, replica_groups=mesh['zl'=8,'x'=4,'c'=2,'zh'=2,'y'=4] {'x'}, dimensions={0} | all-to-all | bytes 1572864 | tf_op jit(solution)/shard_map/all_to_all | solution.py:21
  144.4 0.1 reduce_sum.53
  144.6 16.1 %all_to_all.72 = bf16[8,16,768]{2,1,0:T(8,128)(2,1)S(1)} all-to-all(bf16[8,16,768]{2,1,0:T(8,128)(2,1)S(1)} %reduce_sum.53), channel_id=1, replica_groups=mesh['zl'=8,'x'=4,'c'=2,'zh'=2,'y'=4] {'zl'}, dimensions={0} | all-to-all | bytes 393216 | tf_op jit(solution)/shard_map/all_to_all | solution.py:21
  160.8 18.4 %all_to_all.73 = bf16[8,16,768]{2,1,0:T(8,128)(2,1)S(1)} all-to-all(bf16[8,16,768]{2,1,0:T(8,128)(2,1)S(1)} %broadcast_in_dim.28), channel_id=1, replica_groups=mesh['zl'=8,'x'=4,'c'=2,'zh'=2,'y'=4] {'zl'}, dimensions={0} | all-to-all | bytes 393216 | tf_op jit(solution)/shard_map/all_to_all | solution.py:21
  179.2 11.9 %all_to_all.74 = bf16[4,8,16,768]{3,2,1,0:T(8,128)(2,1)S(1)} all-to-all(bf16[4,8,16,768]{3,2,1,0:T(8,128)(2,1)S(1)} %broadcast_in_dim.29), channel_id=1, replica_groups=mesh['zl'=8,'x'=4,'c'=2,'zh'=2,'y'=4] {'x'}, dimensions={0} | all-to-all | bytes 1572864 | tf_op jit(solution)/shard_map/all_to_all | solution.py:21
  191.1 0.1 broadcast_in_dim.30
  191.3 5.0 %all_to_all.75 = bf16[2,4,8,16,768]{4,3,2,1,0:T(8,128)(2,1)S(1)} all-to-all(bf16[2,4,8,16,768]{4,3,2,1,0:T(8,128)(2,1)S(1)} %broadcast_in_dim.30), channel_id=1, replica_groups=mesh['zl'=8,'x'=4,'c'=2,'zh'=2,'y'=4] {'c'}, dimensions={0} | all-to-all | bytes 3145728 | tf_op jit(solution)/shard_map/all_to_all | solution.py:21
  196.3 0.6 fusion.1
  196.9 44.2 %all_to_all.76 = bf16[8,128,256]{2,1,0:T(8,128)(2,1)S(1)} all-to-all(bf16[8,128,256]{2,1,0:T(8,128)(2,1)S(1)} %bitcast.33), channel_id=1, replica_groups=mesh['zl'=8,'x'=4,'c'=2,'zh'=2,'y'=4] {'zh','y'}, dimensions={0} | all-to-all | bytes 1048576 | tf_op jit(solution)/shard_map/all_to_all | solution.py:21
  241.0 0.1 convert_reduce_fusion
  241.2 0.8 broadcast_in_dim.31
  242.0 4.1 %all-to-all-start.12 = ((bf16[8,128,256]{2,1,0:T(8,128)(2,1)}), bf16[8,128,256]{2,1,0:T(8,128)(2,1)}, u32[]{:S(2)}, u32[]{:S(2)}) async-start(bf16[8,128,256]{2,1,0:T(8,128)(2,1)} %broadcast_in_dim.31), calls=%async_computation.12 | async-start | bytes 1048576 | tf_op jit(solution)/shard_map/all_to_all | solution.py:21
  246.2 1.9 copy.15
  248.1 2.3 copy.14
  250.4 3.0 %multiply_add_fusion = (f32[256,768]{1,0:T(8,128)}, bf16[256,768]{1,0:T(8,128)(2,1)}) fusion(bf16[256,768]{1,0:T(8,128)(2,1)S(1)} %copy-done.1, f32[256,768]{1,0:T(8,128)} %param.11, bf16[1024,256]{1,0:T(8,128)(2,1)} %bitcast.31, bf16[1024,768]{1,0:T(8,128)(2,1)S(1)} %bitcast.26), kind=kOutput, calls=%fused_computation.10 | convolution fusion | flops 404226048 | bytes 4456448 | tf_op jit(solution)/shard_map/tf,td->fd/dot_general | solution.py:77
  253.4 16.7 %all-to-all-done.12 = bf16[8,128,256]{2,1,0:T(8,128)(2,1)} async-done(((bf16[8,128,256]{2,1,0:T(8,128)(2,1)}), bf16[8,128,256]{2,1,0:T(8,128)(2,1)}, u32[]{:S(2)}, u32[]{:S(2)}) %all-to-all-start.12) | async-done | bytes 524320 | tf_op jit(solution)/shard_map/all_to_all | solution.py:21
  270.1 2.1 fusion.3
  272.2 0.9 copy.16
  273.1 1.1 copy.17
  (22 shorter events, 0.4 us)
Async XLA Ops:
  41.2 5.1 %copy-start.4 = (bf16[768,256]{1,0:T(8,128)(2,1)S(1)}, bf16[768,256]{1,0:T(8,128)(2,1)}, u32[]{:S(2)}) copy-start(bf16[768,256]{1,0:T(8,128)(2,1)} %param.8) | copy-start | bytes 1179652
  46.9 73.9 %copy-start.1 = (bf16[256,768]{1,0:T(8,128)(2,1)S(1)}, bf16[256,768]{1,0:T(8,128)(2,1)}, u32[]{:S(2)}) copy-start(bf16[256,768]{1,0:T(8,128)(2,1)} %param.9) | copy-start | bytes 1179652
  92.3 28.5 %copy-start.2 = (f32[128,256]{1,0:T(8,128)}, f32[128,256]{1,0:T(8,128)S(1)}, u32[]{:S(2)}) copy-start(f32[128,256]{1,0:T(8,128)S(1)} %convert_reduce_fusion.1) | copy-start | bytes 393220
  120.8 0.8 copy-start
  128.0 32.8 %copy-start.5 = (bf16[16,768]{1,0:T(8,128)(2,1)S(1)}, bf16[16,768]{1,0:T(8,128)(2,1)}, u32[]{:S(2)}) copy-start(bf16[16,768]{1,0:T(8,128)(2,1)} %param.6) | copy-start | bytes 73732
  128.0 32.8 %copy-start.6 = (bf16[16,768]{1,0:T(8,128)(2,1)S(1)}, bf16[16,768]{1,0:T(8,128)(2,1)}, u32[]{:S(2)}) copy-start(bf16[16,768]{1,0:T(8,128)(2,1)} %param.7) | copy-start | bytes 73732
  196.9 44.2 %copy-start.3 = (f32[128,256]{1,0:T(8,128)S(1)}, f32[128,256]{1,0:T(8,128)}, u32[]{:S(2)}) copy-start(f32[128,256]{1,0:T(8,128)} %copy-done.2) | copy-start | bytes 393220
  242.0 28.0 %all-to-all-start.12 = ((bf16[8,128,256]{2,1,0:T(8,128)(2,1)}), bf16[8,128,256]{2,1,0:T(8,128)(2,1)}, u32[]{:S(2)}, u32[]{:S(2)}) async-start(bf16[8,128,256]{2,1,0:T(8,128)(2,1)} %broadcast_in_dim.31), calls=%async_computation.12 | async-start | bytes 1048576 | tf_op jit(solution)/shard_map/all_to_all | solution.py:21

commit v2 on v1

v2 whole, which is shorter than its diff:
```python
import math

import jax
import jax.numpy as jnp
from jax import lax
from jax.sharding import Mesh
from jax.sharding import PartitionSpec as P

D = 6144
FF = 16384
DP = ("zq", "za", "x", "c")
MP = ("zh", "y")
BF = jnp.bfloat16
F32 = jnp.float32

decay_rate = 0.99
step_size = 0.5


def exchange(pieces, axis):
    return lax.all_to_all(pieces, axis, split_axis=0, concat_axis=0, tiled=True)


def gather(value, axis):
    return exchange(jnp.broadcast_to(value, (lax.axis_size(axis), *value.shape)), axis)


def scatter(partial, axis):
    return exchange(partial.astype(BF), axis).astype(F32).sum(axis=0)


def swap(value, axis):
    return lax.ppermute(value, axis, [(0, 1), (1, 0)])


def sum_pair(value, axis):
    return value + swap(value.astype(BF), axis).astype(F32)


def gelu_value(value):
    return 0.5 * value * (1.0 + jax.scipy.special.erf(value * (1.0 / math.sqrt(2.0))))


def gelu_slope(value):
    normal_cdf = 0.5 * (1.0 + jax.scipy.special.erf(value * (1.0 / math.sqrt(2.0))))
    return normal_cdf + value * jnp.exp(-0.5 * value * value) * (1.0 / math.sqrt(2.0 * math.pi))


def ema(teacher, student, grad):
    return decay_rate * teacher + (1.0 - decay_rate) * (student.astype(F32) - step_size * grad)


def shards(inputs, targets, w_in, w_out, teach_in, teach_out):
    in_scale = 1.0 / math.sqrt(D)
    out_scale = 1.0 / math.sqrt(FF)
    rows, d = inputs.shape
    f = w_in.shape[1]
    nx, na, nq, ny = (lax.axis_size(a) for a in ("x", "za", "zq", "y"))
    tokens = nx * na * nq * rows

    w_in2 = jnp.concatenate([w_in, swap(w_in, "c")], axis=1)
    w_out2 = jnp.concatenate([w_out, swap(w_out, "c")], axis=0)

    gathered = gather(gather(inputs, ("za", "zq")), "x").reshape(tokens, d)
    partial_pre = jnp.dot(gathered, w_in2, preferred_element_type=F32) * in_scale
    preact = sum_pair(scatter(partial_pre.reshape(ny, tokens // ny, 2 * f), "y"), "zh")
    hidden = gather(gelu_value(preact).astype(BF), "y").reshape(tokens, 2 * f)

    partial_out = jnp.dot(hidden, w_out2, preferred_element_type=F32) * out_scale
    sums = scatter(partial_out.reshape(nx, na * nq * rows, d), "x")
    sums = scatter(sums.reshape(na, nq, rows, d), "za")
    own = inputs.astype(F32) - targets.astype(F32)
    mine = lax.broadcasted_iota(jnp.int32, (nq, 1, 1), 0) == lax.axis_index("zq")
    slope = sum_pair(sums + jnp.where(mine, own[None], 0.0), "zq").astype(BF)
    slopes = gather(gather(slope, "za"), "x").reshape(tokens, d)

    slope_part = (
        jnp.einsum("td,fd->tf", slopes, w_out2, preferred_element_type=F32) * out_scale
    )
    hidden_slope = sum_pair(scatter(slope_part.reshape(ny, tokens // ny, 2 * f), "y"), "zh")
    pre_slope = (hidden_slope * gelu_slope(preact)).astype(BF)
    pre_slopes = gather(pre_slope, "y").reshape(tokens, 2 * f)

    part_out = jnp.einsum("tf,td->fd", hidden, slopes, preferred_element_type=F32) * out_scale
    grad_out = part_out[:f] + swap(part_out[f:].astype(BF), "c").astype(F32)
    new_out = ema(teach_out, w_out, grad_out)

    part_in = jnp.einsum("td,tf->df", gathered, pre_slopes, preferred_element_type=F32) * in_scale
    grad_in = part_in[:, :f] + swap(part_in[:, f:].astype(BF), "c").astype(F32)
    new_in = ema(teach_in, w_in, grad_in)
    return (grad_in.astype(BF), grad_out.astype(BF), new_in, new_out)


def solution(mesh):
    finer = Mesh(mesh.devices.reshape(2, 4, 4, 2, 2, 4), (*DP, *MP))
    return jax.shard_map(
        shards,
        mesh=finer,
        in_specs=(P(DP, MP), P(DP, MP), P(MP, DP), P(DP, MP), P(MP, DP), P(DP, MP)),
        out_specs=(P(MP, DP), P(DP, MP), P(MP, DP), P(DP, MP)),
        check_vma=False,
    )
```

time: 275 us -> 204 us (0.74)
  the two profiles are of different devices: /device:TPU:32 before, /device:TPU:1 now
where the time goes in v2:
time: 204 us; the launch traced here: 203 us
  starting transfers between devices  83.6 us (41%)
  blocking collectives  74.7 us (37%)
  waiting for transfers between devices  22.8 us (11%)
  local copies, waits for them, and re-layouts  11.7 us (6%)
  other arithmetic  5.34 us (3%)
  matrix products  4.24 us (2%)
    all_to_all x6, blocking collectives, exchange(): return lax.all_to_all(pieces, axis, split_axis=0, concat_axis=0, tiled=True)  74.7 us
    ppermute x7, starting transfers between devices, swap(): return lax.ppermute(value, axis, [(0, 1), (1, 0)])  67.6 us
    all_to_all x4, starting transfers between devices, exchange(): return lax.all_to_all(pieces, axis, split_axis=0, concat_axis=0, tiled=True)  16 us
    all_to_all x4, waiting for transfers between devices, exchange(): return lax.all_to_all(pieces, axis, split_axis=0, concat_axis=0, tiled=True)  12.2 us
    ppermute x7, waiting for transfers between devices, swap(): return lax.ppermute(value, axis, [(0, 1), (1, 0)])  10.6 us
    unnamed x23, local copies, waits for them, and re-layouts  6.63 us
  transfers between devices with their start and end apart: 11, of which 6 were waited for; matrix products, arithmetic and copies ran while one was open for 6% of the time, Pallas kernels for 0%

profile of v2, /device:TPU:1, one launch (start us, length us, event | category | flops | bytes accessed | tf_op | source)
XLA Modules:
  0.0 203.4 jit_solution(9866535454966228759)
XLA Ops:
  1.4 23.8 %all_to_all.50 = bf16[8,16,768]{2,1,0:T(8,128)(2,1)S(1)} all-to-all(bf16[8,16,768]{2,1,0:T(8,128)(2,1)S(1)} %broadcast_in_dim.39), channel_id=1, replica_groups=mesh['zq'=2,'za'=4,'x'=4,'c'=2,'zh'=2,'y'=4] {'za','zq'}, dimensions={0} | all-to-all | bytes 393216 | tf_op jit(solution)/shard_map/all_to_all | solution.py:21
  25.3 0.9 broadcast_in_dim.40
  26.2 4.0 %all-to-all-start.1 = ((bf16[4,8,16,768]{3,2,1,0:T(8,128)(2,1)}), bf16[4,8,16,768]{3,2,1,0:T(8,128)(2,1)S(1)}, u32[]{:S(2)}, u32[]{:S(2)}) async-start(bf16[4,8,16,768]{3,2,1,0:T(8,128)(2,1)} %broadcast_in_dim.40), calls=%async_computation.1 | async-start | bytes 1572864 | tf_op jit(solution)/shard_map/all_to_all | solution.py:21
  30.2 6.9 %collective-permute-start = (bf16[768,256]{1,0:T(8,128)(2,1)S(1)}, bf16[768,256]{1,0:T(8,128)(2,1)S(1)}, u32[]{:S(2)}, u32[]{:S(2)}) collective-permute-start(bf16[768,256]{1,0:T(8,128)(2,1)S(1)} %copy-done.4), channel_id=1, source_target_pairs={{0,8},{8,0},{1,9},{9,1},{2,10},{10,2},{3,11},{11,3},{4,12},{12,4},... | collective-permute-start | bytes 1179656 | tf_op jit(solution)/shard_map/ppermute | solution.py:33
  37.2 1.3 collective-permute-done
  39.5 11.0 %all_to_all.51 = bf16[4,128,512]{2,1,0:T(8,128)(2,1)S(1)} all-to-all(bf16[4,128,512]{2,1,0:T(8,128)(2,1)S(1)} %bitcast.28), channel_id=1, replica_groups=mesh['zq'=2,'za'=4,'x'=4,'c'=2,'zh'=2,'y'=4] {'y'}, dimensions={0} | all-to-all | bytes 1048576 | tf_op jit(solution)/shard_map/all_to_all | solution.py:21
  50.6 7.9 %collective-permute-start.1 = (bf16[128,512]{1,0:T(8,128)(2,1)S(1)}, bf16[128,512]{1,0:T(8,128)(2,1)S(1)}, u32[]{:S(2)}, u32[]{:S(2)}) collective-permute-start(bf16[128,512]{1,0:T(8,128)(2,1)S(1)} %convert_element_type.92), channel_id=1, source_target_pairs={{0,4},{4,0},{1,5},{5,1},{2,6},{6,2},{3,7},{7,3},{8,12},{12,8},{9,1... | collective-permute-start | bytes 393224 | tf_op jit(solution)/shard_map/ppermute | solution.py:33
  58.6 9.8 %collective-permute-start.2 = (bf16[256,768]{1,0:T(8,128)(2,1)S(1)}, bf16[256,768]{1,0:T(8,128)(2,1)S(1)}, u32[]{:S(2)}, u32[]{:S(2)}) collective-permute-start(bf16[256,768]{1,0:T(8,128)(2,1)S(1)} %copy-done.2), channel_id=1, source_target_pairs={{0,8},{8,0},{1,9},{9,1},{2,10},{10,2},{3,11},{11,3},{4,12},{12,4},... | collective-permute-start | bytes 1179656 | tf_op jit(solution)/shard_map/ppermute | solution.py:33
  68.5 0.8 broadcast_in_dim.41
  69.3 3.5 %all-to-all-start.3 = ((bf16[4,128,512]{2,1,0:T(8,128)(2,1)}), bf16[4,128,512]{2,1,0:T(8,128)(2,1)S(1)}, u32[]{:S(2)}, u32[]{:S(2)}) async-start(bf16[4,128,512]{2,1,0:T(8,128)(2,1)} %broadcast_in_dim.41), calls=%async_computation.3 | async-start | bytes 1048576 | tf_op jit(solution)/shard_map/all_to_all | solution.py:21
  72.9 6.8 %all-to-all-done.3 = bf16[4,128,512]{2,1,0:T(8,128)(2,1)S(1)} async-done(((bf16[4,128,512]{2,1,0:T(8,128)(2,1)}), bf16[4,128,512]{2,1,0:T(8,128)(2,1)S(1)}, u32[]{:S(2)}, u32[]{:S(2)}) %all-to-all-start.3) | async-done | bytes 524320 | tf_op jit(solution)/shard_map/all_to_all | solution.py:21
  80.3 11.0 %all_to_all.52 = bf16[4,128,768]{2,1,0:T(8,128)(2,1)S(1)} all-to-all(bf16[4,128,768]{2,1,0:T(8,128)(2,1)S(1)} %bitcast.27), channel_id=1, replica_groups=mesh['zq'=2,'za'=4,'x'=4,'c'=2,'zh'=2,'y'=4] {'x'}, dimensions={0} | all-to-all | bytes 1572864 | tf_op jit(solution)/shard_map/all_to_all | solution.py:21
  92.2 4.4 %all-to-all-start.5 = ((bf16[4,2,16,768]{3,2,1,0:T(8,128)(2,1)}), bf16[4,2,16,768]{3,2,1,0:T(8,128)(2,1)S(1)}, u32[]{:S(2)}, u32[]{:S(2)}) async-start(bf16[4,2,16,768]{3,2,1,0:T(8,128)(2,1)} %bitcast.5), calls=%async_computation.5 | async-start | bytes 393216 | tf_op jit(solution)/shard_map/all_to_all | solution.py:21
  96.6 5.4 %all-to-all-done.5 = bf16[4,2,16,768]{3,2,1,0:T(8,128)(2,1)S(1)} async-done(((bf16[4,2,16,768]{3,2,1,0:T(8,128)(2,1)}), bf16[4,2,16,768]{3,2,1,0:T(8,128)(2,1)S(1)}, u32[]{:S(2)}, u32[]{:S(2)}) %all-to-all-start.5) | async-done | bytes 196640 | tf_op jit(solution)/shard_map/all_to_all | solution.py:21
  102.1 15.0 %collective-permute-start.3 = (bf16[2,16,768]{2,1,0:T(8,128)(2,1)S(1)}, bf16[2,16,768]{2,1,0:T(8,128)(2,1)S(1)}, u32[]{:S(2)}, u32[]{:S(2)}) collective-permute-start(bf16[2,16,768]{2,1,0:T(8,128)(2,1)S(1)} %fusion.13), channel_id=1, source_target_pairs={{0,256},{256,0},{1,257},{257,1},{2,258},{258,2},{3,259},{259,3},{4... | collective-permute-start | bytes 147464 | tf_op jit(solution)/shard_map/ppermute | solution.py:33
  117.1 1.8 collective-permute-done.3
  119.0 8.7 %all_to_all.53 = bf16[4,2,16,768]{3,2,1,0:T(8,128)(2,1)S(1)} all-to-all(bf16[4,2,16,768]{3,2,1,0:T(8,128)(2,1)S(1)} %broadcast_in_dim.45), channel_id=1, replica_groups=mesh['zq'=2,'za'=4,'x'=4,'c'=2,'zh'=2,'y'=4] {'za'}, dimensions={0} | all-to-all | bytes 393216 | tf_op jit(solution)/shard_map/all_to_all | solution.py:21
  127.7 10.7 %all_to_all.54 = bf16[4,4,2,16,768]{4,3,2,1,0:T(8,128)(2,1)S(1)} all-to-all(bf16[4,4,2,16,768]{4,3,2,1,0:T(8,128)(2,1)S(1)} %broadcast_in_dim.46), channel_id=1, replica_groups=mesh['zq'=2,'za'=4,'x'=4,'c'=2,'zh'=2,'y'=4] {'x'}, dimensions={0} | all-to-all | bytes 1572864 | tf_op jit(solution)/shard_map/all_to_all | solution.py:21
  139.1 9.3 %all_to_all.55 = bf16[4,128,512]{2,1,0:T(8,128)(2,1)S(1)} all-to-all(bf16[4,128,512]{2,1,0:T(8,128)(2,1)S(1)} %bitcast.29), channel_id=1, replica_groups=mesh['zq'=2,'za'=4,'x'=4,'c'=2,'zh'=2,'y'=4] {'y'}, dimensions={0} | all-to-all | bytes 1048576 | tf_op jit(solution)/shard_map/all_to_all | solution.py:21
  148.5 7.0 %collective-permute-start.4 = (bf16[128,512]{1,0:T(8,128)(2,1)S(1)}, bf16[128,512]{1,0:T(8,128)(2,1)S(1)}, u32[]{:S(2)}, u32[]{:S(2)}) collective-permute-start(bf16[128,512]{1,0:T(8,128)(2,1)S(1)} %convert_element_type.107), channel_id=1, source_target_pairs={{0,4},{4,0},{1,5},{5,1},{2,6},{6,2},{3,7},{7,3},{8,12},{12,8},{9,1... | collective-permute-start | bytes 393224 | tf_op jit(solution)/shard_map/ppermute | solution.py:33
  155.5 7.5 %collective-permute-done.4 = bf16[128,512]{1,0:T(8,128)(2,1)S(1)} collective-permute-done((bf16[128,512]{1,0:T(8,128)(2,1)S(1)}, bf16[128,512]{1,0:T(8,128)(2,1)S(1)}, u32[]{:S(2)}, u32[]{:S(2)}) %collective-permute-start.4) | collective-permute-done | bytes 131104 | tf_op jit(solution)/shard_map/ppermute | solution.py:33
  163.2 0.8 broadcast_in_dim.47
  164.0 4.1 %all-to-all-start.9 = ((bf16[4,128,512]{2,1,0:T(8,128)(2,1)}), bf16[4,128,512]{2,1,0:T(8,128)(2,1)}, u32[]{:S(2)}, u32[]{:S(2)}) async-start(bf16[4,128,512]{2,1,0:T(8,128)(2,1)} %broadcast_in_dim.47), calls=%async_computation.9 | async-start | bytes 1048576 | tf_op jit(solution)/shard_map/all_to_all | solution.py:21
  169.6 14.2 %collective-permute-start.6 = (bf16[256,768]{1,0:T(8,128)(2,1)}, bf16[256,768]{1,0:T(8,128)(2,1)}, u32[]{:S(2)}, u32[]{:S(2)}) collective-permute-start(bf16[256,768]{1,0:T(8,128)(2,1)} %slice.34), channel_id=1, source_target_pairs={{0,8},{8,0},{1,9},{9,1},{2,10},{10,2},{3,11},{11,3},{4,12},{12,4},... | collective-permute-start | bytes 1179656 | tf_op jit(solution)/shard_map/ppermute | solution.py:33
  183.7 1.9 multiply_bitcast_fusion
  186.4 6.7 %collective-permute-start.5 = (bf16[768,256]{0,1:T(8,128)(2,1)}, bf16[768,256]{0,1:T(8,128)(2,1)}, u32[]{:S(2)}, u32[]{:S(2)}) collective-permute-start(bf16[768,256]{0,1:T(8,128)(2,1)} %slice.35), channel_id=1, source_target_pairs={{0,8},{8,0},{1,9},{9,1},{2,10},{10,2},{3,11},{11,3},{4,12},{12,4},... | collective-permute-start | bytes 1179656 | tf_op jit(solution)/shard_map/ppermute | solution.py:33
  193.2 1.9 copy.15
  195.1 2.3 %copy.14 = f32[768,256]{0,1:T(8,128)} copy(f32[768,256]{1,0:T(8,128)} %param.10) | data formatting | bytes 1572864 | tf_op args[4]
  197.4 2.7 %multiply_add_fusion = (f32[256,768]{1,0:T(8,128)}, bf16[256,768]{1,0:T(8,128)(2,1)}) fusion(bf16[256,768]{1,0:T(8,128)(2,1)} %param.9, f32[256,768]{1,0:T(8,128)} %param.11, bf16[256,768]{1,0:T(8,128)(2,1)} %collective-permute-done.6, f32[512,768]{1,0:T(8,128)S(1)} %convolution_multiply_fusion), kind=kLoop, calls=%fused_computation.16 | loop fusion | flops 1769472 | bytes 3538944 | tf_op jit(solution)/shard_map/add | solution.py:50
  200.1 1.2 multiply_add_fusion.1
  201.3 1.1 copy.17
  202.5 0.9 copy.16
  (47 shorter events, 6.7 us)
Async XLA Ops:
  0.6 29.6 %copy-start.4 = (bf16[768,256]{1,0:T(8,128)(2,1)S(1)}, bf16[768,256]{1,0:T(8,128)(2,1)}, u32[]{:S(2)}) copy-start(bf16[768,256]{1,0:T(8,128)(2,1)} %param.8) | copy-start | bytes 1179652
  26.2 12.4 %all-to-all-start.1 = ((bf16[4,8,16,768]{3,2,1,0:T(8,128)(2,1)}), bf16[4,8,16,768]{3,2,1,0:T(8,128)(2,1)S(1)}, u32[]{:S(2)}, u32[]{:S(2)}) async-start(bf16[4,8,16,768]{3,2,1,0:T(8,128)(2,1)} %broadcast_in_dim.40), calls=%async_computation.1 | async-start | bytes 1572864 | tf_op jit(solution)/shard_map/all_to_all | solution.py:21
  30.2 8.3 %collective-permute-start = (bf16[768,256]{1,0:T(8,128)(2,1)S(1)}, bf16[768,256]{1,0:T(8,128)(2,1)S(1)}, u32[]{:S(2)}, u32[]{:S(2)}) collective-permute-start(bf16[768,256]{1,0:T(8,128)(2,1)S(1)} %copy-done.4), channel_id=1, source_target_pairs={{0,8},{8,0},{1,9},{9,1},{2,10},{10,2},{3,11},{11,3},{4,12},{12,4},... | collective-permute-start | bytes 1179656 | tf_op jit(solution)/shard_map/ppermute | solution.py:33
  38.6 0.9 copy-start.1
  39.5 19.1 %copy-start.2 = (bf16[256,768]{1,0:T(8,128)(2,1)S(1)}, bf16[256,768]{1,0:T(8,128)(2,1)}, u32[]{:S(2)}) copy-start(bf16[256,768]{1,0:T(8,128)(2,1)} %param.9) | copy-start | bytes 1179652
  50.6 17.8 %collective-permute-start.1 = (bf16[128,512]{1,0:T(8,128)(2,1)S(1)}, bf16[128,512]{1,0:T(8,128)(2,1)S(1)}, u32[]{:S(2)}, u32[]{:S(2)}) collective-permute-start(bf16[128,512]{1,0:T(8,128)(2,1)S(1)} %convert_element_type.92), channel_id=1, source_target_pairs={{0,4},{4,0},{1,5},{5,1},{2,6},{6,2},{3,7},{7,3},{8,12},{12,8},{9,1... | collective-permute-start | bytes 393224 | tf_op jit(solution)/shard_map/ppermute | solution.py:33
  58.6 14.3 %collective-permute-start.2 = (bf16[256,768]{1,0:T(8,128)(2,1)S(1)}, bf16[256,768]{1,0:T(8,128)(2,1)S(1)}, u32[]{:S(2)}, u32[]{:S(2)}) collective-permute-start(bf16[256,768]{1,0:T(8,128)(2,1)S(1)} %copy-done.2), channel_id=1, source_target_pairs={{0,8},{8,0},{1,9},{9,1},{2,10},{10,2},{3,11},{11,3},{4,12},{12,4},... | collective-permute-start | bytes 1179656 | tf_op jit(solution)/shard_map/ppermute | solution.py:33
  69.3 10.4 %all-to-all-start.3 = ((bf16[4,128,512]{2,1,0:T(8,128)(2,1)}), bf16[4,128,512]{2,1,0:T(8,128)(2,1)S(1)}, u32[]{:S(2)}, u32[]{:S(2)}) async-start(bf16[4,128,512]{2,1,0:T(8,128)(2,1)} %broadcast_in_dim.41), calls=%async_computation.3 | async-start | bytes 1048576 | tf_op jit(solution)/shard_map/all_to_all | solution.py:21
  72.9 18.5 %copy-start.5 = (bf16[512,768]{1,0:T(8,128)(2,1)}, bf16[512,768]{1,0:T(8,128)(2,1)S(1)}, u32[]{:S(2)}) copy-start(bf16[512,768]{1,0:T(8,128)(2,1)S(1)} %constant_dynamic-update-slice_fusion) | copy-start | bytes 2359300
  80.3 16.3 %copy-start.7 = (bf16[16,768]{1,0:T(8,128)(2,1)S(1)}, bf16[16,768]{1,0:T(8,128)(2,1)}, u32[]{:S(2)}) copy-start(bf16[16,768]{1,0:T(8,128)(2,1)} %param.6) | copy-start | bytes 73732
  80.3 16.3 %copy-start.8 = (bf16[16,768]{1,0:T(8,128)(2,1)S(1)}, bf16[16,768]{1,0:T(8,128)(2,1)}, u32[]{:S(2)}) copy-start(bf16[16,768]{1,0:T(8,128)(2,1)} %param.7) | copy-start | bytes 73732
  92.2 9.8 %all-to-all-start.5 = ((bf16[4,2,16,768]{3,2,1,0:T(8,128)(2,1)}), bf16[4,2,16,768]{3,2,1,0:T(8,128)(2,1)S(1)}, u32[]{:S(2)}, u32[]{:S(2)}) async-start(bf16[4,2,16,768]{3,2,1,0:T(8,128)(2,1)} %bitcast.5), calls=%async_computation.5 | async-start | bytes 393216 | tf_op jit(solution)/shard_map/all_to_all | solution.py:21
  102.1 16.8 %collective-permute-start.3 = (bf16[2,16,768]{2,1,0:T(8,128)(2,1)S(1)}, bf16[2,16,768]{2,1,0:T(8,128)(2,1)S(1)}, u32[]{:S(2)}, u32[]{:S(2)}) collective-permute-start(bf16[2,16,768]{2,1,0:T(8,128)(2,1)S(1)} %fusion.13), channel_id=1, source_target_pairs={{0,256},{256,0},{1,257},{257,1},{2,258},{258,2},{3,259},{259,3},{4... | collective-permute-start | bytes 147464 | tf_op jit(solution)/shard_map/ppermute | solution.py:33
  118.9 19.6 %copy-start.6 = (bf16[512,768]{1,0:T(8,128)(2,1)S(1)}, bf16[512,768]{1,0:T(8,128)(2,1)}, u32[]{:S(2)}) copy-start(bf16[512,768]{1,0:T(8,128)(2,1)} %copy-done.5) | copy-start | bytes 2359300
  148.5 14.5 %collective-permute-start.4 = (bf16[128,512]{1,0:T(8,128)(2,1)S(1)}, bf16[128,512]{1,0:T(8,128)(2,1)S(1)}, u32[]{:S(2)}, u32[]{:S(2)}) collective-permute-start(bf16[128,512]{1,0:T(8,128)(2,1)S(1)} %convert_element_type.107), channel_id=1, source_target_pairs={{0,4},{4,0},{1,5},{5,1},{2,6},{6,2},{3,7},{7,3},{8,12},{12,8},{9,1... | collective-permute-start | bytes 393224 | tf_op jit(solution)/shard_map/ppermute | solution.py:33
  164.0 19.7 %all-to-all-start.9 = ((bf16[4,128,512]{2,1,0:T(8,128)(2,1)}), bf16[4,128,512]{2,1,0:T(8,128)(2,1)}, u32[]{:S(2)}, u32[]{:S(2)}) async-start(bf16[4,128,512]{2,1,0:T(8,128)(2,1)} %broadcast_in_dim.47), calls=%async_computation.9 | async-start | bytes 1048576 | tf_op jit(solution)/shard_map/all_to_all | solution.py:21
  169.6 27.8 %collective-permute-start.6 = (bf16[256,768]{1,0:T(8,128)(2,1)}, bf16[256,768]{1,0:T(8,128)(2,1)}, u32[]{:S(2)}, u32[]{:S(2)}) collective-permute-start(bf16[256,768]{1,0:T(8,128)(2,1)} %slice.34), channel_id=1, source_target_pairs={{0,8},{8,0},{1,9},{9,1},{2,10},{10,2},{3,11},{11,3},{4,12},{12,4},... | collective-permute-start | bytes 1179656 | tf_op jit(solution)/shard_map/ppermute | solution.py:33
  186.4 13.6 %collective-permute-start.5 = (bf16[768,256]{0,1:T(8,128)(2,1)}, bf16[768,256]{0,1:T(8,128)(2,1)}, u32[]{:S(2)}, u32[]{:S(2)}) collective-permute-start(bf16[768,256]{0,1:T(8,128)(2,1)} %slice.35), channel_id=1, source_target_pairs={{0,8},{8,0},{1,9},{9,1},{2,10},{10,2},{3,11},{11,3},{4,12},{12,4},... | collective-permute-start | bytes 1179656 | tf_op jit(solution)/shard_map/ppermute | solution.py:33
  197.4 2.7 %copy-start = (f32[768,256]{0,1:T(8,128)S(1)}, f32[768,256]{0,1:T(8,128)}, u32[]{:S(2)}) copy-start(f32[768,256]{0,1:T(8,128)} %copy.14) | copy-start | bytes 2359300
  197.4 2.7 %copy-start.3 = (bf16[768,256]{0,1:T(8,128)(2,1)S(1)}, bf16[768,256]{0,1:T(8,128)(2,1)}, u32[]{:S(2)}) copy-start(bf16[768,256]{0,1:T(8,128)(2,1)} %copy.15) | copy-start | bytes 1179652

commit v3 on v2

v3 whole, which is shorter than its diff:
```python
import math

import jax
import jax.numpy as jnp
from jax import lax
from jax.sharding import Mesh
from jax.sharding import PartitionSpec as P

D = 6144
FF = 16384
DP = ("zq", "za", "x", "c")
MP = ("zh", "y")
BF = jnp.bfloat16
F32 = jnp.float32

decay_rate = 0.99
step_size = 0.5


def exchange(pieces, axis):
    return lax.all_to_all(pieces, axis, split_axis=0, concat_axis=0, tiled=True)


def gather(value, axis):
    return exchange(jnp.broadcast_to(value, (lax.axis_size(axis), *value.shape)), axis)


def scatter(partial, axis):
    return exchange(partial.astype(BF), axis).astype(F32).sum(axis=0)


def shift(value, axis, by):
    n = lax.axis_size(axis)
    return lax.ppermute(value, axis, [(i, (i + by) % n) for i in range(n)])


def sum_pair(value, axis):
    return value + shift(value.astype(BF), axis, 1).astype(F32)


def gelu_value(value):
    return 0.5 * value * (1.0 + jax.scipy.special.erf(value * (1.0 / math.sqrt(2.0))))


def gelu_slope(value):
    normal_cdf = 0.5 * (1.0 + jax.scipy.special.erf(value * (1.0 / math.sqrt(2.0))))
    return normal_cdf + value * jnp.exp(-0.5 * value * value) * (1.0 / math.sqrt(2.0 * math.pi))


def ema(teacher, student, grad):
    return decay_rate * teacher + (1.0 - decay_rate) * (student.astype(F32) - step_size * grad)


def dot(a, b):
    return jnp.dot(a, b, preferred_element_type=F32)


def shards(inputs, targets, w_in, w_out, teach_in, teach_out):
    in_scale = 1.0 / math.sqrt(D)
    out_scale = 1.0 / math.sqrt(FF)
    rows, d = inputs.shape
    f = w_in.shape[1]
    nx, na, nq, ny = (lax.axis_size(a) for a in ("x", "za", "zq", "y"))
    blocks = nx * na * nq
    tokens = blocks * rows
    part = tokens // ny
    few = rows // ny
    y = lax.axis_index("y")

    w_in2 = jnp.concatenate([w_in, shift(w_in, "c", 1)], axis=1)
    w_ring = jnp.concatenate([w_out, *(shift(w_out, "y", -k) for k in range(1, ny))], axis=1)
    w_out2 = jnp.concatenate([w_ring, shift(w_ring, "c", 1)], axis=0)

    arrived = gather(gather(inputs, ("za", "zq")), "x").reshape(tokens, d)
    at = lax.broadcasted_iota(jnp.int32, (tokens, tokens), 0)
    here = at // part
    source = (at % part) // few * rows + here * few + at % few
    order = (source == lax.broadcasted_iota(jnp.int32, (tokens, tokens), 1)).astype(BF)
    gathered = dot(order, arrived).astype(BF)
    gathered_t = lax.optimization_barrier(gathered.T)

    partial_pre = dot(gathered, w_in2) * in_scale
    sums = scatter(partial_pre.reshape(ny, part, 2 * f), "y")

    both = jnp.stack([inputs.reshape(ny, few, d), targets.reshape(ny, few, d)], axis=1)
    both, sums = lax.optimization_barrier((both, sums))
    both = exchange(both, "y").astype(F32)
    own = both[:, 0] - both[:, 1]
    own = jnp.concatenate(
        [lax.dynamic_index_in_dim(own, (y + k) & (ny - 1), keepdims=False) for k in range(ny)],
        axis=1,
    )
    own, other = lax.optimization_barrier((own, shift(sums.astype(BF), "zh", 1)))
    preact = sums + other.astype(F32)
    hidden = gelu_value(preact).astype(BF)

    partial_out = dot(hidden, w_out2) * out_scale
    sums = scatter(partial_out.reshape(nx, part // nx, ny * d), "x")
    sums = scatter(sums.reshape(na, nq * few, ny * d), "za")
    mine = lax.broadcasted_iota(jnp.int32, (nq * few, 1), 0) // few == lax.axis_index("zq")
    sums = sums + jnp.where(mine, jnp.concatenate([own] * nq, axis=0), 0.0)
    slope = sum_pair(sums, "zq").astype(BF)
    slopes = gather(gather(slope, "za"), "x").reshape(part, ny * d)

    slope_part = jnp.einsum("td,fd->tf", slopes, w_out2, preferred_element_type=F32) * out_scale
    hidden_slope = sum_pair(slope_part, "zh")
    pre_slope = (hidden_slope * gelu_slope(preact)).astype(BF)
    pre_slopes = gather(pre_slope, "y").reshape(tokens, 2 * f)

    hiddens = jnp.concatenate([hidden, *(shift(hidden, "y", k) for k in range(1, ny))], axis=0)
    own_slopes = jnp.concatenate(
        [slopes[:, :d], *(shift(slopes[:, k * d : (k + 1) * d], "y", k) for k in range(1, ny))],
        axis=0,
    )

    def grad_of(units):
        return jnp.einsum("tf,td->fd", units, own_slopes, preferred_element_type=F32) * out_scale

    theirs = shift(grad_of(hiddens[:, f:]).astype(BF), "c", 1).astype(F32)
    grad_out = grad_of(hiddens[:, :f]) + theirs
    new_out = ema(teach_out, w_out, grad_out)

    theirs = shift((dot(gathered_t, pre_slopes[:, f:]) * in_scale).astype(BF), "c", 1).astype(F32)
    grad_in = dot(gathered_t, pre_slopes[:, :f]) * in_scale + theirs
    new_in = ema(teach_in, w_in, grad_in)
    return (grad_in.astype(BF), grad_out.astype(BF), new_in, new_out)


def solution(mesh):
    finer = Mesh(mesh.devices.reshape(2, 4, 4, 2, 2, 4), (*DP, *MP))
    return jax.shard_map(
        shards,
        mesh=finer,
        in_specs=(P(DP, MP), P(DP, MP), P(MP, DP), P(DP, MP), P(MP, DP), P(DP, MP)),
        out_specs=(P(MP, DP), P(DP, MP), P(MP, DP), P(DP, MP)),
        check_vma=False,
    )
```

time: 204 us -> 201 us (0.985)
  blocking collectives: 74.7 us -> 22.5 us
  starting transfers between devices: 83.6 us -> 119 us
  matrix products: 4.24 us -> 15.7 us
  waiting for transfers between devices: 22.8 us -> 30.1 us
  local copies, waits for them, and re-layouts: 11.7 us -> 8.24 us
  other arithmetic: 5.34 us -> 3.11 us
    all_to_all x6 -> x2, blocking collectives: 74.7 us -> 22.5 us  [exchange(): return lax.all_to_all(pieces, axis, split_axis=0, concat_axis=0, tiled=True)]
    all_to_all x4 -> x7, starting transfers between devices: 16 us -> 39.9 us  [exchange(): return lax.all_to_all(pieces, axis, split_axis=0, concat_axis=0, tiled=True)]
    ppermute x7 -> x16, starting transfers between devices: 67.6 us -> 78.7 us  [shift(): return lax.ppermute(value, axis, [(i, (i + by) % n) for i in range(n)])]
    dot_general x4 -> x7, matrix products: 3.64 us -> 12.6 us  [the longest x5 7.72 us: dot(): return jnp.dot(a, b, preferred_element_type=F32)]
    ppermute x7 -> x16, waiting for transfers between devices: 10.6 us -> 16.8 us  [shift(): return lax.ppermute(value, axis, [(i, (i + by) % n) for i in range(n)])]
    unnamed x23 -> x15, local copies, waits for them, and re-layouts: 6.63 us -> 2.45 us
    add x2 -> x1, other arithmetic: 3.91 us -> 0.01 us  [shards(): source = at % part // few * rows + here * few + at % few]
    dot_general x1, matrix products: 0.6 us -> 3.06 us  [shards(): jnp.einsum('td,fd->tf', slopes, w_out2, preferred_element_type=F32)]
  transfers between devices with their start and end apart: 11 -> 23, of which waited for: 6 -> 5; matrix products, arithmetic and copies ran while one was open for 6% -> 10% of each run, Pallas kernels for 0% -> 0%
where the time goes in v3:
time: 201 us; the launch traced here: 199 us
  starting transfers between devices  119 us (59%)
  waiting for transfers between devices  30.1 us (15%)
  blocking collectives  22.5 us (11%)
  matrix products  15.7 us (8%)
  local copies, waits for them, and re-layouts  8.24 us (4%)
  other arithmetic  3.11 us (2%)
    ppermute x16, starting transfers between devices, shift(): return lax.ppermute(value, axis, [(i, (i + by) % n) for i in range(n)])  78.7 us
    all_to_all x7, starting transfers between devices, exchange(): return lax.all_to_all(pieces, axis, split_axis=0, concat_axis=0, tiled=True)  39.9 us
    all_to_all x2, blocking collectives, exchange(): return lax.all_to_all(pieces, axis, split_axis=0, concat_axis=0, tiled=True)  22.5 us
    ppermute x16, waiting for transfers between devices, shift(): return lax.ppermute(value, axis, [(i, (i + by) % n) for i in range(n)])  16.8 us
    all_to_all x7, waiting for transfers between devices, exchange(): return lax.all_to_all(pieces, axis, split_axis=0, concat_axis=0, tiled=True)  13.3 us
    dot_general x5, matrix products, dot(): return jnp.dot(a, b, preferred_element_type=F32)  7.72 us
    dot_general x2, matrix products, grad_of(): jnp.einsum('tf,td->fd', units, own_slopes, preferred_element_type=F32)  4.89 us
    broadcast_in_dim x5, local copies, waits for them, and re-layouts, gather(): jnp.broadcast_to(value, (lax.axis_size(axis), *value.shape))  4.22 us
  transfers between devices with their start and end apart: 23, of which 5 were waited for; matrix products, arithmetic and copies ran while one was open for 10% of the time, Pallas kernels for 0%

profile of v3, /device:TPU:1, one launch (start us, length us, event | category | flops | bytes accessed | tf_op | source)
XLA Modules:
  0.0 199.4 jit_solution(13596792094946066239)
XLA Ops:
  2.1 13.1 %all-to-all-start = ((bf16[8,16,768]{2,1,0:T(8,128)(2,1)}), bf16[8,16,768]{2,1,0:T(8,128)(2,1)S(1)}, u32[]{:S(2)}, u32[]{:S(2)}) async-start(bf16[8,16,768]{2,1,0:T(8,128)(2,1)} %broadcast_in_dim.27), calls=%async_computation | async-start | bytes 393216 | tf_op jit(solution)/shard_map/all_to_all | solution.py:21
  15.2 4.6 %collective-permute-start.2 = (bf16[256,768]{1,0:T(8,128)(2,1)}, bf16[256,768]{1,0:T(8,128)(2,1)S(1)}, u32[]{:S(2)}, u32[]{:S(2)}) collective-permute-start(bf16[256,768]{1,0:T(8,128)(2,1)} %param.9), channel_id=1, source_target_pairs={{0,3},{1,0},{2,1},{3,2},{4,7},{5,4},{6,5},{7,6},{8,11},{9,8},{10,9... | collective-permute-start | bytes 1179656 | tf_op jit(solution)/shard_map/ppermute | solution.py:34
  19.8 2.3 %collective-permute-start.3 = (bf16[256,768]{1,0:T(8,128)(2,1)}, bf16[256,768]{1,0:T(8,128)(2,1)S(1)}, u32[]{:S(2)}, u32[]{:S(2)}) collective-permute-start(bf16[256,768]{1,0:T(8,128)(2,1)} %param.9), channel_id=1, source_target_pairs={{0,2},{1,3},{2,0},{3,1},{4,6},{5,7},{6,4},{7,5},{8,10},{9,11},{10,... | collective-permute-start | bytes 1179656 | tf_op jit(solution)/shard_map/ppermute | solution.py:34
  22.1 2.6 %collective-permute-start.4 = (bf16[256,768]{1,0:T(8,128)(2,1)}, bf16[256,768]{1,0:T(8,128)(2,1)S(1)}, u32[]{:S(2)}, u32[]{:S(2)}) collective-permute-start(bf16[256,768]{1,0:T(8,128)(2,1)} %param.9), channel_id=1, source_target_pairs={{0,1},{1,2},{2,3},{3,0},{4,5},{5,6},{6,7},{7,4},{8,9},{9,10},{10,1... | collective-permute-start | bytes 1179656 | tf_op jit(solution)/shard_map/ppermute | solution.py:34
  24.7 3.7 %collective-permute-start = (bf16[768,256]{1,0:T(8,128)(2,1)}, bf16[768,256]{1,0:T(8,128)(2,1)S(1)}, u32[]{:S(2)}, u32[]{:S(2)}) collective-permute-start(bf16[768,256]{1,0:T(8,128)(2,1)} %param.8), channel_id=1, source_target_pairs={{0,8},{8,0},{1,9},{9,1},{2,10},{10,2},{3,11},{11,3},{4,12},{12,4},... | collective-permute-start | bytes 1179656 | tf_op jit(solution)/shard_map/ppermute | solution.py:34
  29.4 4.0 %all-to-all-start.1 = ((bf16[4,8,16,768]{3,2,1,0:T(8,128)(2,1)}), bf16[4,8,16,768]{3,2,1,0:T(8,128)(2,1)S(1)}, u32[]{:S(2)}, u32[]{:S(2)}) async-start(bf16[4,8,16,768]{3,2,1,0:T(8,128)(2,1)} %broadcast_in_dim.28), calls=%async_computation.1 | async-start | bytes 1572864 | tf_op jit(solution)/shard_map/all_to_all | solution.py:21
  35.9 7.0 %collective-permute-done.4 = bf16[256,768]{1,0:T(8,128)(2,1)S(1)} collective-permute-done((bf16[256,768]{1,0:T(8,128)(2,1)}, bf16[256,768]{1,0:T(8,128)(2,1)S(1)}, u32[]{:S(2)}, u32[]{:S(2)}) %collective-permute-start.4) | collective-permute-done | bytes 393248 | tf_op jit(solution)/shard_map/ppermute | solution.py:34
  43.7 2.4 %collective-permute-start.5 = (bf16[256,3072]{1,0:T(8,128)(2,1)}, bf16[256,3072]{1,0:T(8,128)(2,1)}, u32[]{:S(2)}, u32[]{:S(2)}) collective-permute-start(bf16[256,3072]{1,0:T(8,128)(2,1)} %constant_dynamic-update-slice_fusion), channel_id=1, source_target_pairs={{0,8},{8,0},{1,9},{9,1},{2,10},{10,2},{3,11},{11,3},{4,12},{12,4},... | collective-permute-start | bytes 4718600 | tf_op jit(solution)/shard_map/ppermute | solution.py:34
  49.5 3.5 %all-to-all-start.2 = ((bf16[4,128,512]{2,1,0:T(8,128)(2,1)}), bf16[4,128,512]{2,1,0:T(8,128)(2,1)S(1)}, u32[]{:S(2)}, u32[]{:S(2)}) async-start(bf16[4,128,512]{2,1,0:T(8,128)(2,1)} %bitcast.2), calls=%async_computation.2 | async-start | bytes 1048576 | tf_op jit(solution)/shard_map/all_to_all | solution.py:21
  53.7 8.2 %all-to-all-done.2 = bf16[4,128,512]{2,1,0:T(8,128)(2,1)S(1)} async-done(((bf16[4,128,512]{2,1,0:T(8,128)(2,1)}), bf16[4,128,512]{2,1,0:T(8,128)(2,1)S(1)}, u32[]{:S(2)}, u32[]{:S(2)}) %all-to-all-start.2) | async-done | bytes 524320 | tf_op jit(solution)/shard_map/all_to_all | solution.py:21
  62.0 3.3 %all-to-all-start.3 = ((bf16[4,2,4,768]{3,2,1,0:T(4,128)(2,1)}), bf16[4,2,4,768]{3,2,1,0:T(4,128)(2,1)S(1)}, u32[]{:S(2)}, u32[]{:S(2)}) async-start(bf16[4,2,4,768]{3,2,1,0:T(4,128)(2,1)} %pad_maximum_fusion.9), calls=%async_computation.3 | async-start | bytes 98304 | tf_op jit(solution)/shard_map/all_to_all | solution.py:21
  65.3 7.9 %collective-permute-start.1 = (bf16[128,512]{1,0:T(8,128)(2,1)S(1)}, bf16[128,512]{1,0:T(8,128)(2,1)S(1)}, u32[]{:S(2)}, u32[]{:S(2)}) collective-permute-start(bf16[128,512]{1,0:T(8,128)(2,1)S(1)} %convert_element_type.91), channel_id=1, source_target_pairs={{0,4},{4,0},{1,5},{5,1},{2,6},{6,2},{3,7},{7,3},{8,12},{12,8},{9,1... | collective-permute-start | bytes 393224 | tf_op jit(solution)/shard_map/ppermute | solution.py:34
  73.4 6.7 %collective-permute-done.1 = bf16[128,512]{1,0:T(8,128)(2,1)S(1)} collective-permute-done((bf16[128,512]{1,0:T(8,128)(2,1)S(1)}, bf16[128,512]{1,0:T(8,128)(2,1)S(1)}, u32[]{:S(2)}, u32[]{:S(2)}) %collective-permute-start.1) | collective-permute-done | bytes 131104 | tf_op jit(solution)/shard_map/ppermute | solution.py:34
  80.2 2.5 %fusion = bf16[128,3072]{1,0:T(8,128)(2,1)S(1)} fusion(bf16[128,512]{1,0:T(8,128)(2,1)S(1)} %multiply_convert_fusion, bf16[256,3072]{1,0:T(8,128)(2,1)} %collective-permute-done.5, bf16[256,3072]{1,0:T(8,128)(2,1)} %constant_dynamic-update-slice_fusion), kind=kOutput, calls=%fused_computation.1 | convolution fusion | flops 409731072 | bytes 4063232 | tf_op jit(solution)/shard_map/dot_general | solution.py:55
  82.6 14.5 %all_to_all.45 = bf16[4,32,3072]{2,1,0:T(8,128)(2,1)S(1)} all-to-all(bf16[4,32,3072]{2,1,0:T(8,128)(2,1)S(1)} %bitcast.26), channel_id=1, replica_groups=mesh['zq'=2,'za'=4,'x'=4,'c'=2,'zh'=2,'y'=4] {'x'}, dimensions={0} | all-to-all | bytes 1572864 | tf_op jit(solution)/shard_map/all_to_all | solution.py:21
  97.9 8.8 %all-to-all-start.5 = ((bf16[4,8,3072]{2,1,0:T(8,128)(2,1)}), bf16[4,8,3072]{2,1,0:T(8,128)(2,1)S(1)}, u32[]{:S(2)}, u32[]{:S(2)}) async-start(bf16[4,8,3072]{2,1,0:T(8,128)(2,1)} %bitcast.8), calls=%async_computation.5 | async-start | bytes 393216 | tf_op jit(solution)/shard_map/all_to_all | solution.py:21
  106.7 5.1 %all-to-all-done.5 = bf16[4,8,3072]{2,1,0:T(8,128)(2,1)S(1)} async-done(((bf16[4,8,3072]{2,1,0:T(8,128)(2,1)}), bf16[4,8,3072]{2,1,0:T(8,128)(2,1)S(1)}, u32[]{:S(2)}, u32[]{:S(2)}) %all-to-all-start.5) | async-done | bytes 196640 | tf_op jit(solution)/shard_map/all_to_all | solution.py:21
  111.9 12.5 %collective-permute-start.6 = (bf16[8,3072]{1,0:T(8,128)(2,1)S(1)}, bf16[8,3072]{1,0:T(8,128)(2,1)S(1)}, u32[]{:S(2)}, u32[]{:S(2)}) collective-permute-start(bf16[8,3072]{1,0:T(8,128)(2,1)S(1)} %fusion.50), channel_id=1, source_target_pairs={{0,256},{256,0},{1,257},{257,1},{2,258},{258,2},{3,259},{259,3},{4... | collective-permute-start | bytes 147464 | tf_op jit(solution)/shard_map/ppermute | solution.py:34
  124.5 3.0 %collective-permute-done.6 = bf16[8,3072]{1,0:T(8,128)(2,1)S(1)} collective-permute-done((bf16[8,3072]{1,0:T(8,128)(2,1)S(1)}, bf16[8,3072]{1,0:T(8,128)(2,1)S(1)}, u32[]{:S(2)}, u32[]{:S(2)}) %collective-permute-start.6) | collective-permute-done | bytes 49184 | tf_op jit(solution)/shard_map/ppermute | solution.py:34
  127.6 8.0 %all_to_all.46 = bf16[4,8,3072]{2,1,0:T(8,128)(2,1)S(1)} all-to-all(bf16[4,8,3072]{2,1,0:T(8,128)(2,1)S(1)} %broadcast_in_dim.31), channel_id=1, replica_groups=mesh['zq'=2,'za'=4,'x'=4,'c'=2,'zh'=2,'y'=4] {'za'}, dimensions={0} | all-to-all | bytes 393216 | tf_op jit(solution)/shard_map/all_to_all | solution.py:21
  136.6 3.5 %all-to-all-start.7 = ((bf16[4,4,8,3072]{3,2,1,0:T(8,128)(2,1)}), bf16[4,4,8,3072]{3,2,1,0:T(8,128)(2,1)S(1)}, u32[]{:S(2)}, u32[]{:S(2)}) async-start(bf16[4,4,8,3072]{3,2,1,0:T(8,128)(2,1)} %broadcast_in_dim.32), calls=%async_computation.7 | async-start | bytes 1572864 | tf_op jit(solution)/shard_map/all_to_all | solution.py:21
  140.1 4.5 %collective-permute-start.11 = (bf16[128,512]{1,0:T(8,128)(2,1)S(1)}, bf16[128,512]{1,0:T(8,128)(2,1)}, u32[]{:S(2)}, u32[]{:S(2)}) collective-permute-start(bf16[128,512]{1,0:T(8,128)(2,1)S(1)} %multiply_convert_fusion), channel_id=1, source_target_pairs={{0,3},{1,0},{2,1},{3,2},{4,7},{5,4},{6,5},{7,6},{8,11},{9,8},{10,9... | collective-permute-start | bytes 393224 | tf_op jit(solution)/shard_map/ppermute | solution.py:34
  144.6 2.5 %collective-permute-start.10 = (bf16[128,512]{1,0:T(8,128)(2,1)S(1)}, bf16[128,512]{1,0:T(8,128)(2,1)}, u32[]{:S(2)}, u32[]{:S(2)}) collective-permute-start(bf16[128,512]{1,0:T(8,128)(2,1)S(1)} %multiply_convert_fusion), channel_id=1, source_target_pairs={{0,2},{1,3},{2,0},{3,1},{4,6},{5,7},{6,4},{7,5},{8,10},{9,11},{10,... | collective-permute-start | bytes 393224 | tf_op jit(solution)/shard_map/ppermute | solution.py:34
  147.1 2.5 %collective-permute-start.9 = (bf16[128,512]{1,0:T(8,128)(2,1)S(1)}, bf16[128,512]{1,0:T(8,128)(2,1)}, u32[]{:S(2)}, u32[]{:S(2)}) collective-permute-start(bf16[128,512]{1,0:T(8,128)(2,1)S(1)} %multiply_convert_fusion), channel_id=1, source_target_pairs={{0,1},{1,2},{2,3},{3,0},{4,5},{5,6},{6,7},{7,4},{8,9},{9,10},{10,1... | collective-permute-start | bytes 393224 | tf_op jit(solution)/shard_map/ppermute | solution.py:34
  149.6 3.1 %fusion.75 = (bf16[128,512]{1,0:T(8,128)(2,1)S(1)}, f32[128,512]{1,0:T(8,128)S(1)}) fusion(bf16[128,3072]{1,0:T(8,128)(2,1)S(1)} %bitcast.21, bf16[256,3072]{1,0:T(8,128)(2,1)} %collective-permute-done.5, bf16[256,3072]{1,0:T(8,128)(2,1)} %constant_dynamic-update-slice_fusion), kind=kOutput, calls=%fused_computation.120 | convolution fusion | flops 409075712 | bytes 4325376 | tf_op jit(solution)/shard_map/td,fd->tf/dot_general | solution.py:105
  152.7 7.9 %collective-permute-start.7 = (bf16[128,512]{1,0:T(8,128)(2,1)S(1)}, bf16[128,512]{1,0:T(8,128)(2,1)S(1)}, u32[]{:S(2)}, u32[]{:S(2)}) collective-permute-start(bf16[128,512]{1,0:T(8,128)(2,1)S(1)} %get-tuple-element.24), channel_id=1, source_target_pairs={{0,4},{4,0},{1,5},{5,1},{2,6},{6,2},{3,7},{7,3},{8,12},{12,8},{9,1... | collective-permute-start | bytes 393224 | tf_op jit(solution)/shard_map/ppermute | solution.py:34
  161.4 4.0 %collective-permute-start.14 = (bf16[128,768]{1,0:T(8,128)(2,1)}, bf16[128,768]{1,0:T(8,128)(2,1)}, u32[]{:S(2)}, u32[]{:S(2)}) collective-permute-start(bf16[128,768]{1,0:T(8,128)(2,1)} %get-tuple-element.17), channel_id=1, source_target_pairs={{0,3},{1,0},{2,1},{3,2},{4,7},{5,4},{6,5},{7,6},{8,11},{9,8},{10,9... | collective-permute-start | bytes 589832 | tf_op jit(solution)/shard_map/ppermute | solution.py:34
  165.4 3.1 %collective-permute-start.13 = (bf16[128,768]{1,0:T(8,128)(2,1)S(1)}, bf16[128,768]{1,0:T(8,128)(2,1)}, u32[]{:S(2)}, u32[]{:S(2)}) collective-permute-start(bf16[128,768]{1,0:T(8,128)(2,1)S(1)} %get-tuple-element.18), channel_id=1, source_target_pairs={{0,2},{1,3},{2,0},{3,1},{4,6},{5,7},{6,4},{7,5},{8,10},{9,11},{10,... | collective-permute-start | bytes 589832 | tf_op jit(solution)/shard_map/ppermute | solution.py:34
  171.6 3.7 %all-to-all-start.8 = ((bf16[4,128,512]{2,1,0:T(8,128)(2,1)}), bf16[4,128,512]{2,1,0:T(8,128)(2,1)S(1)}, u32[]{:S(2)}, u32[]{:S(2)}) async-start(bf16[4,128,512]{2,1,0:T(8,128)(2,1)} %broadcast_in_dim.33), calls=%async_computation.8 | async-start | bytes 1048576 | tf_op jit(solution)/shard_map/all_to_all | solution.py:21
  178.7 11.7 %collective-permute-start.15 = (bf16[256,768]{1,0:T(8,128)(2,1)}, bf16[256,768]{1,0:T(8,128)(2,1)S(1)}, u32[]{:S(2)}, u32[]{:S(2)}) collective-permute-start(bf16[256,768]{1,0:T(8,128)(2,1)} %fusion.5), channel_id=1, source_target_pairs={{0,8},{8,0},{1,9},{9,1},{2,10},{10,2},{3,11},{11,3},{4,12},{12,4},... | collective-permute-start | bytes 1179656 | tf_op jit(solution)/shard_map/ppermute | solution.py:34
  190.9 4.4 %collective-permute-start.8 = (bf16[768,256]{1,0:T(8,128)(2,1)S(1)}, bf16[768,256]{1,0:T(8,128)(2,1)S(1)}, u32[]{:S(2)}, u32[]{:S(2)}) collective-permute-start(bf16[768,256]{1,0:T(8,128)(2,1)S(1)} %fusion.4), channel_id=1, source_target_pairs={{0,8},{8,0},{1,9},{9,1},{2,10},{10,2},{3,11},{11,3},{4,12},{12,4},... | collective-permute-start | bytes 1179656 | tf_op jit(solution)/shard_map/ppermute | solution.py:34
  195.3 2.6 %multiply_add_fusion = (f32[256,768]{1,0:T(8,128)}, bf16[256,768]{1,0:T(8,128)(2,1)}) fusion(bf16[256,768]{1,0:T(8,128)(2,1)S(1)} %copy-done.2, f32[256,768]{1,0:T(8,128)S(1)} %copy-done.5, bf16[256,768]{1,0:T(8,128)(2,1)S(1)} %collective-permute-done.15, bf16[128,768]{1,0:T(8,128)(2,1)} %collective-permute-done.14, ...), kind=kOutput, calls=%fused_computation.36 | convolution fusion | flops 206438400 | bytes 3801088 | tf_op jit(solution)/shard_map/tf,td->fd/dot_general | solution.py:117
  (68 shorter events, 21.0 us)
Async XLA Ops:
  0.6 32.8 %copy-start.2 = (bf16[256,768]{1,0:T(8,128)(2,1)S(1)}, bf16[256,768]{1,0:T(8,128)(2,1)}, u32[]{:S(2)}) copy-start(bf16[256,768]{1,0:T(8,128)(2,1)} %param.9) | copy-start | bytes 1179652
  2.1 26.3 %all-to-all-start = ((bf16[8,16,768]{2,1,0:T(8,128)(2,1)}), bf16[8,16,768]{2,1,0:T(8,128)(2,1)S(1)}, u32[]{:S(2)}, u32[]{:S(2)}) async-start(bf16[8,16,768]{2,1,0:T(8,128)(2,1)} %broadcast_in_dim.27), calls=%async_computation | async-start | bytes 393216 | tf_op jit(solution)/shard_map/all_to_all | solution.py:21
  15.2 19.1 %collective-permute-start.2 = (bf16[256,768]{1,0:T(8,128)(2,1)}, bf16[256,768]{1,0:T(8,128)(2,1)S(1)}, u32[]{:S(2)}, u32[]{:S(2)}) collective-permute-start(bf16[256,768]{1,0:T(8,128)(2,1)} %param.9), channel_id=1, source_target_pairs={{0,3},{1,0},{2,1},{3,2},{4,7},{5,4},{6,5},{7,6},{8,11},{9,8},{10,9... | collective-permute-start | bytes 1179656 | tf_op jit(solution)/shard_map/ppermute | solution.py:34
  19.8 15.2 %collective-permute-start.3 = (bf16[256,768]{1,0:T(8,128)(2,1)}, bf16[256,768]{1,0:T(8,128)(2,1)S(1)}, u32[]{:S(2)}, u32[]{:S(2)}) collective-permute-start(bf16[256,768]{1,0:T(8,128)(2,1)} %param.9), channel_id=1, source_target_pairs={{0,2},{1,3},{2,0},{3,1},{4,6},{5,7},{6,4},{7,5},{8,10},{9,11},{10,... | collective-permute-start | bytes 1179656 | tf_op jit(solution)/shard_map/ppermute | solution.py:34
  22.1 20.8 %collective-permute-start.4 = (bf16[256,768]{1,0:T(8,128)(2,1)}, bf16[256,768]{1,0:T(8,128)(2,1)S(1)}, u32[]{:S(2)}, u32[]{:S(2)}) collective-permute-start(bf16[256,768]{1,0:T(8,128)(2,1)} %param.9), channel_id=1, source_target_pairs={{0,1},{1,2},{2,3},{3,0},{4,5},{5,6},{6,7},{7,4},{8,9},{9,10},{10,1... | collective-permute-start | bytes 1179656 | tf_op jit(solution)/shard_map/ppermute | solution.py:34
  24.7 23.4 %collective-permute-start = (bf16[768,256]{1,0:T(8,128)(2,1)}, bf16[768,256]{1,0:T(8,128)(2,1)S(1)}, u32[]{:S(2)}, u32[]{:S(2)}) collective-permute-start(bf16[768,256]{1,0:T(8,128)(2,1)} %param.8), channel_id=1, source_target_pairs={{0,8},{8,0},{1,9},{9,1},{2,10},{10,2},{3,11},{11,3},{4,12},{12,4},... | collective-permute-start | bytes 1179656 | tf_op jit(solution)/shard_map/ppermute | solution.py:34
  29.4 16.7 %all-to-all-start.1 = ((bf16[4,8,16,768]{3,2,1,0:T(8,128)(2,1)}), bf16[4,8,16,768]{3,2,1,0:T(8,128)(2,1)S(1)}, u32[]{:S(2)}, u32[]{:S(2)}) async-start(bf16[4,8,16,768]{3,2,1,0:T(8,128)(2,1)} %broadcast_in_dim.28), calls=%async_computation.1 | async-start | bytes 1572864 | tf_op jit(solution)/shard_map/all_to_all | solution.py:21
  43.7 36.4 %collective-permute-start.5 = (bf16[256,3072]{1,0:T(8,128)(2,1)}, bf16[256,3072]{1,0:T(8,128)(2,1)}, u32[]{:S(2)}, u32[]{:S(2)}) collective-permute-start(bf16[256,3072]{1,0:T(8,128)(2,1)} %constant_dynamic-update-slice_fusion), channel_id=1, source_target_pairs={{0,8},{8,0},{1,9},{9,1},{2,10},{10,2},{3,11},{11,3},{4,12},{12,4},... | collective-permute-start | bytes 4718600 | tf_op jit(solution)/shard_map/ppermute | solution.py:34
  46.1 2.0 %copy-start.1 = (bf16[768,256]{1,0:T(8,128)(2,1)S(1)}, bf16[768,256]{1,0:T(8,128)(2,1)}, u32[]{:S(2)}) copy-start(bf16[768,256]{1,0:T(8,128)(2,1)} %param.8) | copy-start | bytes 1179652
  48.1 4.9 %copy-start.3 = (bf16[16,768]{1,0:T(8,128)(2,1)S(1)}, bf16[16,768]{1,0:T(8,128)(2,1)}, u32[]{:S(2)}) copy-start(bf16[16,768]{1,0:T(8,128)(2,1)} %param.6) | copy-start | bytes 73732
  48.1 4.9 %copy-start.4 = (bf16[16,768]{1,0:T(8,128)(2,1)S(1)}, bf16[16,768]{1,0:T(8,128)(2,1)}, u32[]{:S(2)}) copy-start(bf16[16,768]{1,0:T(8,128)(2,1)} %param.7) | copy-start | bytes 73732
  49.5 12.4 %all-to-all-start.2 = ((bf16[4,128,512]{2,1,0:T(8,128)(2,1)}), bf16[4,128,512]{2,1,0:T(8,128)(2,1)S(1)}, u32[]{:S(2)}, u32[]{:S(2)}) async-start(bf16[4,128,512]{2,1,0:T(8,128)(2,1)} %bitcast.2), calls=%async_computation.2 | async-start | bytes 1048576 | tf_op jit(solution)/shard_map/all_to_all | solution.py:21
  62.0 11.3 %all-to-all-start.3 = ((bf16[4,2,4,768]{3,2,1,0:T(4,128)(2,1)}), bf16[4,2,4,768]{3,2,1,0:T(4,128)(2,1)S(1)}, u32[]{:S(2)}, u32[]{:S(2)}) async-start(bf16[4,2,4,768]{3,2,1,0:T(4,128)(2,1)} %pad_maximum_fusion.9), calls=%async_computation.3 | async-start | bytes 98304 | tf_op jit(solution)/shard_map/all_to_all | solution.py:21
  65.3 14.7 %collective-permute-start.1 = (bf16[128,512]{1,0:T(8,128)(2,1)S(1)}, bf16[128,512]{1,0:T(8,128)(2,1)S(1)}, u32[]{:S(2)}, u32[]{:S(2)}) collective-permute-start(bf16[128,512]{1,0:T(8,128)(2,1)S(1)} %convert_element_type.91), channel_id=1, source_target_pairs={{0,4},{4,0},{1,5},{5,1},{2,6},{6,2},{3,7},{7,3},{8,12},{12,8},{9,1... | collective-permute-start | bytes 393224 | tf_op jit(solution)/shard_map/ppermute | solution.py:34
  97.9 13.9 %all-to-all-start.5 = ((bf16[4,8,3072]{2,1,0:T(8,128)(2,1)}), bf16[4,8,3072]{2,1,0:T(8,128)(2,1)S(1)}, u32[]{:S(2)}, u32[]{:S(2)}) async-start(bf16[4,8,3072]{2,1,0:T(8,128)(2,1)} %bitcast.8), calls=%async_computation.5 | async-start | bytes 393216 | tf_op jit(solution)/shard_map/all_to_all | solution.py:21
  111.9 15.6 %collective-permute-start.6 = (bf16[8,3072]{1,0:T(8,128)(2,1)S(1)}, bf16[8,3072]{1,0:T(8,128)(2,1)S(1)}, u32[]{:S(2)}, u32[]{:S(2)}) collective-permute-start(bf16[8,3072]{1,0:T(8,128)(2,1)S(1)} %fusion.50), channel_id=1, source_target_pairs={{0,256},{256,0},{1,257},{257,1},{2,258},{258,2},{3,259},{259,3},{4... | collective-permute-start | bytes 147464 | tf_op jit(solution)/shard_map/ppermute | solution.py:34
  136.6 13.0 %all-to-all-start.7 = ((bf16[4,4,8,3072]{3,2,1,0:T(8,128)(2,1)}), bf16[4,4,8,3072]{3,2,1,0:T(8,128)(2,1)S(1)}, u32[]{:S(2)}, u32[]{:S(2)}) async-start(bf16[4,4,8,3072]{3,2,1,0:T(8,128)(2,1)} %broadcast_in_dim.32), calls=%async_computation.7 | async-start | bytes 1572864 | tf_op jit(solution)/shard_map/all_to_all | solution.py:21
  140.1 25.3 %collective-permute-start.11 = (bf16[128,512]{1,0:T(8,128)(2,1)S(1)}, bf16[128,512]{1,0:T(8,128)(2,1)}, u32[]{:S(2)}, u32[]{:S(2)}) collective-permute-start(bf16[128,512]{1,0:T(8,128)(2,1)S(1)} %multiply_convert_fusion), channel_id=1, source_target_pairs={{0,3},{1,0},{2,1},{3,2},{4,7},{5,4},{6,5},{7,6},{8,11},{9,8},{10,9... | collective-permute-start | bytes 393224 | tf_op jit(solution)/shard_map/ppermute | solution.py:34
  144.6 30.7 %collective-permute-start.10 = (bf16[128,512]{1,0:T(8,128)(2,1)S(1)}, bf16[128,512]{1,0:T(8,128)(2,1)}, u32[]{:S(2)}, u32[]{:S(2)}) collective-permute-start(bf16[128,512]{1,0:T(8,128)(2,1)S(1)} %multiply_convert_fusion), channel_id=1, source_target_pairs={{0,2},{1,3},{2,0},{3,1},{4,6},{5,7},{6,4},{7,5},{8,10},{9,11},{10,... | collective-permute-start | bytes 393224 | tf_op jit(solution)/shard_map/ppermute | solution.py:34
  147.1 28.3 %collective-permute-start.9 = (bf16[128,512]{1,0:T(8,128)(2,1)S(1)}, bf16[128,512]{1,0:T(8,128)(2,1)}, u32[]{:S(2)}, u32[]{:S(2)}) collective-permute-start(bf16[128,512]{1,0:T(8,128)(2,1)S(1)} %multiply_convert_fusion), channel_id=1, source_target_pairs={{0,1},{1,2},{2,3},{3,0},{4,5},{5,6},{6,7},{7,4},{8,9},{9,10},{10,1... | collective-permute-start | bytes 393224 | tf_op jit(solution)/shard_map/ppermute | solution.py:34
  152.7 15.8 %collective-permute-start.7 = (bf16[128,512]{1,0:T(8,128)(2,1)S(1)}, bf16[128,512]{1,0:T(8,128)(2,1)S(1)}, u32[]{:S(2)}, u32[]{:S(2)}) collective-permute-start(bf16[128,512]{1,0:T(8,128)(2,1)S(1)} %get-tuple-element.24), channel_id=1, source_target_pairs={{0,4},{4,0},{1,5},{5,1},{2,6},{6,2},{3,7},{7,3},{8,12},{12,8},{9,1... | collective-permute-start | bytes 393224 | tf_op jit(solution)/shard_map/ppermute | solution.py:34
  161.4 15.1 %collective-permute-start.14 = (bf16[128,768]{1,0:T(8,128)(2,1)}, bf16[128,768]{1,0:T(8,128)(2,1)}, u32[]{:S(2)}, u32[]{:S(2)}) collective-permute-start(bf16[128,768]{1,0:T(8,128)(2,1)} %get-tuple-element.17), channel_id=1, source_target_pairs={{0,3},{1,0},{2,1},{3,2},{4,7},{5,4},{6,5},{7,6},{8,11},{9,8},{10,9... | collective-permute-start | bytes 589832 | tf_op jit(solution)/shard_map/ppermute | solution.py:34
  165.4 11.1 %collective-permute-start.13 = (bf16[128,768]{1,0:T(8,128)(2,1)S(1)}, bf16[128,768]{1,0:T(8,128)(2,1)}, u32[]{:S(2)}, u32[]{:S(2)}) collective-permute-start(bf16[128,768]{1,0:T(8,128)(2,1)S(1)} %get-tuple-element.18), channel_id=1, source_target_pairs={{0,2},{1,3},{2,0},{3,1},{4,6},{5,7},{6,4},{7,5},{8,10},{9,11},{10,... | collective-permute-start | bytes 589832 | tf_op jit(solution)/shard_map/ppermute | solution.py:34
  168.5 8.0 %collective-permute-start.12 = (bf16[128,768]{1,0:T(8,128)(2,1)S(1)}, bf16[128,768]{1,0:T(8,128)(2,1)}, u32[]{:S(2)}, u32[]{:S(2)}) collective-permute-start(bf16[128,768]{1,0:T(8,128)(2,1)S(1)} %get-tuple-element.19), channel_id=1, source_target_pairs={{0,1},{1,2},{2,3},{3,0},{4,5},{5,6},{6,7},{7,4},{8,9},{9,10},{10,1... | collective-permute-start | bytes 589832 | tf_op jit(solution)/shard_map/ppermute | solution.py:34
  171.6 18.8 %all-to-all-start.8 = ((bf16[4,128,512]{2,1,0:T(8,128)(2,1)}), bf16[4,128,512]{2,1,0:T(8,128)(2,1)S(1)}, u32[]{:S(2)}, u32[]{:S(2)}) async-start(bf16[4,128,512]{2,1,0:T(8,128)(2,1)} %broadcast_in_dim.33), calls=%async_computation.8 | async-start | bytes 1048576 | tf_op jit(solution)/shard_map/all_to_all | solution.py:21
  178.7 16.5 %collective-permute-start.15 = (bf16[256,768]{1,0:T(8,128)(2,1)}, bf16[256,768]{1,0:T(8,128)(2,1)S(1)}, u32[]{:S(2)}, u32[]{:S(2)}) collective-permute-start(bf16[256,768]{1,0:T(8,128)(2,1)} %fusion.5), channel_id=1, source_target_pairs={{0,8},{8,0},{1,9},{9,1},{2,10},{10,2},{3,11},{11,3},{4,12},{12,4},... | collective-permute-start | bytes 1179656 | tf_op jit(solution)/shard_map/ppermute | solution.py:34
  190.4 4.8 %copy-start.5 = (f32[256,768]{1,0:T(8,128)S(1)}, f32[256,768]{1,0:T(8,128)}, u32[]{:S(2)}) copy-start(f32[256,768]{1,0:T(8,128)} %param.11) | copy-start | bytes 2359300
  190.9 7.0 %copy-start = (f32[768,256]{1,0:T(8,128)S(1)}, f32[768,256]{1,0:T(8,128)}, u32[]{:S(2)}) copy-start(f32[768,256]{1,0:T(8,128)} %param.10) | copy-start | bytes 2359300
  190.9 7.0 %collective-permute-start.8 = (bf16[768,256]{1,0:T(8,128)(2,1)S(1)}, bf16[768,256]{1,0:T(8,128)(2,1)S(1)}, u32[]{:S(2)}, u32[]{:S(2)}) collective-permute-start(bf16[768,256]{1,0:T(8,128)(2,1)S(1)} %fusion.4), channel_id=1, source_target_pairs={{0,8},{8,0},{1,9},{9,1},{2,10},{10,2},{3,11},{11,3},{4,12},{12,4},... | collective-permute-start | bytes 1179656 | tf_op jit(solution)/shard_map/ppermute | solution.py:34

commit v4 on v3

v4 whole, which is shorter than its diff:
```python
import math

import jax
import jax.numpy as jnp
import numpy as np
from jax import lax
from jax.experimental.layout import Layout, with_layout_constraint
from jax.sharding import Mesh
from jax.sharding import PartitionSpec as P

D = 6144
FF = 16384
DP = ("zq", "za", "x", "c")
MP = ("zh", "y")
BF = jnp.bfloat16
F32 = jnp.float32

decay_rate = 0.99
step_size = 0.5


def exchange(pieces, axis):
    return lax.all_to_all(pieces, axis, split_axis=0, concat_axis=0, tiled=True)


def gather(value, axis):
    return exchange(jnp.broadcast_to(value, (lax.axis_size(axis), *value.shape)), axis)


def scatter(partial, axis):
    return exchange(partial.astype(BF), axis).astype(F32).sum(axis=0)


def shift(value, axis, by):
    n = lax.axis_size(axis)
    return lax.ppermute(value, axis, [(i, (i + by) % n) for i in range(n)])


def gelu_value(value):
    return 0.5 * value * (1.0 + jax.scipy.special.erf(value * (1.0 / math.sqrt(2.0))))


def gelu_slope(value):
    normal_cdf = 0.5 * (1.0 + jax.scipy.special.erf(value * (1.0 / math.sqrt(2.0))))
    return normal_cdf + value * jnp.exp(-0.5 * value * value) * (1.0 / math.sqrt(2.0 * math.pi))


def ema(teacher, student, grad):
    return decay_rate * teacher + (1.0 - decay_rate) * (student.astype(F32) - step_size * grad)


def tie(*values):
    return lax.optimization_barrier(values)


def dot(a, b):
    return jnp.dot(a, b, preferred_element_type=F32)


def shards(inputs, targets, w_in, w_out, teach_in, teach_out):
    in_scale = 1.0 / math.sqrt(D)
    out_scale = 1.0 / math.sqrt(FF)
    rows, d = inputs.shape
    f = w_in.shape[1]
    nx, na, nq, ny = (lax.axis_size(a) for a in ("x", "za", "zq", "y"))
    blocks = nx * na * nq
    tokens = blocks * rows
    part = tokens // ny
    few = rows // ny
    y = lax.axis_index("y")

    w_both = shift(w_in, "c", 1)
    w_ring = [w_out, shift(w_out, "y", -1), None, shift(w_out, "y", 1)]
    near = gather(inputs, ("za", "zq"))
    near, w_both, w_ring[1], w_ring[3], w_later = tie(near, w_both, w_ring[1], w_ring[3], w_out)
    w_ring[2] = shift(w_later, "y", 2)
    w_both = jnp.concatenate([w_in, w_both], axis=1)

    arrived = gather(near, "x").reshape(tokens, d)
    arrived, w_both, *w_ring[1:] = tie(arrived, w_both, *w_ring[1:])
    at = np.arange(tokens)
    source = (at % part) // few * rows + at // part * few + at % few
    order = jnp.asarray(np.eye(tokens, dtype=np.float32)[source], BF)
    gathered = with_layout_constraint(dot(order, arrived).astype(BF), Layout((0, 1)))
    w_ring = jnp.concatenate(w_ring, axis=1)

    partial_pre = dot(gathered, w_both) * in_scale
    sums = scatter(partial_pre.reshape(ny, part, 2 * f), "y")

    sums, w_ring, arrived = tie(sums, w_ring, arrived)
    other = shift(sums.astype(BF), "zh", 1)
    w_ring_theirs = shift(w_ring, "c", 1)
    gathered_t = jnp.einsum("td,pt->dp", arrived, order, preferred_element_type=F32).astype(BF)

    both = jnp.stack([inputs.reshape(ny, few, d), targets.reshape(ny, few, d)], axis=1)
    both = exchange(both, "y")
    both = both.astype(F32)
    own = both[:, 0] - both[:, 1]
    own = jnp.concatenate(
        [lax.dynamic_index_in_dim(own, (y + k) & (ny - 1), keepdims=False) for k in range(ny)],
        axis=1,
    )
    own, other, gathered_t = tie(own, other, gathered_t)
    preact = sums + other.astype(F32)
    hidden = gelu_value(preact).astype(BF)
    hiddens = [shift(hidden, "y", k) for k in range(1, ny)]

    partial_out = (dot(hidden[:, :f], w_ring) + dot(hidden[:, f:], w_ring_theirs)) * out_scale
    sums = scatter(partial_out.reshape(nx, part // nx, ny * d), "x")
    sums, hiddens[0] = tie(sums, hiddens[0])
    sums = scatter(sums.reshape(na, nq * few, ny * d), "za")
    sums, hiddens[1] = tie(sums, hiddens[1])
    mine = lax.broadcasted_iota(jnp.int32, (nq * few, 1), 0) // few == lax.axis_index("zq")
    sums = sums + jnp.where(mine, jnp.concatenate([own] * nq, axis=0), 0.0)
    other = shift(sums.astype(BF), "zq", 1)
    other, hiddens[2] = tie(other, hiddens[2])
    slope = (sums + other.astype(F32)).astype(BF)
    slopes = gather(gather(slope, "za"), "x").reshape(part, ny * d)

    slope_part = out_scale * jnp.concatenate(
        [
            jnp.einsum("td,fd->tf", slopes, w, preferred_element_type=F32)
            for w in (w_ring, w_ring_theirs)
        ],
        axis=1,
    )
    slopes, slope_part = tie(slopes, slope_part)
    other = shift(slope_part.astype(BF), "zh", 1)
    their_slopes = [shift(slopes[:, k * d : (k + 1) * d], "y", k) for k in range(1, ny)]
    other, *their_slopes = tie(other, *their_slopes)
    hidden_slope = slope_part + other.astype(F32)
    pre_slope = (hidden_slope * gelu_slope(preact)).astype(BF)
    pre_slopes = gather(pre_slope, "y").reshape(tokens, 2 * f)

    hiddens = jnp.concatenate([hidden, *hiddens], axis=0)
    own_slopes = jnp.concatenate([slopes[:, :d], *their_slopes], axis=0)

    def grad_of(units):
        return jnp.einsum("tf,td->fd", units, own_slopes, preferred_element_type=F32) * out_scale

    theirs = shift(grad_of(hiddens[:, f:]).astype(BF), "c", 1).astype(F32)
    grad_out = grad_of(hiddens[:, :f]) + theirs
    new_out = ema(teach_out, w_out, grad_out)

    theirs = shift((dot(gathered_t, pre_slopes[:, f:]) * in_scale).astype(BF), "c", 1).astype(F32)
    grad_in = dot(gathered_t, pre_slopes[:, :f]) * in_scale + theirs
    new_in = ema(teach_in, w_in, grad_in)
    return (grad_in.astype(BF), grad_out.astype(BF), new_in, new_out)


def solution(mesh):
    finer = Mesh(mesh.devices.reshape(2, 4, 4, 2, 2, 4), (*DP, *MP))

    def step(*args):
        return shards(*args)

    step = jax.shard_map(
        step,
        mesh=finer,
        in_specs=(P(DP, MP), P(DP, MP), P(MP, DP), P(DP, MP), P(MP, DP), P(DP, MP)),
        out_specs=(P(MP, DP), P(DP, MP), P(MP, DP), P(DP, MP)),
        check_vma=False,
    )
    return step
```

time: 201 us -> 227 us (1.13)
  waiting for transfers between devices: 30.1 us -> 49.7 us
  other arithmetic: 3.11 us -> 10.6 us
  local copies, waits for them, and re-layouts: 8.24 us -> 5.39 us
    ppermute x16, waiting for transfers between devices: 16.8 us -> 33.4 us  [shift(): return lax.ppermute(value, axis, [(i, (i + by) % n) for i in range(n)])]
    all_to_all x7, waiting for transfers between devices: 13.3 us -> 16.4 us  [exchange(): return lax.all_to_all(pieces, axis, split_axis=0, concat_axis=0, tiled=True)]
  transfers between devices with their start and end apart: 23 -> 23, of which waited for: 5 -> 9; matrix products, arithmetic and copies ran while one was open for 10% -> 8% of each run, Pallas kernels for 0% -> 0%
where the time goes in v4:
time: 227 us; the launch traced here: 225 us
  starting transfers between devices  121 us (53%)
  waiting for transfers between devices  49.7 us (22%)
  blocking collectives  21.6 us (10%)
  matrix products  15.6 us (7%)
  other arithmetic  10.6 us (5%)
  local copies, waits for them, and re-layouts  5.39 us (2%)
    ppermute x16, starting transfers between devices, shift(): return lax.ppermute(value, axis, [(i, (i + by) % n) for i in range(n)])  80.5 us
    all_to_all x7, starting transfers between devices, exchange(): return lax.all_to_all(pieces, axis, split_axis=0, concat_axis=0, tiled=True)  40.6 us
    ppermute x16, waiting for transfers between devices, shift(): return lax.ppermute(value, axis, [(i, (i + by) % n) for i in range(n)])  33.4 us
    all_to_all x2, blocking collectives, exchange(): return lax.all_to_all(pieces, axis, split_axis=0, concat_axis=0, tiled=True)  21.6 us
    all_to_all x7, waiting for transfers between devices, exchange(): return lax.all_to_all(pieces, axis, split_axis=0, concat_axis=0, tiled=True)  16.4 us
    dot_general x5, matrix products, dot(): return jnp.dot(a, b, preferred_element_type=F32)  6.72 us
    dot_general x2, matrix products, grad_of(): jnp.einsum('tf,td->fd', units, own_slopes, preferred_element_type=F32)  4.76 us
  transfers between devices with their start and end apart: 23, of which 9 were waited for; matrix products, arithmetic and copies ran while one was open for 8% of the time, Pallas kernels for 0%

profile of v4, /device:TPU:1, one launch (start us, length us, event | category | flops | bytes accessed | tf_op | source)
XLA Modules:
  0.0 225.1 jit_solution(537962789974507206)
XLA Ops:
  2.2 13.1 %all-to-all-start.1 = ((bf16[8,16,768]{2,1,0:T(8,128)(2,1)}), bf16[8,16,768]{2,1,0:T(8,128)(2,1)S(1)}, u32[]{:S(2)}, u32[]{:S(2)}) async-start(bf16[8,16,768]{2,1,0:T(8,128)(2,1)} %broadcast_in_dim.27), calls=%async_computation.1 | async-start | bytes 393216 | tf_op jit(solution)/shard_map/all_to_all | solution.py:23
  15.2 2.9 %collective-permute-start = (bf16[768,256]{1,0:T(8,128)(2,1)}, bf16[768,256]{1,0:T(8,128)(2,1)S(1)}, u32[]{:S(2)}, u32[]{:S(2)}) collective-permute-start(bf16[768,256]{1,0:T(8,128)(2,1)} %param.9), channel_id=1, source_target_pairs={{0,8},{8,0},{1,9},{9,1},{2,10},{10,2},{3,11},{11,3},{4,12},{12,4},... | collective-permute-start | bytes 1179656 | tf_op jit(solution)/shard_map/ppermute | solution.py:36
  18.1 4.6 %collective-permute-start.1 = (bf16[256,768]{1,0:T(8,128)(2,1)}, bf16[256,768]{1,0:T(8,128)(2,1)S(1)}, u32[]{:S(2)}, u32[]{:S(2)}) collective-permute-start(bf16[256,768]{1,0:T(8,128)(2,1)} %param.10), channel_id=1, source_target_pairs={{0,3},{1,0},{2,1},{3,2},{4,7},{5,4},{6,5},{7,6},{8,11},{9,8},{10,9... | collective-permute-start | bytes 1179656 | tf_op jit(solution)/shard_map/ppermute | solution.py:36
  24.7 6.8 %collective-permute-done.1 = bf16[256,768]{1,0:T(8,128)(2,1)S(1)} collective-permute-done((bf16[256,768]{1,0:T(8,128)(2,1)}, bf16[256,768]{1,0:T(8,128)(2,1)S(1)}, u32[]{:S(2)}, u32[]{:S(2)}) %collective-permute-start.1) | collective-permute-done | bytes 393248 | tf_op jit(solution)/shard_map/ppermute | solution.py:36
  31.5 4.9 %collective-permute-done.2 = bf16[256,768]{1,0:T(8,128)(2,1)S(1)} collective-permute-done((bf16[256,768]{1,0:T(8,128)(2,1)}, bf16[256,768]{1,0:T(8,128)(2,1)S(1)}, u32[]{:S(2)}, u32[]{:S(2)}) %collective-permute-start.2) | collective-permute-done | bytes 393248 | tf_op jit(solution)/shard_map/ppermute | solution.py:36
  37.4 4.0 %all-to-all-start.2 = ((bf16[4,8,16,768]{3,2,1,0:T(8,128)(2,1)}), bf16[4,8,16,768]{3,2,1,0:T(8,128)(2,1)S(1)}, u32[]{:S(2)}, u32[]{:S(2)}) async-start(bf16[4,8,16,768]{3,2,1,0:T(8,128)(2,1)} %broadcast_in_dim.28), calls=%async_computation.2 | async-start | bytes 1572864 | tf_op jit(solution)/shard_map/all_to_all | solution.py:23
  44.4 9.6 %collective-permute-done.3 = bf16[256,768]{1,0:T(8,128)(2,1)S(1)} collective-permute-done((bf16[256,768]{1,0:T(8,128)(2,1)S(1)}, bf16[256,768]{1,0:T(8,128)(2,1)S(1)}, u32[]{:S(2)}, u32[]{:S(2)}) %collective-permute-start.3) | collective-permute-done | bytes 393248 | tf_op jit(solution)/shard_map/ppermute | solution.py:36
  54.0 3.3 %fusion.3 = bf16[512,512]{1,0:T(8,128)(2,1)} fusion(bf16[768,512]{1,0:T(8,128)(2,1)S(1)} %pad_maximum_fusion.1, bf16[512,512]{1,0:T(8,128)(2,1)} %constant.75.clone, bf16[512,768]{1,0:T(8,128)(2,1)S(1)} %bitcast.41), kind=kOutput, calls=%fused_computation.9 | convolution fusion | flops 806223872 | bytes 2621440 | tf_op jit(solution)/shard_map/dot_general | solution.py:57
  57.3 3.5 %all-to-all-start.3 = ((bf16[4,128,512]{2,1,0:T(8,128)(2,1)}), bf16[4,128,512]{2,1,0:T(8,128)(2,1)S(1)}, u32[]{:S(2)}, u32[]{:S(2)}) async-start(bf16[4,128,512]{2,1,0:T(8,128)(2,1)} %bitcast.6), calls=%async_computation.3 | async-start | bytes 1048576 | tf_op jit(solution)/shard_map/all_to_all | solution.py:23
  63.2 4.5 %all-to-all-done.3 = bf16[4,128,512]{2,1,0:T(8,128)(2,1)S(1)} async-done(((bf16[4,128,512]{2,1,0:T(8,128)(2,1)}), bf16[4,128,512]{2,1,0:T(8,128)(2,1)S(1)}, u32[]{:S(2)}, u32[]{:S(2)}) %all-to-all-start.3) | async-done | bytes 524320 | tf_op jit(solution)/shard_map/all_to_all | solution.py:23
  67.8 5.3 %collective-permute-start.5 = (bf16[256,3072]{1,0:T(8,128)(2,1)S(1)}, bf16[256,3072]{1,0:T(8,128)(2,1)S(1)}, u32[]{:S(2)}, u32[]{:S(2)}) collective-permute-start(bf16[256,3072]{1,0:T(8,128)(2,1)S(1)} %pad_maximum_fusion), channel_id=1, source_target_pairs={{0,8},{8,0},{1,9},{9,1},{2,10},{10,2},{3,11},{11,3},{4,12},{12,4},... | collective-permute-start | bytes 4718600 | tf_op jit(solution)/shard_map/ppermute | solution.py:36
  74.6 3.3 %all-to-all-start = ((bf16[4,2,4,768]{3,2,1,0:T(4,128)(2,1)}), bf16[4,2,4,768]{3,2,1,0:T(4,128)(2,1)S(1)}, u32[]{:S(2)}, u32[]{:S(2)}) async-start(bf16[4,2,4,768]{3,2,1,0:T(4,128)(2,1)} %pad_maximum_fusion.6), calls=%async_computation | async-start | bytes 98304 | tf_op jit(solution)/shard_map/all_to_all | solution.py:23
  77.9 4.3 %all-to-all-done = bf16[4,2,4,768]{3,2,1,0:T(4,128)(2,1)S(1)} async-done(((bf16[4,2,4,768]{3,2,1,0:T(4,128)(2,1)}), bf16[4,2,4,768]{3,2,1,0:T(4,128)(2,1)S(1)}, u32[]{:S(2)}, u32[]{:S(2)}) %all-to-all-start) | async-done | bytes 49184 | tf_op jit(solution)/shard_map/all_to_all | solution.py:23
  82.9 7.9 %collective-permute-start.4 = (bf16[128,512]{1,0:T(8,128)(2,1)S(1)}, bf16[128,512]{1,0:T(8,128)(2,1)S(1)}, u32[]{:S(2)}, u32[]{:S(2)}) collective-permute-start(bf16[128,512]{1,0:T(8,128)(2,1)S(1)} %convert_element_type.96), channel_id=1, source_target_pairs={{0,4},{4,0},{1,5},{5,1},{2,6},{6,2},{3,7},{7,3},{8,12},{12,8},{9,1... | collective-permute-start | bytes 393224 | tf_op jit(solution)/shard_map/ppermute | solution.py:36
  90.9 2.8 %convolution_convert_fusion.1 = bf16[768,512]{1,0:T(8,128)(2,1)} fusion(bf16[512,768]{1,0:T(8,128)(2,1)} %bitcast.42, bf16[512,512]{1,0:T(8,128)(2,1)} %constant.75.clone), kind=kOutput, calls=%fused_computation.6 | convolution fusion | flops 403046400 | bytes 2097152 | tf_op jit(solution)/shard_map/td,pt->dp/dot_general | solution.py:93
  93.7 4.0 %collective-permute-done.4 = bf16[128,512]{1,0:T(8,128)(2,1)S(1)} collective-permute-done((bf16[128,512]{1,0:T(8,128)(2,1)S(1)}, bf16[128,512]{1,0:T(8,128)(2,1)S(1)}, u32[]{:S(2)}, u32[]{:S(2)}) %collective-permute-start.4) | collective-permute-done | bytes 131104 | tf_op jit(solution)/shard_map/ppermute | solution.py:36
  100.0 4.2 %all-to-all-start.4 = ((bf16[4,32,3072]{2,1,0:T(8,128)(2,1)}), bf16[4,32,3072]{2,1,0:T(8,128)(2,1)}, u32[]{:S(2)}, u32[]{:S(2)}) async-start(bf16[4,32,3072]{2,1,0:T(8,128)(2,1)} %bitcast.38), calls=%async_computation.4 | async-start | bytes 1572864 | tf_op jit(solution)/shard_map/all_to_all | solution.py:23
  106.4 7.5 %all-to-all-done.4 = bf16[4,32,3072]{2,1,0:T(8,128)(2,1)} async-done(((bf16[4,32,3072]{2,1,0:T(8,128)(2,1)}), bf16[4,32,3072]{2,1,0:T(8,128)(2,1)}, u32[]{:S(2)}, u32[]{:S(2)}) %all-to-all-start.4) | async-done | bytes 786464 | tf_op jit(solution)/shard_map/all_to_all | solution.py:23
  115.9 9.1 %all-to-all-start.5 = ((bf16[4,8,3072]{2,1,0:T(8,128)(2,1)}), bf16[4,8,3072]{2,1,0:T(8,128)(2,1)}, u32[]{:S(2)}, u32[]{:S(2)}) async-start(bf16[4,8,3072]{2,1,0:T(8,128)(2,1)} %bitcast.43), calls=%async_computation.5 | async-start | bytes 393216 | tf_op jit(solution)/shard_map/all_to_all | solution.py:23
  125.0 3.0 %collective-permute-start.7 = (bf16[128,512]{1,0:T(8,128)(2,1)S(1)}, bf16[128,512]{1,0:T(8,128)(2,1)}, u32[]{:S(2)}, u32[]{:S(2)}) collective-permute-start(bf16[128,512]{1,0:T(8,128)(2,1)S(1)} %multiply_convert_fusion), channel_id=1, source_target_pairs={{0,2},{1,3},{2,0},{3,1},{4,6},{5,7},{6,4},{7,5},{8,10},{9,11},{10,... | collective-permute-start | bytes 393224 | tf_op jit(solution)/shard_map/ppermute | solution.py:36
  128.0 3.4 %collective-permute-start.9 = (bf16[128,512]{1,0:T(8,128)(2,1)S(1)}, bf16[128,512]{1,0:T(8,128)(2,1)}, u32[]{:S(2)}, u32[]{:S(2)}) collective-permute-start(bf16[128,512]{1,0:T(8,128)(2,1)S(1)} %multiply_convert_fusion), channel_id=1, source_target_pairs={{0,3},{1,0},{2,1},{3,2},{4,7},{5,4},{6,5},{7,6},{8,11},{9,8},{10,9... | collective-permute-start | bytes 393224 | tf_op jit(solution)/shard_map/ppermute | solution.py:36
  133.4 13.1 %collective-permute-start.8 = (bf16[8,3072]{1,0:T(8,128)(2,1)S(1)}, bf16[8,3072]{1,0:T(8,128)(2,1)S(1)}, u32[]{:S(2)}, u32[]{:S(2)}) collective-permute-start(bf16[8,3072]{1,0:T(8,128)(2,1)S(1)} %fusion.22), channel_id=1, source_target_pairs={{0,256},{256,0},{1,257},{257,1},{2,258},{258,2},{3,259},{259,3},{4... | collective-permute-start | bytes 147464 | tf_op jit(solution)/shard_map/ppermute | solution.py:36
  148.9 10.8 %all_to_all.45 = bf16[4,8,3072]{2,1,0:T(8,128)(2,1)S(1)} all-to-all(bf16[4,8,3072]{2,1,0:T(8,128)(2,1)S(1)} %broadcast_in_dim.31), channel_id=1, replica_groups=mesh['zq'=2,'za'=4,'x'=4,'c'=2,'zh'=2,'y'=4] {'za'}, dimensions={0} | all-to-all | bytes 393216 | tf_op jit(solution)/shard_map/all_to_all | solution.py:23
  159.8 10.7 %all_to_all.46 = bf16[4,4,8,3072]{3,2,1,0:T(8,128)(2,1)S(1)} all-to-all(bf16[4,4,8,3072]{3,2,1,0:T(8,128)(2,1)S(1)} %broadcast_in_dim.32), channel_id=1, replica_groups=mesh['zq'=2,'za'=4,'x'=4,'c'=2,'zh'=2,'y'=4] {'x'}, dimensions={0} | all-to-all | bytes 1572864 | tf_op jit(solution)/shard_map/all_to_all | solution.py:23
  174.3 3.5 %collective-permute-start.12 = (bf16[128,768]{1,0:T(8,128)(2,1)S(1)}, bf16[128,768]{1,0:T(8,128)(2,1)S(1)}, u32[]{:S(2)}, u32[]{:S(2)}) collective-permute-start(bf16[128,768]{1,0:T(8,128)(2,1)S(1)} %get-tuple-element.66), channel_id=1, source_target_pairs={{0,2},{1,3},{2,0},{3,1},{4,6},{5,7},{6,4},{7,5},{8,10},{9,11},{10,... | collective-permute-start | bytes 589832 | tf_op jit(solution)/shard_map/ppermute | solution.py:36
  177.8 3.0 %collective-permute-start.13 = (bf16[128,768]{1,0:T(8,128)(2,1)S(1)}, bf16[128,768]{1,0:T(8,128)(2,1)}, u32[]{:S(2)}, u32[]{:S(2)}) collective-permute-start(bf16[128,768]{1,0:T(8,128)(2,1)S(1)} %get-tuple-element.65), channel_id=1, source_target_pairs={{0,3},{1,0},{2,1},{3,2},{4,7},{5,4},{6,5},{7,6},{8,11},{9,8},{10,9... | collective-permute-start | bytes 589832 | tf_op jit(solution)/shard_map/ppermute | solution.py:36
  180.8 7.9 %collective-permute-start.10 = (bf16[128,512]{1,0:T(8,128)(2,1)S(1)}, bf16[128,512]{1,0:T(8,128)(2,1)S(1)}, u32[]{:S(2)}, u32[]{:S(2)}) collective-permute-start(bf16[128,512]{1,0:T(8,128)(2,1)S(1)} %convert_element_type.109), channel_id=1, source_target_pairs={{0,4},{4,0},{1,5},{5,1},{2,6},{6,2},{3,7},{7,3},{8,12},{12,8},{9,1... | collective-permute-start | bytes 393224 | tf_op jit(solution)/shard_map/ppermute | solution.py:36
  188.8 6.5 %collective-permute-done.10 = bf16[128,512]{1,0:T(8,128)(2,1)S(1)} collective-permute-done((bf16[128,512]{1,0:T(8,128)(2,1)S(1)}, bf16[128,512]{1,0:T(8,128)(2,1)S(1)}, u32[]{:S(2)}, u32[]{:S(2)}) %collective-permute-start.10) | collective-permute-done | bytes 131104 | tf_op jit(solution)/shard_map/ppermute | solution.py:36
  196.4 3.5 %all-to-all-start.8 = ((bf16[4,128,512]{2,1,0:T(8,128)(2,1)}), bf16[4,128,512]{2,1,0:T(8,128)(2,1)S(1)}, u32[]{:S(2)}, u32[]{:S(2)}) async-start(bf16[4,128,512]{2,1,0:T(8,128)(2,1)} %broadcast_in_dim.33), calls=%async_computation.8 | async-start | bytes 1048576 | tf_op jit(solution)/shard_map/all_to_all | solution.py:23
  203.1 12.6 %collective-permute-start.15 = (bf16[256,768]{1,0:T(8,128)(2,1)}, bf16[256,768]{1,0:T(8,128)(2,1)}, u32[]{:S(2)}, u32[]{:S(2)}) collective-permute-start(bf16[256,768]{1,0:T(8,128)(2,1)} %fusion.6), channel_id=1, source_target_pairs={{0,8},{8,0},{1,9},{9,1},{2,10},{10,2},{3,11},{11,3},{4,12},{12,4},... | collective-permute-start | bytes 1179656 | tf_op jit(solution)/shard_map/ppermute | solution.py:36
  216.2 4.8 %collective-permute-start.14 = (bf16[768,256]{1,0:T(8,128)(2,1)S(1)}, bf16[768,256]{1,0:T(8,128)(2,1)S(1)}, u32[]{:S(2)}, u32[]{:S(2)}) collective-permute-start(bf16[768,256]{1,0:T(8,128)(2,1)S(1)} %fusion.5), channel_id=1, source_target_pairs={{0,8},{8,0},{1,9},{9,1},{2,10},{10,2},{3,11},{11,3},{4,12},{12,4},... | collective-permute-start | bytes 1179656 | tf_op jit(solution)/shard_map/ppermute | solution.py:36
  221.0 2.6 %multiply_add_fusion = (f32[256,768]{1,0:T(8,128)}, bf16[256,768]{1,0:T(8,128)(2,1)}) fusion(bf16[256,768]{1,0:T(8,128)(2,1)S(1)} %copy-done.8, f32[256,768]{1,0:T(8,128)S(1)} %copy-done.13, bf16[256,768]{1,0:T(8,128)(2,1)} %collective-permute-done.15, bf16[128,768]{1,0:T(8,128)(2,1)} %collective-permute-done.13, bf16[128,768]{1,0:T(8,128)(2,1)S(1)} %copy-done.17, ...), kind=kOutput, calls=%fused_computation.20 | convolution fusion | flops 206438400 | bytes 3801088 | tf_op jit(solution)/shard_map/tf,td->fd/dot_general | solution.py:139
  (89 shorter events, 32.7 us)
Async XLA Ops:
  0.6 42.7 %copy-start = (bf16[768,256]{1,0:T(8,128)(2,1)S(1)}, bf16[768,256]{1,0:T(8,128)(2,1)}, u32[]{:S(2)}) copy-start(bf16[768,256]{1,0:T(8,128)(2,1)} %param.9) | copy-start | bytes 1179652
  0.6 40.7 %copy-start.7 = (bf16[256,768]{1,0:T(8,128)(2,1)S(1)}, bf16[256,768]{1,0:T(8,128)(2,1)}, u32[]{:S(2)}) copy-start(bf16[256,768]{1,0:T(8,128)(2,1)} %param.10) | copy-start | bytes 1179652
  2.2 34.3 %all-to-all-start.1 = ((bf16[8,16,768]{2,1,0:T(8,128)(2,1)}), bf16[8,16,768]{2,1,0:T(8,128)(2,1)S(1)}, u32[]{:S(2)}, u32[]{:S(2)}) async-start(bf16[8,16,768]{2,1,0:T(8,128)(2,1)} %broadcast_in_dim.27), calls=%async_computation.1 | async-start | bytes 393216 | tf_op jit(solution)/shard_map/all_to_all | solution.py:23
  15.2 9.4 %collective-permute-start = (bf16[768,256]{1,0:T(8,128)(2,1)}, bf16[768,256]{1,0:T(8,128)(2,1)S(1)}, u32[]{:S(2)}, u32[]{:S(2)}) collective-permute-start(bf16[768,256]{1,0:T(8,128)(2,1)} %param.9), channel_id=1, source_target_pairs={{0,8},{8,0},{1,9},{9,1},{2,10},{10,2},{3,11},{11,3},{4,12},{12,4},... | collective-permute-start | bytes 1179656 | tf_op jit(solution)/shard_map/ppermute | solution.py:36
  18.1 13.4 %collective-permute-start.1 = (bf16[256,768]{1,0:T(8,128)(2,1)}, bf16[256,768]{1,0:T(8,128)(2,1)S(1)}, u32[]{:S(2)}, u32[]{:S(2)}) collective-permute-start(bf16[256,768]{1,0:T(8,128)(2,1)} %param.10), channel_id=1, source_target_pairs={{0,3},{1,0},{2,1},{3,2},{4,7},{5,4},{6,5},{7,6},{8,11},{9,8},{10,9... | collective-permute-start | bytes 1179656 | tf_op jit(solution)/shard_map/ppermute | solution.py:36
  22.7 13.7 %collective-permute-start.2 = (bf16[256,768]{1,0:T(8,128)(2,1)}, bf16[256,768]{1,0:T(8,128)(2,1)S(1)}, u32[]{:S(2)}, u32[]{:S(2)}) collective-permute-start(bf16[256,768]{1,0:T(8,128)(2,1)} %param.10), channel_id=1, source_target_pairs={{0,1},{1,2},{2,3},{3,0},{4,5},{5,6},{6,7},{7,4},{8,9},{9,10},{10,1... | collective-permute-start | bytes 1179656 | tf_op jit(solution)/shard_map/ppermute | solution.py:36
  24.7 12.7 %copy-start.10 = (bf16[768,256]{1,0:T(8,128)(2,1)}, bf16[768,256]{1,0:T(8,128)(2,1)S(1)}, u32[]{:S(2)}) copy-start(bf16[768,256]{1,0:T(8,128)(2,1)S(1)} %collective-permute-done) | copy-start | bytes 1179652
  37.4 16.7 %all-to-all-start.2 = ((bf16[4,8,16,768]{3,2,1,0:T(8,128)(2,1)}), bf16[4,8,16,768]{3,2,1,0:T(8,128)(2,1)S(1)}, u32[]{:S(2)}, u32[]{:S(2)}) async-start(bf16[4,8,16,768]{3,2,1,0:T(8,128)(2,1)} %broadcast_in_dim.28), calls=%async_computation.2 | async-start | bytes 1572864 | tf_op jit(solution)/shard_map/all_to_all | solution.py:23
  41.4 12.6 %collective-permute-start.3 = (bf16[256,768]{1,0:T(8,128)(2,1)S(1)}, bf16[256,768]{1,0:T(8,128)(2,1)S(1)}, u32[]{:S(2)}, u32[]{:S(2)}) collective-permute-start(bf16[256,768]{1,0:T(8,128)(2,1)S(1)} %copy-done.7), channel_id=1, source_target_pairs={{0,2},{1,3},{2,0},{3,1},{4,6},{5,7},{6,4},{7,5},{8,10},{9,11},{10,... | collective-permute-start | bytes 1179656 | tf_op jit(solution)/shard_map/ppermute | solution.py:36
  57.3 10.4 %all-to-all-start.3 = ((bf16[4,128,512]{2,1,0:T(8,128)(2,1)}), bf16[4,128,512]{2,1,0:T(8,128)(2,1)S(1)}, u32[]{:S(2)}, u32[]{:S(2)}) async-start(bf16[4,128,512]{2,1,0:T(8,128)(2,1)} %bitcast.6), calls=%async_computation.3 | async-start | bytes 1048576 | tf_op jit(solution)/shard_map/all_to_all | solution.py:23
  67.8 30.9 %collective-permute-start.5 = (bf16[256,3072]{1,0:T(8,128)(2,1)S(1)}, bf16[256,3072]{1,0:T(8,128)(2,1)S(1)}, u32[]{:S(2)}, u32[]{:S(2)}) collective-permute-start(bf16[256,3072]{1,0:T(8,128)(2,1)S(1)} %pad_maximum_fusion), channel_id=1, source_target_pairs={{0,8},{8,0},{1,9},{9,1},{2,10},{10,2},{3,11},{11,3},{4,12},{12,4},... | collective-permute-start | bytes 4718600 | tf_op jit(solution)/shard_map/ppermute | solution.py:36
  74.6 7.6 %all-to-all-start = ((bf16[4,2,4,768]{3,2,1,0:T(4,128)(2,1)}), bf16[4,2,4,768]{3,2,1,0:T(4,128)(2,1)S(1)}, u32[]{:S(2)}, u32[]{:S(2)}) async-start(bf16[4,2,4,768]{3,2,1,0:T(4,128)(2,1)} %pad_maximum_fusion.6), calls=%async_computation | async-start | bytes 98304 | tf_op jit(solution)/shard_map/all_to_all | solution.py:23
  82.9 14.7 %collective-permute-start.4 = (bf16[128,512]{1,0:T(8,128)(2,1)S(1)}, bf16[128,512]{1,0:T(8,128)(2,1)S(1)}, u32[]{:S(2)}, u32[]{:S(2)}) collective-permute-start(bf16[128,512]{1,0:T(8,128)(2,1)S(1)} %convert_element_type.96), channel_id=1, source_target_pairs={{0,4},{4,0},{1,5},{5,1},{2,6},{6,2},{3,7},{7,3},{8,12},{12,8},{9,1... | collective-permute-start | bytes 393224 | tf_op jit(solution)/shard_map/ppermute | solution.py:36
  100.0 13.9 %all-to-all-start.4 = ((bf16[4,32,3072]{2,1,0:T(8,128)(2,1)}), bf16[4,32,3072]{2,1,0:T(8,128)(2,1)}, u32[]{:S(2)}, u32[]{:S(2)}) async-start(bf16[4,32,3072]{2,1,0:T(8,128)(2,1)} %bitcast.38), calls=%async_computation.4 | async-start | bytes 1572864 | tf_op jit(solution)/shard_map/all_to_all | solution.py:23
  104.2 11.6 %collective-permute-start.6 = (bf16[128,512]{1,0:T(8,128)(2,1)S(1)}, bf16[128,512]{1,0:T(8,128)(2,1)}, u32[]{:S(2)}, u32[]{:S(2)}) collective-permute-start(bf16[128,512]{1,0:T(8,128)(2,1)S(1)} %multiply_convert_fusion), channel_id=1, source_target_pairs={{0,1},{1,2},{2,3},{3,0},{4,5},{5,6},{6,7},{7,4},{8,9},{9,10},{10,1... | collective-permute-start | bytes 393224 | tf_op jit(solution)/shard_map/ppermute | solution.py:36
  115.9 15.6 %all-to-all-start.5 = ((bf16[4,8,3072]{2,1,0:T(8,128)(2,1)}), bf16[4,8,3072]{2,1,0:T(8,128)(2,1)}, u32[]{:S(2)}, u32[]{:S(2)}) async-start(bf16[4,8,3072]{2,1,0:T(8,128)(2,1)} %bitcast.43), calls=%async_computation.5 | async-start | bytes 393216 | tf_op jit(solution)/shard_map/all_to_all | solution.py:23
  125.0 7.5 %collective-permute-start.7 = (bf16[128,512]{1,0:T(8,128)(2,1)S(1)}, bf16[128,512]{1,0:T(8,128)(2,1)}, u32[]{:S(2)}, u32[]{:S(2)}) collective-permute-start(bf16[128,512]{1,0:T(8,128)(2,1)S(1)} %multiply_convert_fusion), channel_id=1, source_target_pairs={{0,2},{1,3},{2,0},{3,1},{4,6},{5,7},{6,4},{7,5},{8,10},{9,11},{10,... | collective-permute-start | bytes 393224 | tf_op jit(solution)/shard_map/ppermute | solution.py:36
  128.0 18.5 %collective-permute-start.9 = (bf16[128,512]{1,0:T(8,128)(2,1)S(1)}, bf16[128,512]{1,0:T(8,128)(2,1)}, u32[]{:S(2)}, u32[]{:S(2)}) collective-permute-start(bf16[128,512]{1,0:T(8,128)(2,1)S(1)} %multiply_convert_fusion), channel_id=1, source_target_pairs={{0,3},{1,0},{2,1},{3,2},{4,7},{5,4},{6,5},{7,6},{8,11},{9,8},{10,9... | collective-permute-start | bytes 393224 | tf_op jit(solution)/shard_map/ppermute | solution.py:36
  133.4 14.5 %collective-permute-start.8 = (bf16[8,3072]{1,0:T(8,128)(2,1)S(1)}, bf16[8,3072]{1,0:T(8,128)(2,1)S(1)}, u32[]{:S(2)}, u32[]{:S(2)}) collective-permute-start(bf16[8,3072]{1,0:T(8,128)(2,1)S(1)} %fusion.22), channel_id=1, source_target_pairs={{0,256},{256,0},{1,257},{257,1},{2,258},{258,2},{3,259},{259,3},{4... | collective-permute-start | bytes 147464 | tf_op jit(solution)/shard_map/ppermute | solution.py:36
  171.9 23.5 %copy-start.6 = (bf16[128,512]{1,0:T(8,128)(2,1)S(1)}, bf16[128,512]{1,0:T(8,128)(2,1)}, u32[]{:S(2)}) copy-start(bf16[128,512]{1,0:T(8,128)(2,1)} %copy-done.5) | copy-start | bytes 393220
  172.0 23.3 %collective-permute-start.11 = (bf16[128,768]{1,0:T(8,128)(2,1)S(1)}, bf16[128,768]{1,0:T(8,128)(2,1)S(1)}, u32[]{:S(2)}, u32[]{:S(2)}) collective-permute-start(bf16[128,768]{1,0:T(8,128)(2,1)S(1)} %get-tuple-element.67), channel_id=1, source_target_pairs={{0,1},{1,2},{2,3},{3,0},{4,5},{5,6},{6,7},{7,4},{8,9},{9,10},{10,1... | collective-permute-start | bytes 589832 | tf_op jit(solution)/shard_map/ppermute | solution.py:36
  174.3 21.1 %collective-permute-start.12 = (bf16[128,768]{1,0:T(8,128)(2,1)S(1)}, bf16[128,768]{1,0:T(8,128)(2,1)S(1)}, u32[]{:S(2)}, u32[]{:S(2)}) collective-permute-start(bf16[128,768]{1,0:T(8,128)(2,1)S(1)} %get-tuple-element.66), channel_id=1, source_target_pairs={{0,2},{1,3},{2,0},{3,1},{4,6},{5,7},{6,4},{7,5},{8,10},{9,11},{10,... | collective-permute-start | bytes 589832 | tf_op jit(solution)/shard_map/ppermute | solution.py:36
  177.8 17.5 %collective-permute-start.13 = (bf16[128,768]{1,0:T(8,128)(2,1)S(1)}, bf16[128,768]{1,0:T(8,128)(2,1)}, u32[]{:S(2)}, u32[]{:S(2)}) collective-permute-start(bf16[128,768]{1,0:T(8,128)(2,1)S(1)} %get-tuple-element.65), channel_id=1, source_target_pairs={{0,3},{1,0},{2,1},{3,2},{4,7},{5,4},{6,5},{7,6},{8,11},{9,8},{10,9... | collective-permute-start | bytes 589832 | tf_op jit(solution)/shard_map/ppermute | solution.py:36
  180.8 14.5 %collective-permute-start.10 = (bf16[128,512]{1,0:T(8,128)(2,1)S(1)}, bf16[128,512]{1,0:T(8,128)(2,1)S(1)}, u32[]{:S(2)}, u32[]{:S(2)}) collective-permute-start(bf16[128,512]{1,0:T(8,128)(2,1)S(1)} %convert_element_type.109), channel_id=1, source_target_pairs={{0,4},{4,0},{1,5},{5,1},{2,6},{6,2},{3,7},{7,3},{8,12},{12,8},{9,1... | collective-permute-start | bytes 393224 | tf_op jit(solution)/shard_map/ppermute | solution.py:36
  196.4 19.4 %all-to-all-start.8 = ((bf16[4,128,512]{2,1,0:T(8,128)(2,1)}), bf16[4,128,512]{2,1,0:T(8,128)(2,1)S(1)}, u32[]{:S(2)}, u32[]{:S(2)}) async-start(bf16[4,128,512]{2,1,0:T(8,128)(2,1)} %broadcast_in_dim.33), calls=%async_computation.8 | async-start | bytes 1048576 | tf_op jit(solution)/shard_map/all_to_all | solution.py:23
  200.9 14.8 %copy-start.4 = (bf16[768,512]{1,0:T(8,128)(2,1)S(1)}, bf16[768,512]{1,0:T(8,128)(2,1)}, u32[]{:S(2)}) copy-start(bf16[768,512]{1,0:T(8,128)(2,1)} %convolution_convert_fusion.1) | copy-start | bytes 2359300
  203.1 17.9 %copy-start.8 = (bf16[256,768]{1,0:T(8,128)(2,1)S(1)}, bf16[256,768]{1,0:T(8,128)(2,1)}, u32[]{:S(2)}) copy-start(bf16[256,768]{1,0:T(8,128)(2,1)} %param.10) | copy-start | bytes 1179652
  203.1 17.9 %copy-start.13 = (f32[256,768]{1,0:T(8,128)S(1)}, f32[256,768]{1,0:T(8,128)}, u32[]{:S(2)}) copy-start(f32[256,768]{1,0:T(8,128)} %param.12) | copy-start | bytes 2359300
  203.1 17.9 %copy-start.15 = (bf16[128,768]{1,0:T(8,128)(2,1)S(1)}, bf16[128,768]{1,0:T(8,128)(2,1)}, u32[]{:S(2)}) copy-start(bf16[128,768]{1,0:T(8,128)(2,1)} %copy-done.14) | copy-start | bytes 589828
  203.1 17.9 %collective-permute-start.15 = (bf16[256,768]{1,0:T(8,128)(2,1)}, bf16[256,768]{1,0:T(8,128)(2,1)}, u32[]{:S(2)}, u32[]{:S(2)}) collective-permute-start(bf16[256,768]{1,0:T(8,128)(2,1)} %fusion.6), channel_id=1, source_target_pairs={{0,8},{8,0},{1,9},{9,1},{2,10},{10,2},{3,11},{11,3},{4,12},{12,4},... | collective-permute-start | bytes 1179656 | tf_op jit(solution)/shard_map/ppermute | solution.py:36
  216.1 7.5 %copy-start.1 = (bf16[768,256]{1,0:T(8,128)(2,1)S(1)}, bf16[768,256]{1,0:T(8,128)(2,1)}, u32[]{:S(2)}) copy-start(bf16[768,256]{1,0:T(8,128)(2,1)} %param.9) | copy-start | bytes 1179652
  216.2 7.5 %collective-permute-start.14 = (bf16[768,256]{1,0:T(8,128)(2,1)S(1)}, bf16[768,256]{1,0:T(8,128)(2,1)S(1)}, u32[]{:S(2)}, u32[]{:S(2)}) collective-permute-start(bf16[768,256]{1,0:T(8,128)(2,1)S(1)} %fusion.5), channel_id=1, source_target_pairs={{0,8},{8,0},{1,9},{9,1},{2,10},{10,2},{3,11},{11,3},{4,12},{12,4},... | collective-permute-start | bytes 1179656 | tf_op jit(solution)/shard_map/ppermute | solution.py:36
  (9 other events, 45.3 us)

commit v5 on v4

--- a/solution.py
+++ b/solution.py
@@ -4,7 +4,6 @@
 import jax.numpy as jnp
 import numpy as np
 from jax import lax
-from jax.experimental.layout import Layout, with_layout_constraint
 from jax.sharding import Mesh
 from jax.sharding import PartitionSpec as P
 
@@ -72,25 +71,26 @@
     w_both = shift(w_in, "c", 1)
     w_ring = [w_out, shift(w_out, "y", -1), None, shift(w_out, "y", 1)]
     near = gather(inputs, ("za", "zq"))
-    near, w_both, w_ring[1], w_ring[3], w_later = tie(near, w_both, w_ring[1], w_ring[3], w_out)
+    near, w_later = tie(near, w_out)
     w_ring[2] = shift(w_later, "y", 2)
     w_both = jnp.concatenate([w_in, w_both], axis=1)
 
-    arrived = gather(near, "x").reshape(tokens, d)
-    arrived, w_both, *w_ring[1:] = tie(arrived, w_both, *w_ring[1:])
-    at = np.arange(tokens)
-    source = (at % part) // few * rows + at // part * few + at % few
-    order = jnp.asarray(np.eye(tokens, dtype=np.float32)[source], BF)
-    gathered = with_layout_constraint(dot(order, arrived).astype(BF), Layout((0, 1)))
+    at = np.arange(na * nq * rows)
+    source = at % (part // nx) // few * rows + at // (part // nx) * few + at % few
+    order = jnp.asarray(np.eye(at.size, dtype=np.float32)[source], BF)
+    near = dot(order, near.reshape(at.size, d)).astype(BF)
+
+    arrived = gather(near, "x")
+    arrived, w_both, w_ring[1], w_ring[3] = tie(arrived, w_both, w_ring[1], w_ring[3])
     w_ring = jnp.concatenate(w_ring, axis=1)
 
-    partial_pre = dot(gathered, w_both) * in_scale
+    partial_pre = (dot(arrived.reshape(tokens, d), w_both) * in_scale).astype(BF)
+    partial_pre = partial_pre.reshape(nx, ny, part // nx, 2 * f).swapaxes(0, 1)
     sums = scatter(partial_pre.reshape(ny, part, 2 * f), "y")
 
-    sums, w_ring, arrived = tie(sums, w_ring, arrived)
+    sums, w_ring = tie(sums, w_ring)
     other = shift(sums.astype(BF), "zh", 1)
     w_ring_theirs = shift(w_ring, "c", 1)
-    gathered_t = jnp.einsum("td,pt->dp", arrived, order, preferred_element_type=F32).astype(BF)
 
     both = jnp.stack([inputs.reshape(ny, few, d), targets.reshape(ny, few, d)], axis=1)
     both = exchange(both, "y")
@@ -100,22 +100,26 @@
         [lax.dynamic_index_in_dim(own, (y + k) & (ny - 1), keepdims=False) for k in range(ny)],
         axis=1,
     )
-    own, other, gathered_t = tie(own, other, gathered_t)
+    own, other = tie(own, other)
     preact = sums + other.astype(F32)
     hidden = gelu_value(preact).astype(BF)
-    hiddens = [shift(hidden, "y", k) for k in range(1, ny)]
+    hiddens = []
+    for k in range(1, ny):
+        hiddens.append(shift(hidden, "y", k))
 
     partial_out = (dot(hidden[:, :f], w_ring) + dot(hidden[:, f:], w_ring_theirs)) * out_scale
+    partial_out, arrived = tie(partial_out, arrived)
     sums = scatter(partial_out.reshape(nx, part // nx, ny * d), "x")
-    sums, hiddens[0] = tie(sums, hiddens[0])
+    gathered_t = arrived.reshape(nx, ny, part // nx, d).swapaxes(0, 1).reshape(tokens, d).T
+    sums, gathered_t = tie(sums, gathered_t)
     sums = scatter(sums.reshape(na, nq * few, ny * d), "za")
-    sums, hiddens[1] = tie(sums, hiddens[1])
     mine = lax.broadcasted_iota(jnp.int32, (nq * few, 1), 0) // few == lax.axis_index("zq")
     sums = sums + jnp.where(mine, jnp.concatenate([own] * nq, axis=0), 0.0)
     other = shift(sums.astype(BF), "zq", 1)
-    other, hiddens[2] = tie(other, hiddens[2])
     slope = (sums + other.astype(F32)).astype(BF)
-    slopes = gather(gather(slope, "za"), "x").reshape(part, ny * d)
+    slopes = gather(slope, "za")
+    slopes = gather(slopes, "x")
+    slopes = slopes.reshape(part, ny * d)
 
     slope_part = out_scale * jnp.concatenate(
         [
@@ -127,10 +131,10 @@
     slopes, slope_part = tie(slopes, slope_part)
     other = shift(slope_part.astype(BF), "zh", 1)
     their_slopes = [shift(slopes[:, k * d : (k + 1) * d], "y", k) for k in range(1, ny)]
-    other, *their_slopes = tie(other, *their_slopes)
     hidden_slope = slope_part + other.astype(F32)
     pre_slope = (hidden_slope * gelu_slope(preact)).astype(BF)
-    pre_slopes = gather(pre_slope, "y").reshape(tokens, 2 * f)
+    pre_slopes = gather(pre_slope, "y")
+    pre_slopes = pre_slopes.reshape(tokens, 2 * f)
 
     hiddens = jnp.concatenate([hidden, *hiddens], axis=0)
     own_slopes = jnp.concatenate([slopes[:, :d], *their_slopes], axis=0)

time: 227 us -> 225 us (level)
  starting transfers between devices: 121 us -> 102 us
  waiting for transfers between devices: 49.7 us -> 63.5 us
  blocking collectives: 21.6 us -> 31.9 us
  matrix products: 15.6 us -> 9.58 us
  other arithmetic: 10.6 us -> 4.94 us
  local copies, waits for them, and re-layouts: 5.39 us -> 9.91 us
    all_to_all x7, starting transfers between devices: 40.6 us -> 27.9 us  [exchange(): return lax.all_to_all(pieces, axis, split_axis=0, concat_axis=0, tiled=True)]
    all_to_all x2, blocking collectives: 21.6 us -> 31.9 us  [exchange(): return lax.all_to_all(pieces, axis, split_axis=0, concat_axis=0, tiled=True)]
    all_to_all x7, waiting for transfers between devices: 16.4 us -> 25.7 us  [exchange(): return lax.all_to_all(pieces, axis, split_axis=0, concat_axis=0, tiled=True)]
    ppermute x16, starting transfers between devices: 80.5 us -> 74.1 us  [shift(): return lax.ppermute(value, axis, [(i, (i + by) % n) for i in range(n)])]
    ppermute x16, waiting for transfers between devices: 33.4 us -> 37.8 us  [shift(): return lax.ppermute(value, axis, [(i, (i + by) % n) for i in range(n)])]
    dot_general x1 -> x0, matrix products: 2.79 us -> none  [shards(): jnp.einsum('td,pt->dp', arrived, order, preferred_element_type=F32)]
    dot_general x5 -> x6, matrix products: 6.72 us -> 5.23 us  [dot(): return jnp.dot(a, b, preferred_element_type=F32)]
  transfers between devices with their start and end apart: 23 -> 23, of which waited for: 9 -> 10; matrix products, arithmetic and copies ran while one was open for 8% -> 6% of each run, Pallas kernels for 0% -> 0%
where the time goes in v5:
time: 225 us; the launch traced here: 223 us
  starting transfers between devices  102 us (45%)
  waiting for transfers between devices  63.5 us (28%)
  blocking collectives  31.9 us (14%)
  local copies, waits for them, and re-layouts  9.91 us (4%)
  matrix products  9.58 us (4%)
  other arithmetic  4.94 us (2%)
    ppermute x16, starting transfers between devices, shift(): return lax.ppermute(value, axis, [(i, (i + by) % n) for i in range(n)])  74.1 us
    ppermute x16, waiting for transfers between devices, shift(): return lax.ppermute(value, axis, [(i, (i + by) % n) for i in range(n)])  37.8 us
    all_to_all x2, blocking collectives, exchange(): return lax.all_to_all(pieces, axis, split_axis=0, concat_axis=0, tiled=True)  31.9 us
    all_to_all x7, starting transfers between devices, exchange(): return lax.all_to_all(pieces, axis, split_axis=0, concat_axis=0, tiled=True)  27.9 us
    all_to_all x7, waiting for transfers between devices, exchange(): return lax.all_to_all(pieces, axis, split_axis=0, concat_axis=0, tiled=True)  25.7 us
    dot_general x6, matrix products, dot(): return jnp.dot(a, b, preferred_element_type=F32)  5.23 us
  transfers between devices with their start and end apart: 23, of which 10 were waited for; matrix products, arithmetic and copies ran while one was open for 6% of the time, Pallas kernels for 0%

profile of v5, /device:TPU:1, one launch (start us, length us, event | category | flops | bytes accessed | tf_op | source)
XLA Modules:
  0.0 223.0 jit_solution(7242405388191645108)
XLA Ops:
  1.4 23.8 %all_to_all.45 = bf16[8,16,768]{2,1,0:T(8,128)(2,1)S(1)} all-to-all(bf16[8,16,768]{2,1,0:T(8,128)(2,1)S(1)} %broadcast_in_dim.27), channel_id=1, replica_groups=mesh['zq'=2,'za'=4,'x'=4,'c'=2,'zh'=2,'y'=4] {'za','zq'}, dimensions={0} | all-to-all | bytes 393216 | tf_op jit(solution)/shard_map/all_to_all | solution.py:22
  27.3 4.0 %all-to-all-start.1 = ((bf16[4,128,768]{2,1,0:T(8,128)(2,1)}), bf16[4,128,768]{2,1,0:T(8,128)(2,1)S(1)}, u32[]{:S(2)}, u32[]{:S(2)}) async-start(bf16[4,128,768]{2,1,0:T(8,128)(2,1)} %broadcast_in_dim.28), calls=%async_computation.1 | async-start | bytes 1572864 | tf_op jit(solution)/shard_map/all_to_all | solution.py:22
  31.4 6.9 %collective-permute-start = (bf16[768,256]{1,0:T(8,128)(2,1)S(1)}, bf16[768,256]{1,0:T(8,128)(2,1)S(1)}, u32[]{:S(2)}, u32[]{:S(2)}) collective-permute-start(bf16[768,256]{1,0:T(8,128)(2,1)S(1)} %copy-done.5), channel_id=1, source_target_pairs={{0,8},{8,0},{1,9},{9,1},{2,10},{10,2},{3,11},{11,3},{4,12},{12,4},... | collective-permute-start | bytes 1179656 | tf_op jit(solution)/shard_map/ppermute | solution.py:35
  38.3 4.6 %collective-permute-start.1 = (bf16[256,768]{1,0:T(8,128)(2,1)S(1)}, bf16[256,768]{1,0:T(8,128)(2,1)S(1)}, u32[]{:S(2)}, u32[]{:S(2)}) collective-permute-start(bf16[256,768]{1,0:T(8,128)(2,1)S(1)} %copy-done.11), channel_id=1, source_target_pairs={{0,3},{1,0},{2,1},{3,2},{4,7},{5,4},{6,5},{7,6},{8,11},{9,8},{10,9... | collective-permute-start | bytes 1179656 | tf_op jit(solution)/shard_map/ppermute | solution.py:35
  44.9 3.5 %collective-permute-start.3 = (bf16[256,768]{1,0:T(8,128)(2,1)S(1)}, bf16[256,768]{1,0:T(8,128)(2,1)}, u32[]{:S(2)}, u32[]{:S(2)}) collective-permute-start(bf16[256,768]{1,0:T(8,128)(2,1)S(1)} %copy-done.11), channel_id=1, source_target_pairs={{0,2},{1,3},{2,0},{3,1},{4,6},{5,7},{6,4},{7,5},{8,10},{9,11},{10,... | collective-permute-start | bytes 1179656 | tf_op jit(solution)/shard_map/ppermute | solution.py:35
  48.5 11.2 %collective-permute-done.1 = bf16[256,768]{1,0:T(8,128)(2,1)S(1)} collective-permute-done((bf16[256,768]{1,0:T(8,128)(2,1)S(1)}, bf16[256,768]{1,0:T(8,128)(2,1)S(1)}, u32[]{:S(2)}, u32[]{:S(2)}) %collective-permute-start.1) | collective-permute-done | bytes 393248 | tf_op jit(solution)/shard_map/ppermute | solution.py:35
  59.7 5.2 %collective-permute-done.2 = bf16[256,768]{1,0:T(8,128)(2,1)S(1)} collective-permute-done((bf16[256,768]{1,0:T(8,128)(2,1)S(1)}, bf16[256,768]{1,0:T(8,128)(2,1)S(1)}, u32[]{:S(2)}, u32[]{:S(2)}) %collective-permute-start.2) | collective-permute-done | bytes 393248 | tf_op jit(solution)/shard_map/ppermute | solution.py:35
  66.3 3.5 %all-to-all-start.2 = ((bf16[4,128,512]{2,1,0:T(8,128)(2,1)}), bf16[4,128,512]{2,1,0:T(8,128)(2,1)S(1)}, u32[]{:S(2)}, u32[]{:S(2)}) async-start(bf16[4,128,512]{2,1,0:T(8,128)(2,1)} %bitcast.5), calls=%async_computation.2 | async-start | bytes 1048576 | tf_op jit(solution)/shard_map/all_to_all | solution.py:22
  71.0 6.9 %all-to-all-done.2 = bf16[4,128,512]{2,1,0:T(8,128)(2,1)S(1)} async-done(((bf16[4,128,512]{2,1,0:T(8,128)(2,1)}), bf16[4,128,512]{2,1,0:T(8,128)(2,1)S(1)}, u32[]{:S(2)}, u32[]{:S(2)}) %all-to-all-start.2) | async-done | bytes 524320 | tf_op jit(solution)/shard_map/all_to_all | solution.py:22
  77.9 4.2 %collective-permute-start.5 = (bf16[256,3072]{1,0:T(8,128)(2,1)S(1)}, bf16[256,3072]{1,0:T(8,128)(2,1)S(1)}, u32[]{:S(2)}, u32[]{:S(2)}) collective-permute-start(bf16[256,3072]{1,0:T(8,128)(2,1)S(1)} %pad_maximum_fusion), channel_id=1, source_target_pairs={{0,8},{8,0},{1,9},{9,1},{2,10},{10,2},{3,11},{11,3},{4,12},{12,4},... | collective-permute-start | bytes 4718600 | tf_op jit(solution)/shard_map/ppermute | solution.py:35
  84.3 3.3 %all-to-all-start.3 = ((bf16[4,2,4,768]{3,2,1,0:T(4,128)(2,1)}), bf16[4,2,4,768]{3,2,1,0:T(4,128)(2,1)S(1)}, u32[]{:S(2)}, u32[]{:S(2)}) async-start(bf16[4,2,4,768]{3,2,1,0:T(4,128)(2,1)} %pad_maximum_fusion.6), calls=%async_computation.3 | async-start | bytes 98304 | tf_op jit(solution)/shard_map/all_to_all | solution.py:22
  87.6 4.3 %all-to-all-done.3 = bf16[4,2,4,768]{3,2,1,0:T(4,128)(2,1)S(1)} async-done(((bf16[4,2,4,768]{3,2,1,0:T(4,128)(2,1)}), bf16[4,2,4,768]{3,2,1,0:T(4,128)(2,1)S(1)}, u32[]{:S(2)}, u32[]{:S(2)}) %all-to-all-start.3) | async-done | bytes 49184 | tf_op jit(solution)/shard_map/all_to_all | solution.py:22
  92.1 7.9 %collective-permute-start.4 = (bf16[128,512]{1,0:T(8,128)(2,1)S(1)}, bf16[128,512]{1,0:T(8,128)(2,1)S(1)}, u32[]{:S(2)}, u32[]{:S(2)}) collective-permute-start(bf16[128,512]{1,0:T(8,128)(2,1)S(1)} %convert_element_type.89), channel_id=1, source_target_pairs={{0,4},{4,0},{1,5},{5,1},{2,6},{6,2},{3,7},{7,3},{8,12},{12,8},{9,1... | collective-permute-start | bytes 393224 | tf_op jit(solution)/shard_map/ppermute | solution.py:35
  100.6 13.1 %collective-permute-done.4 = bf16[128,512]{1,0:T(8,128)(2,1)S(1)} collective-permute-done((bf16[128,512]{1,0:T(8,128)(2,1)S(1)}, bf16[128,512]{1,0:T(8,128)(2,1)S(1)}, u32[]{:S(2)}, u32[]{:S(2)}) %collective-permute-start.4) | collective-permute-done | bytes 131104 | tf_op jit(solution)/shard_map/ppermute | solution.py:35
  116.3 4.7 %all-to-all-start.4 = ((bf16[4,32,3072]{2,1,0:T(8,128)(2,1)}), bf16[4,32,3072]{2,1,0:T(8,128)(2,1)S(1)}, u32[]{:S(2)}, u32[]{:S(2)}) async-start(bf16[4,32,3072]{2,1,0:T(8,128)(2,1)} %bitcast.47), calls=%async_computation.4 | async-start | bytes 1572864 | tf_op jit(solution)/shard_map/all_to_all | solution.py:22
  121.9 8.9 %all-to-all-done.4 = bf16[4,32,3072]{2,1,0:T(8,128)(2,1)S(1)} async-done(((bf16[4,32,3072]{2,1,0:T(8,128)(2,1)}), bf16[4,32,3072]{2,1,0:T(8,128)(2,1)S(1)}, u32[]{:S(2)}, u32[]{:S(2)}) %all-to-all-start.4) | async-done | bytes 786464 | tf_op jit(solution)/shard_map/all_to_all | solution.py:22
  131.6 5.4 %all-to-all-start.5 = ((bf16[4,8,3072]{2,1,0:T(8,128)(2,1)}), bf16[4,8,3072]{2,1,0:T(8,128)(2,1)S(1)}, u32[]{:S(2)}, u32[]{:S(2)}) async-start(bf16[4,8,3072]{2,1,0:T(8,128)(2,1)} %bitcast.27), calls=%async_computation.5 | async-start | bytes 393216 | tf_op jit(solution)/shard_map/all_to_all | solution.py:22
  136.9 5.1 %all-to-all-done.5 = bf16[4,8,3072]{2,1,0:T(8,128)(2,1)S(1)} async-done(((bf16[4,8,3072]{2,1,0:T(8,128)(2,1)}), bf16[4,8,3072]{2,1,0:T(8,128)(2,1)S(1)}, u32[]{:S(2)}, u32[]{:S(2)}) %all-to-all-start.5) | async-done | bytes 196640 | tf_op jit(solution)/shard_map/all_to_all | solution.py:22
  144.1 7.9 %collective-permute-done.6 = bf16[8,3072]{1,0:T(8,128)(2,1)S(1)} collective-permute-done((bf16[8,3072]{1,0:T(8,128)(2,1)S(1)}, bf16[8,3072]{1,0:T(8,128)(2,1)S(1)}, u32[]{:S(2)}, u32[]{:S(2)}) %collective-permute-start.6) | collective-permute-done | bytes 49184 | tf_op jit(solution)/shard_map/ppermute | solution.py:35
  152.0 8.0 %all_to_all.46 = bf16[4,8,3072]{2,1,0:T(8,128)(2,1)S(1)} all-to-all(bf16[4,8,3072]{2,1,0:T(8,128)(2,1)S(1)} %broadcast_in_dim.31), channel_id=1, replica_groups=mesh['zq'=2,'za'=4,'x'=4,'c'=2,'zh'=2,'y'=4] {'za'}, dimensions={0} | all-to-all | bytes 393216 | tf_op jit(solution)/shard_map/all_to_all | solution.py:22
  161.0 3.5 %all-to-all-start.7 = ((bf16[4,4,8,3072]{3,2,1,0:T(8,128)(2,1)}), bf16[4,4,8,3072]{3,2,1,0:T(8,128)(2,1)S(1)}, u32[]{:S(2)}, u32[]{:S(2)}) async-start(bf16[4,4,8,3072]{3,2,1,0:T(8,128)(2,1)} %broadcast_in_dim.32), calls=%async_computation.7 | async-start | bytes 1572864 | tf_op jit(solution)/shard_map/all_to_all | solution.py:22
  164.5 2.8 %collective-permute-start.11 = (bf16[128,512]{1,0:T(8,128)(2,1)S(1)}, bf16[128,512]{1,0:T(8,128)(2,1)}, u32[]{:S(2)}, u32[]{:S(2)}) collective-permute-start(bf16[128,512]{1,0:T(8,128)(2,1)S(1)} %multiply_convert_fusion), channel_id=1, source_target_pairs={{0,3},{1,0},{2,1},{3,2},{4,7},{5,4},{6,5},{7,6},{8,11},{9,8},{10,9... | collective-permute-start | bytes 393224 | tf_op jit(solution)/shard_map/ppermute | solution.py:35
  167.3 3.1 %collective-permute-start.10 = (bf16[128,512]{1,0:T(8,128)(2,1)S(1)}, bf16[128,512]{1,0:T(8,128)(2,1)}, u32[]{:S(2)}, u32[]{:S(2)}) collective-permute-start(bf16[128,512]{1,0:T(8,128)(2,1)S(1)} %multiply_convert_fusion), channel_id=1, source_target_pairs={{0,2},{1,3},{2,0},{3,1},{4,6},{5,7},{6,4},{7,5},{8,10},{9,11},{10,... | collective-permute-start | bytes 393224 | tf_op jit(solution)/shard_map/ppermute | solution.py:35
  170.4 1.9 collective-permute-start.9
  175.0 9.1 %collective-permute-start.7 = (bf16[128,512]{1,0:T(8,128)(2,1)S(1)}, bf16[128,512]{1,0:T(8,128)(2,1)S(1)}, u32[]{:S(2)}, u32[]{:S(2)}) collective-permute-start(bf16[128,512]{1,0:T(8,128)(2,1)S(1)} %convert_element_type.101), channel_id=1, source_target_pairs={{0,4},{4,0},{1,5},{5,1},{2,6},{6,2},{3,7},{7,3},{8,12},{12,8},{9,1... | collective-permute-start | bytes 393224 | tf_op jit(solution)/shard_map/ppermute | solution.py:35
  184.8 4.1 %collective-permute-start.14 = (bf16[128,768]{1,0:T(8,128)(2,1)}, bf16[128,768]{1,0:T(8,128)(2,1)S(1)}, u32[]{:S(2)}, u32[]{:S(2)}) collective-permute-start(bf16[128,768]{1,0:T(8,128)(2,1)} %get-tuple-element.41), channel_id=1, source_target_pairs={{0,3},{1,0},{2,1},{3,2},{4,7},{5,4},{6,5},{7,6},{8,11},{9,8},{10,9... | collective-permute-start | bytes 589832 | tf_op jit(solution)/shard_map/ppermute | solution.py:35
  189.0 2.5 %collective-permute-start.13 = (bf16[128,768]{1,0:T(8,128)(2,1)S(1)}, bf16[128,768]{1,0:T(8,128)(2,1)S(1)}, u32[]{:S(2)}, u32[]{:S(2)}) collective-permute-start(bf16[128,768]{1,0:T(8,128)(2,1)S(1)} %get-tuple-element.42), channel_id=1, source_target_pairs={{0,2},{1,3},{2,0},{3,1},{4,6},{5,7},{6,4},{7,5},{8,10},{9,11},{10,... | collective-permute-start | bytes 589832 | tf_op jit(solution)/shard_map/ppermute | solution.py:35
  191.8 2.9 %collective-permute-start.12 = (bf16[128,768]{1,0:T(8,128)(2,1)S(1)}, bf16[128,768]{1,0:T(8,128)(2,1)S(1)}, u32[]{:S(2)}, u32[]{:S(2)}) collective-permute-start(bf16[128,768]{1,0:T(8,128)(2,1)S(1)} %get-tuple-element.43), channel_id=1, source_target_pairs={{0,1},{1,2},{2,3},{3,0},{4,5},{5,6},{6,7},{7,4},{8,9},{9,10},{10,1... | collective-permute-start | bytes 589832 | tf_op jit(solution)/shard_map/ppermute | solution.py:35
  195.7 3.7 %all-to-all-start.8 = ((bf16[4,128,512]{2,1,0:T(8,128)(2,1)}), bf16[4,128,512]{2,1,0:T(8,128)(2,1)S(1)}, u32[]{:S(2)}, u32[]{:S(2)}) async-start(bf16[4,128,512]{2,1,0:T(8,128)(2,1)} %broadcast_in_dim.33), calls=%async_computation.8 | async-start | bytes 1048576 | tf_op jit(solution)/shard_map/all_to_all | solution.py:22
  201.7 11.2 %collective-permute-start.15 = (bf16[256,768]{1,0:T(8,128)(2,1)S(1)}, bf16[256,768]{1,0:T(8,128)(2,1)S(1)}, u32[]{:S(2)}, u32[]{:S(2)}) collective-permute-start(bf16[256,768]{1,0:T(8,128)(2,1)S(1)} %fusion.4), channel_id=1, source_target_pairs={{0,8},{8,0},{1,9},{9,1},{2,10},{10,2},{3,11},{11,3},{4,12},{12,4},... | collective-permute-start | bytes 1179656 | tf_op jit(solution)/shard_map/ppermute | solution.py:35
  213.4 5.4 %collective-permute-start.8 = (bf16[768,256]{1,0:T(8,128)(2,1)S(1)}, bf16[768,256]{1,0:T(8,128)(2,1)S(1)}, u32[]{:S(2)}, u32[]{:S(2)}) collective-permute-start(bf16[768,256]{1,0:T(8,128)(2,1)S(1)} %fusion.3), channel_id=1, source_target_pairs={{0,8},{8,0},{1,9},{9,1},{2,10},{10,2},{3,11},{11,3},{4,12},{12,4},... | collective-permute-start | bytes 1179656 | tf_op jit(solution)/shard_map/ppermute | solution.py:35
  218.9 2.7 %multiply_add_fusion = (f32[256,768]{1,0:T(8,128)}, bf16[256,768]{1,0:T(8,128)(2,1)}) fusion(bf16[256,768]{1,0:T(8,128)(2,1)S(1)} %copy-done.12, f32[256,768]{1,0:T(8,128)} %param.12, bf16[256,768]{1,0:T(8,128)(2,1)S(1)} %collective-permute-done.15, bf16[128,768]{1,0:T(8,128)(2,1)S(1)} %copy-done.14, bf16[128,768]{1,0:T(8,128)(2,1)S(1)} %copy-done.16, ...), kind=kOutput, calls=%fused_computation.18 | convolution fusion | flops 206438400 | bytes 3801088 | tf_op jit(solution)/shard_map/tf,td->fd/dot_general | solution.py:143
  (94 shorter events, 26.5 us)
Async XLA Ops:
  26.2 12.1 %copy-start.11 = (bf16[256,768]{1,0:T(8,128)(2,1)S(1)}, bf16[256,768]{1,0:T(8,128)(2,1)}, u32[]{:S(2)}) copy-start(bf16[256,768]{1,0:T(8,128)(2,1)} %param.10) | copy-start | bytes 1179652
  27.3 37.5 %all-to-all-start.1 = ((bf16[4,128,768]{2,1,0:T(8,128)(2,1)}), bf16[4,128,768]{2,1,0:T(8,128)(2,1)S(1)}, u32[]{:S(2)}, u32[]{:S(2)}) async-start(bf16[4,128,768]{2,1,0:T(8,128)(2,1)} %broadcast_in_dim.28), calls=%async_computation.1 | async-start | bytes 1572864 | tf_op jit(solution)/shard_map/all_to_all | solution.py:22
  31.4 17.1 %collective-permute-start = (bf16[768,256]{1,0:T(8,128)(2,1)S(1)}, bf16[768,256]{1,0:T(8,128)(2,1)S(1)}, u32[]{:S(2)}, u32[]{:S(2)}) collective-permute-start(bf16[768,256]{1,0:T(8,128)(2,1)S(1)} %copy-done.5), channel_id=1, source_target_pairs={{0,8},{8,0},{1,9},{9,1},{2,10},{10,2},{3,11},{11,3},{4,12},{12,4},... | collective-permute-start | bytes 1179656 | tf_op jit(solution)/shard_map/ppermute | solution.py:35
  38.3 21.4 %collective-permute-start.1 = (bf16[256,768]{1,0:T(8,128)(2,1)S(1)}, bf16[256,768]{1,0:T(8,128)(2,1)S(1)}, u32[]{:S(2)}, u32[]{:S(2)}) collective-permute-start(bf16[256,768]{1,0:T(8,128)(2,1)S(1)} %copy-done.11), channel_id=1, source_target_pairs={{0,3},{1,0},{2,1},{3,2},{4,7},{5,4},{6,5},{7,6},{8,11},{9,8},{10,9... | collective-permute-start | bytes 1179656 | tf_op jit(solution)/shard_map/ppermute | solution.py:35
  43.0 21.9 %collective-permute-start.2 = (bf16[256,768]{1,0:T(8,128)(2,1)S(1)}, bf16[256,768]{1,0:T(8,128)(2,1)S(1)}, u32[]{:S(2)}, u32[]{:S(2)}) collective-permute-start(bf16[256,768]{1,0:T(8,128)(2,1)S(1)} %copy-done.11), channel_id=1, source_target_pairs={{0,1},{1,2},{2,3},{3,0},{4,5},{5,6},{6,7},{7,4},{8,9},{9,10},{10,1... | collective-permute-start | bytes 1179656 | tf_op jit(solution)/shard_map/ppermute | solution.py:35
  44.9 24.9 %collective-permute-start.3 = (bf16[256,768]{1,0:T(8,128)(2,1)S(1)}, bf16[256,768]{1,0:T(8,128)(2,1)}, u32[]{:S(2)}, u32[]{:S(2)}) collective-permute-start(bf16[256,768]{1,0:T(8,128)(2,1)S(1)} %copy-done.11), channel_id=1, source_target_pairs={{0,2},{1,3},{2,0},{3,1},{4,6},{5,7},{6,4},{7,5},{8,10},{9,11},{10,... | collective-permute-start | bytes 1179656 | tf_op jit(solution)/shard_map/ppermute | solution.py:35
  66.3 11.6 %all-to-all-start.2 = ((bf16[4,128,512]{2,1,0:T(8,128)(2,1)}), bf16[4,128,512]{2,1,0:T(8,128)(2,1)S(1)}, u32[]{:S(2)}, u32[]{:S(2)}) async-start(bf16[4,128,512]{2,1,0:T(8,128)(2,1)} %bitcast.5), calls=%async_computation.2 | async-start | bytes 1048576 | tf_op jit(solution)/shard_map/all_to_all | solution.py:22
  77.9 36.9 %collective-permute-start.5 = (bf16[256,3072]{1,0:T(8,128)(2,1)S(1)}, bf16[256,3072]{1,0:T(8,128)(2,1)S(1)}, u32[]{:S(2)}, u32[]{:S(2)}) collective-permute-start(bf16[256,3072]{1,0:T(8,128)(2,1)S(1)} %pad_maximum_fusion), channel_id=1, source_target_pairs={{0,8},{8,0},{1,9},{9,1},{2,10},{10,2},{3,11},{11,3},{4,12},{12,4},... | collective-permute-start | bytes 4718600 | tf_op jit(solution)/shard_map/ppermute | solution.py:35
  84.3 7.6 %all-to-all-start.3 = ((bf16[4,2,4,768]{3,2,1,0:T(4,128)(2,1)}), bf16[4,2,4,768]{3,2,1,0:T(4,128)(2,1)S(1)}, u32[]{:S(2)}, u32[]{:S(2)}) async-start(bf16[4,2,4,768]{3,2,1,0:T(4,128)(2,1)} %pad_maximum_fusion.6), calls=%async_computation.3 | async-start | bytes 98304 | tf_op jit(solution)/shard_map/all_to_all | solution.py:22
  92.1 21.7 %collective-permute-start.4 = (bf16[128,512]{1,0:T(8,128)(2,1)S(1)}, bf16[128,512]{1,0:T(8,128)(2,1)S(1)}, u32[]{:S(2)}, u32[]{:S(2)}) collective-permute-start(bf16[128,512]{1,0:T(8,128)(2,1)S(1)} %convert_element_type.89), channel_id=1, source_target_pairs={{0,4},{4,0},{1,5},{5,1},{2,6},{6,2},{3,7},{7,3},{8,12},{12,8},{9,1... | collective-permute-start | bytes 393224 | tf_op jit(solution)/shard_map/ppermute | solution.py:35
  116.3 14.5 %all-to-all-start.4 = ((bf16[4,32,3072]{2,1,0:T(8,128)(2,1)}), bf16[4,32,3072]{2,1,0:T(8,128)(2,1)S(1)}, u32[]{:S(2)}, u32[]{:S(2)}) async-start(bf16[4,32,3072]{2,1,0:T(8,128)(2,1)} %bitcast.47), calls=%async_computation.4 | async-start | bytes 1572864 | tf_op jit(solution)/shard_map/all_to_all | solution.py:22
  121.9 20.1 %copy-start.10 = (f32[4,3072]{1,0:T(4,128)S(1)}, f32[4,3072]{1,0:T(4,128)}, u32[]{:S(2)}) copy-start(f32[4,3072]{1,0:T(4,128)} %pad_maximum_fusion.7) | copy-start | bytes 147460
  131.6 10.5 %all-to-all-start.5 = ((bf16[4,8,3072]{2,1,0:T(8,128)(2,1)}), bf16[4,8,3072]{2,1,0:T(8,128)(2,1)S(1)}, u32[]{:S(2)}, u32[]{:S(2)}) async-start(bf16[4,8,3072]{2,1,0:T(8,128)(2,1)} %bitcast.27), calls=%async_computation.5 | async-start | bytes 393216 | tf_op jit(solution)/shard_map/all_to_all | solution.py:22
  142.1 9.8 %collective-permute-start.6 = (bf16[8,3072]{1,0:T(8,128)(2,1)S(1)}, bf16[8,3072]{1,0:T(8,128)(2,1)S(1)}, u32[]{:S(2)}, u32[]{:S(2)}) collective-permute-start(bf16[8,3072]{1,0:T(8,128)(2,1)S(1)} %fusion.21), channel_id=1, source_target_pairs={{0,256},{256,0},{1,257},{257,1},{2,258},{258,2},{3,259},{259,3},{4... | collective-permute-start | bytes 147464 | tf_op jit(solution)/shard_map/ppermute | solution.py:35
  161.0 11.8 %all-to-all-start.7 = ((bf16[4,4,8,3072]{3,2,1,0:T(8,128)(2,1)}), bf16[4,4,8,3072]{3,2,1,0:T(8,128)(2,1)S(1)}, u32[]{:S(2)}, u32[]{:S(2)}) async-start(bf16[4,4,8,3072]{3,2,1,0:T(8,128)(2,1)} %broadcast_in_dim.32), calls=%async_computation.7 | async-start | bytes 1572864 | tf_op jit(solution)/shard_map/all_to_all | solution.py:22
  164.5 24.4 %collective-permute-start.11 = (bf16[128,512]{1,0:T(8,128)(2,1)S(1)}, bf16[128,512]{1,0:T(8,128)(2,1)}, u32[]{:S(2)}, u32[]{:S(2)}) collective-permute-start(bf16[128,512]{1,0:T(8,128)(2,1)S(1)} %multiply_convert_fusion), channel_id=1, source_target_pairs={{0,3},{1,0},{2,1},{3,2},{4,7},{5,4},{6,5},{7,6},{8,11},{9,8},{10,9... | collective-permute-start | bytes 393224 | tf_op jit(solution)/shard_map/ppermute | solution.py:35
  167.3 32.1 %collective-permute-start.10 = (bf16[128,512]{1,0:T(8,128)(2,1)S(1)}, bf16[128,512]{1,0:T(8,128)(2,1)}, u32[]{:S(2)}, u32[]{:S(2)}) collective-permute-start(bf16[128,512]{1,0:T(8,128)(2,1)S(1)} %multiply_convert_fusion), channel_id=1, source_target_pairs={{0,2},{1,3},{2,0},{3,1},{4,6},{5,7},{6,4},{7,5},{8,10},{9,11},{10,... | collective-permute-start | bytes 393224 | tf_op jit(solution)/shard_map/ppermute | solution.py:35
  170.4 29.0 %collective-permute-start.9 = (bf16[128,512]{1,0:T(8,128)(2,1)S(1)}, bf16[128,512]{1,0:T(8,128)(2,1)}, u32[]{:S(2)}, u32[]{:S(2)}) collective-permute-start(bf16[128,512]{1,0:T(8,128)(2,1)S(1)} %multiply_convert_fusion), channel_id=1, source_target_pairs={{0,1},{1,2},{2,3},{3,0},{4,5},{5,6},{6,7},{7,4},{8,9},{9,10},{10,1... | collective-permute-start | bytes 393224 | tf_op jit(solution)/shard_map/ppermute | solution.py:35
  174.9 19.8 %copy-start.9 = (bf16[128,512]{1,0:T(8,128)(2,1)S(1)}, bf16[128,512]{1,0:T(8,128)(2,1)}, u32[]{:S(2)}) copy-start(bf16[128,512]{1,0:T(8,128)(2,1)} %copy-done.8) | copy-start | bytes 393220
  175.0 16.9 %collective-permute-start.7 = (bf16[128,512]{1,0:T(8,128)(2,1)S(1)}, bf16[128,512]{1,0:T(8,128)(2,1)S(1)}, u32[]{:S(2)}, u32[]{:S(2)}) collective-permute-start(bf16[128,512]{1,0:T(8,128)(2,1)S(1)} %convert_element_type.101), channel_id=1, source_target_pairs={{0,4},{4,0},{1,5},{5,1},{2,6},{6,2},{3,7},{7,3},{8,12},{12,8},{9,1... | collective-permute-start | bytes 393224 | tf_op jit(solution)/shard_map/ppermute | solution.py:35
  184.8 15.7 %collective-permute-start.14 = (bf16[128,768]{1,0:T(8,128)(2,1)}, bf16[128,768]{1,0:T(8,128)(2,1)S(1)}, u32[]{:S(2)}, u32[]{:S(2)}) collective-permute-start(bf16[128,768]{1,0:T(8,128)(2,1)} %get-tuple-element.41), channel_id=1, source_target_pairs={{0,3},{1,0},{2,1},{3,2},{4,7},{5,4},{6,5},{7,6},{8,11},{9,8},{10,9... | collective-permute-start | bytes 589832 | tf_op jit(solution)/shard_map/ppermute | solution.py:35
  189.0 11.6 %collective-permute-start.13 = (bf16[128,768]{1,0:T(8,128)(2,1)S(1)}, bf16[128,768]{1,0:T(8,128)(2,1)S(1)}, u32[]{:S(2)}, u32[]{:S(2)}) collective-permute-start(bf16[128,768]{1,0:T(8,128)(2,1)S(1)} %get-tuple-element.42), channel_id=1, source_target_pairs={{0,2},{1,3},{2,0},{3,1},{4,6},{5,7},{6,4},{7,5},{8,10},{9,11},{10,... | collective-permute-start | bytes 589832 | tf_op jit(solution)/shard_map/ppermute | solution.py:35
  191.8 8.7 %collective-permute-start.12 = (bf16[128,768]{1,0:T(8,128)(2,1)S(1)}, bf16[128,768]{1,0:T(8,128)(2,1)S(1)}, u32[]{:S(2)}, u32[]{:S(2)}) collective-permute-start(bf16[128,768]{1,0:T(8,128)(2,1)S(1)} %get-tuple-element.43), channel_id=1, source_target_pairs={{0,1},{1,2},{2,3},{3,0},{4,5},{5,6},{6,7},{7,4},{8,9},{9,10},{10,1... | collective-permute-start | bytes 589832 | tf_op jit(solution)/shard_map/ppermute | solution.py:35
  195.7 17.2 %all-to-all-start.8 = ((bf16[4,128,512]{2,1,0:T(8,128)(2,1)}), bf16[4,128,512]{2,1,0:T(8,128)(2,1)S(1)}, u32[]{:S(2)}, u32[]{:S(2)}) async-start(bf16[4,128,512]{2,1,0:T(8,128)(2,1)} %broadcast_in_dim.33), calls=%async_computation.8 | async-start | bytes 1048576 | tf_op jit(solution)/shard_map/all_to_all | solution.py:22
  201.3 11.7 %copy-start.4 = (bf16[4,4,32,768]{3,2,1,0:T(8,128)(2,1)S(1)}, bf16[4,4,32,768]{3,2,1,0:T(8,128)(2,1)}, u32[]{:S(2)}) copy-start(bf16[4,4,32,768]{3,2,1,0:T(8,128)(2,1)} %copy.22) | copy-start | bytes 2359300
  201.7 17.1 %copy-start.12 = (bf16[256,768]{1,0:T(8,128)(2,1)S(1)}, bf16[256,768]{1,0:T(8,128)(2,1)}, u32[]{:S(2)}) copy-start(bf16[256,768]{1,0:T(8,128)(2,1)} %param.10) | copy-start | bytes 1179652
  201.7 17.1 %copy-start.14 = (bf16[128,768]{1,0:T(8,128)(2,1)S(1)}, bf16[128,768]{1,0:T(8,128)(2,1)}, u32[]{:S(2)}) copy-start(bf16[128,768]{1,0:T(8,128)(2,1)} %copy-done.13) | copy-start | bytes 589828
  201.7 17.1 %collective-permute-start.15 = (bf16[256,768]{1,0:T(8,128)(2,1)S(1)}, bf16[256,768]{1,0:T(8,128)(2,1)S(1)}, u32[]{:S(2)}, u32[]{:S(2)}) collective-permute-start(bf16[256,768]{1,0:T(8,128)(2,1)S(1)} %fusion.4), channel_id=1, source_target_pairs={{0,8},{8,0},{1,9},{9,1},{2,10},{10,2},{3,11},{11,3},{4,12},{12,4},... | collective-permute-start | bytes 1179656 | tf_op jit(solution)/shard_map/ppermute | solution.py:35
  213.0 5.9 %copy-start.16 = (bf16[128,768]{1,0:T(8,128)(2,1)S(1)}, bf16[128,768]{1,0:T(8,128)(2,1)}, u32[]{:S(2)}) copy-start(bf16[128,768]{1,0:T(8,128)(2,1)} %copy-done.15) | copy-start | bytes 589828
  213.4 8.1 %copy-start.6 = (bf16[768,256]{1,0:T(8,128)(2,1)S(1)}, bf16[768,256]{1,0:T(8,128)(2,1)}, u32[]{:S(2)}) copy-start(bf16[768,256]{1,0:T(8,128)(2,1)} %param.9) | copy-start | bytes 1179652
  213.4 8.1 %copy-start.7 = (f32[768,256]{1,0:T(8,128)S(1)}, f32[768,256]{1,0:T(8,128)}, u32[]{:S(2)}) copy-start(f32[768,256]{1,0:T(8,128)} %param.11) | copy-start | bytes 2359300
  213.4 8.1 %collective-permute-start.8 = (bf16[768,256]{1,0:T(8,128)(2,1)S(1)}, bf16[768,256]{1,0:T(8,128)(2,1)S(1)}, u32[]{:S(2)}, u32[]{:S(2)}) collective-permute-start(bf16[768,256]{1,0:T(8,128)(2,1)S(1)} %fusion.3), channel_id=1, source_target_pairs={{0,8},{8,0},{1,9},{9,1},{2,10},{10,2},{3,11},{11,3},{4,12},{12,4},... | collective-permute-start | bytes 1179656 | tf_op jit(solution)/shard_map/ppermute | solution.py:35
  (10 other events, 22.7 us)

commit v6 on v5

--- a/solution.py
+++ b/solution.py
@@ -4,6 +4,7 @@
 import jax.numpy as jnp
 import numpy as np
 from jax import lax
+from jax.experimental.layout import Layout, with_layout_constraint
 from jax.sharding import Mesh
 from jax.sharding import PartitionSpec as P
 
@@ -13,6 +14,7 @@
 MP = ("zh", "y")
 BF = jnp.bfloat16
 F32 = jnp.float32
+
 
 decay_rate = 0.99
 step_size = 0.5
@@ -79,6 +81,7 @@
     source = at % (part // nx) // few * rows + at // (part // nx) * few + at % few
     order = jnp.asarray(np.eye(at.size, dtype=np.float32)[source], BF)
     near = dot(order, near.reshape(at.size, d)).astype(BF)
+    near = with_layout_constraint(near, Layout((0, 1)))
 
     arrived = gather(near, "x")
     arrived, w_both, w_ring[1], w_ring[3] = tie(arrived, w_both, w_ring[1], w_ring[3])
@@ -100,7 +103,10 @@
         [lax.dynamic_index_in_dim(own, (y + k) & (ny - 1), keepdims=False) for k in range(ny)],
         axis=1,
     )
-    own, other = tie(own, other)
+    mine = lax.broadcasted_iota(jnp.int32, (nq * few, 1), 0) // few == lax.axis_index("zq")
+    own = jnp.where(mine, jnp.concatenate([own] * nq, axis=0), 0.0)
+    first = lax.axis_index("c") == 0
+    own, other, first = tie(own, other, first)
     preact = sums + other.astype(F32)
     hidden = gelu_value(preact).astype(BF)
     hiddens = []
@@ -111,11 +117,12 @@
     partial_out, arrived = tie(partial_out, arrived)
     sums = scatter(partial_out.reshape(nx, part // nx, ny * d), "x")
     gathered_t = arrived.reshape(nx, ny, part // nx, d).swapaxes(0, 1).reshape(tokens, d).T
+    gathered_t = with_layout_constraint(gathered_t, Layout((0, 1)))
     sums, gathered_t = tie(sums, gathered_t)
     sums = scatter(sums.reshape(na, nq * few, ny * d), "za")
-    mine = lax.broadcasted_iota(jnp.int32, (nq * few, 1), 0) // few == lax.axis_index("zq")
-    sums = sums + jnp.where(mine, jnp.concatenate([own] * nq, axis=0), 0.0)
+    sums = sums + own
     other = shift(sums.astype(BF), "zq", 1)
+    turned = shift(gathered_t, "c", 1)
     slope = (sums + other.astype(F32)).astype(BF)
     slopes = gather(slope, "za")
     slopes = gather(slopes, "x")
@@ -131,10 +138,15 @@
     slopes, slope_part = tie(slopes, slope_part)
     other = shift(slope_part.astype(BF), "zh", 1)
     their_slopes = [shift(slopes[:, k * d : (k + 1) * d], "y", k) for k in range(1, ny)]
-    hidden_slope = slope_part + other.astype(F32)
-    pre_slope = (hidden_slope * gelu_slope(preact)).astype(BF)
-    pre_slopes = gather(pre_slope, "y")
-    pre_slopes = pre_slopes.reshape(tokens, 2 * f)
+    turned = jnp.concatenate(
+        [jnp.where(first, gathered_t, turned), jnp.where(first, turned, gathered_t)], axis=1
+    )
+    other, turned = tie(other, turned)
+    pre_slope = ((slope_part + other.astype(F32)) * gelu_slope(preact)).astype(BF)
+    halves = pre_slope[:, :f], pre_slope[:, f:]
+    halves = jnp.stack([jnp.where(first, *halves), jnp.where(first, *halves[::-1])])
+    halves = jnp.broadcast_to(halves[:, None], (2, ny, part, f)).reshape(2 * ny, part, f)
+    pre_slopes = exchange(halves, ("c", "y")).reshape(2 * tokens, f)
 
     hiddens = jnp.concatenate([hidden, *hiddens], axis=0)
     own_slopes = jnp.concatenate([slopes[:, :d], *their_slopes], axis=0)
@@ -142,12 +154,12 @@
     def grad_of(units):
         return jnp.einsum("tf,td->fd", units, own_slopes, preferred_element_type=F32) * out_scale
 
-    theirs = shift(grad_of(hiddens[:, f:]).astype(BF), "c", 1).astype(F32)
+    theirs = grad_of(hiddens[:, f:]).astype(BF)
+    theirs = shift(theirs, "c", 1).astype(F32)
     grad_out = grad_of(hiddens[:, :f]) + theirs
     new_out = ema(teach_out, w_out, grad_out)
 
-    theirs = shift((dot(gathered_t, pre_slopes[:, f:]) * in_scale).astype(BF), "c", 1).astype(F32)
-    grad_in = dot(gathered_t, pre_slopes[:, :f]) * in_scale + theirs
+    grad_in = dot(turned, pre_slopes) * in_scale
     new_in = ema(teach_in, w_in, grad_in)
     return (grad_in.astype(BF), grad_out.astype(BF), new_in, new_out)
 

time: 225 us -> 227 us (level)
  waiting for transfers between devices: 63.5 us -> 48.9 us
  blocking collectives: 31.9 us -> 44.1 us
  other arithmetic: 4.94 us -> 8.05 us
    all_to_all x2 -> x3, blocking collectives: 31.9 us -> 44.1 us  [exchange(): return lax.all_to_all(pieces, axis, split_axis=0, concat_axis=0, tiled=True)]
    all_to_all x7 -> x6, waiting for transfers between devices: 25.7 us -> 17.1 us  [exchange(): return lax.all_to_all(pieces, axis, split_axis=0, concat_axis=0, tiled=True)]
    ppermute x16, starting transfers between devices: 74.1 us -> 67.4 us  [shift(): return lax.ppermute(value, axis, [(i, (i + by) % n) for i in range(n)])]
    all_to_all x7 -> x6, starting transfers between devices: 27.9 us -> 34.3 us  [exchange(): return lax.all_to_all(pieces, axis, split_axis=0, concat_axis=0, tiled=True)]
    ppermute x16, waiting for transfers between devices: 37.8 us -> 31.8 us  [shift(): return lax.ppermute(value, axis, [(i, (i + by) % n) for i in range(n)])]
    dot_general x6 -> x5, matrix products: 5.23 us -> 5.01 us  [dot(): return jnp.dot(a, b, preferred_element_type=F32)]
  transfers between devices with their start and end apart: 23 -> 22, of which waited for: 10 -> 8; matrix products, arithmetic and copies ran while one was open for 6% -> 8% of each run, Pallas kernels for 0% -> 0%
where the time goes in v6:
time: 227 us; the launch traced here: 225 us
  starting transfers between devices  102 us (45%)
  waiting for transfers between devices  48.9 us (22%)
  blocking collectives  44.1 us (19%)
  matrix products  11.5 us (5%)
  local copies, waits for them, and re-layouts  9.75 us (4%)
  other arithmetic  8.05 us (4%)
    ppermute x16, starting transfers between devices, shift(): return lax.ppermute(value, axis, [(i, (i + by) % n) for i in range(n)])  67.4 us
    all_to_all x3, blocking collectives, exchange(): return lax.all_to_all(pieces, axis, split_axis=0, concat_axis=0, tiled=True)  44.1 us
    all_to_all x6, starting transfers between devices, exchange(): return lax.all_to_all(pieces, axis, split_axis=0, concat_axis=0, tiled=True)  34.3 us
    ppermute x16, waiting for transfers between devices, shift(): return lax.ppermute(value, axis, [(i, (i + by) % n) for i in range(n)])  31.8 us
    all_to_all x6, waiting for transfers between devices, exchange(): return lax.all_to_all(pieces, axis, split_axis=0, concat_axis=0, tiled=True)  17.1 us
    dot_general x2, matrix products, grad_of(): jnp.einsum('tf,td->fd', units, own_slopes, preferred_element_type=F32)  5.21 us
    dot_general x5, matrix products, dot(): return jnp.dot(a, b, preferred_element_type=F32)  5.01 us
  transfers between devices with their start and end apart: 22, of which 8 were waited for; matrix products, arithmetic and copies ran while one was open for 8% of the time, Pallas kernels for 0%

profile of v6, /device:TPU:1, one launch (start us, length us, event | category | flops | bytes accessed | tf_op | source)
XLA Modules:
  0.0 225.3 jit_solution(15868339309975222486)
XLA Ops:
  1.4 23.8 %all_to_all.45 = bf16[8,16,768]{2,1,0:T(8,128)(2,1)S(1)} all-to-all(bf16[8,16,768]{2,1,0:T(8,128)(2,1)S(1)} %broadcast_in_dim.30), channel_id=1, replica_groups=mesh['zq'=2,'za'=4,'x'=4,'c'=2,'zh'=2,'y'=4] {'za','zq'}, dimensions={0} | all-to-all | bytes 393216 | tf_op jit(solution)/shard_map/all_to_all | solution.py:24
  27.2 4.0 %all-to-all-start.1 = ((bf16[4,128,768]{2,1,0:T(8,128)(2,1)}), bf16[4,128,768]{2,1,0:T(8,128)(2,1)S(1)}, u32[]{:S(2)}, u32[]{:S(2)}) async-start(bf16[4,128,768]{2,1,0:T(8,128)(2,1)} %broadcast_in_dim.31), calls=%async_computation.1 | async-start | bytes 1572864 | tf_op jit(solution)/shard_map/all_to_all | solution.py:24
  31.2 6.9 %collective-permute-start = (bf16[768,256]{1,0:T(8,128)(2,1)S(1)}, bf16[768,256]{1,0:T(8,128)(2,1)S(1)}, u32[]{:S(2)}, u32[]{:S(2)}) collective-permute-start(bf16[768,256]{1,0:T(8,128)(2,1)S(1)} %copy-done.5), channel_id=1, source_target_pairs={{0,8},{8,0},{1,9},{9,1},{2,10},{10,2},{3,11},{11,3},{4,12},{12,4},... | collective-permute-start | bytes 1179656 | tf_op jit(solution)/shard_map/ppermute | solution.py:37
  38.2 4.6 %collective-permute-start.1 = (bf16[256,768]{1,0:T(8,128)(2,1)S(1)}, bf16[256,768]{1,0:T(8,128)(2,1)S(1)}, u32[]{:S(2)}, u32[]{:S(2)}) collective-permute-start(bf16[256,768]{1,0:T(8,128)(2,1)S(1)} %copy-done.12), channel_id=1, source_target_pairs={{0,3},{1,0},{2,1},{3,2},{4,7},{5,4},{6,5},{7,6},{8,11},{9,8},{10,9... | collective-permute-start | bytes 1179656 | tf_op jit(solution)/shard_map/ppermute | solution.py:37
  42.8 1.9 collective-permute-start.2
  46.0 3.5 %collective-permute-start.3 = (bf16[256,768]{1,0:T(8,128)(2,1)S(1)}, bf16[256,768]{1,0:T(8,128)(2,1)}, u32[]{:S(2)}, u32[]{:S(2)}) collective-permute-start(bf16[256,768]{1,0:T(8,128)(2,1)S(1)} %copy-done.12), channel_id=1, source_target_pairs={{0,2},{1,3},{2,0},{3,1},{4,6},{5,7},{6,4},{7,5},{8,10},{9,11},{10,... | collective-permute-start | bytes 1179656 | tf_op jit(solution)/shard_map/ppermute | solution.py:37
  51.3 13.5 %collective-permute-done.2 = bf16[256,768]{1,0:T(8,128)(2,1)S(1)} collective-permute-done((bf16[256,768]{1,0:T(8,128)(2,1)S(1)}, bf16[256,768]{1,0:T(8,128)(2,1)S(1)}, u32[]{:S(2)}, u32[]{:S(2)}) %collective-permute-start.2) | collective-permute-done | bytes 393248 | tf_op jit(solution)/shard_map/ppermute | solution.py:37
  66.2 3.5 %all-to-all-start.2 = ((bf16[4,128,512]{2,1,0:T(8,128)(2,1)}), bf16[4,128,512]{2,1,0:T(8,128)(2,1)S(1)}, u32[]{:S(2)}, u32[]{:S(2)}) async-start(bf16[4,128,512]{2,1,0:T(8,128)(2,1)} %bitcast.5), calls=%async_computation.2 | async-start | bytes 1048576 | tf_op jit(solution)/shard_map/all_to_all | solution.py:24
  71.5 6.2 %all-to-all-done.2 = bf16[4,128,512]{2,1,0:T(8,128)(2,1)S(1)} async-done(((bf16[4,128,512]{2,1,0:T(8,128)(2,1)}), bf16[4,128,512]{2,1,0:T(8,128)(2,1)S(1)}, u32[]{:S(2)}, u32[]{:S(2)}) %all-to-all-start.2) | async-done | bytes 524320 | tf_op jit(solution)/shard_map/all_to_all | solution.py:24
  77.8 3.3 %all-to-all-start.3 = ((bf16[4,2,4,768]{3,2,1,0:T(4,128)(2,1)}), bf16[4,2,4,768]{3,2,1,0:T(4,128)(2,1)S(1)}, u32[]{:S(2)}, u32[]{:S(2)}) async-start(bf16[4,2,4,768]{3,2,1,0:T(4,128)(2,1)} %pad_maximum_fusion.8), calls=%async_computation.3 | async-start | bytes 98304 | tf_op jit(solution)/shard_map/all_to_all | solution.py:24
  81.1 4.2 %collective-permute-start.5 = (bf16[256,3072]{1,0:T(8,128)(2,1)S(1)}, bf16[256,3072]{1,0:T(8,128)(2,1)S(1)}, u32[]{:S(2)}, u32[]{:S(2)}) collective-permute-start(bf16[256,3072]{1,0:T(8,128)(2,1)S(1)} %pad_maximum_fusion), channel_id=1, source_target_pairs={{0,8},{8,0},{1,9},{9,1},{2,10},{10,2},{3,11},{11,3},{4,12},{12,4},... | collective-permute-start | bytes 4718600 | tf_op jit(solution)/shard_map/ppermute | solution.py:37
  85.5 7.9 %collective-permute-start.4 = (bf16[128,512]{1,0:T(8,128)(2,1)S(1)}, bf16[128,512]{1,0:T(8,128)(2,1)S(1)}, u32[]{:S(2)}, u32[]{:S(2)}) collective-permute-start(bf16[128,512]{1,0:T(8,128)(2,1)S(1)} %convert_element_type.83), channel_id=1, source_target_pairs={{0,4},{4,0},{1,5},{5,1},{2,6},{6,2},{3,7},{7,3},{8,12},{12,8},{9,1... | collective-permute-start | bytes 393224 | tf_op jit(solution)/shard_map/ppermute | solution.py:37
  94.2 12.1 %collective-permute-done.4 = bf16[128,512]{1,0:T(8,128)(2,1)S(1)} collective-permute-done((bf16[128,512]{1,0:T(8,128)(2,1)S(1)}, bf16[128,512]{1,0:T(8,128)(2,1)S(1)}, u32[]{:S(2)}, u32[]{:S(2)}) %collective-permute-start.4) | collective-permute-done | bytes 131104 | tf_op jit(solution)/shard_map/ppermute | solution.py:37
  108.8 4.6 %all-to-all-start.4 = ((bf16[4,32,3072]{2,1,0:T(8,128)(2,1)}), bf16[4,32,3072]{2,1,0:T(8,128)(2,1)}, u32[]{:S(2)}, u32[]{:S(2)}) async-start(bf16[4,32,3072]{2,1,0:T(8,128)(2,1)} %bitcast.50), calls=%async_computation.4 | async-start | bytes 1572864 | tf_op jit(solution)/shard_map/all_to_all | solution.py:24
  114.6 7.8 %all-to-all-done.4 = bf16[4,32,3072]{2,1,0:T(8,128)(2,1)} async-done(((bf16[4,32,3072]{2,1,0:T(8,128)(2,1)}), bf16[4,32,3072]{2,1,0:T(8,128)(2,1)}, u32[]{:S(2)}, u32[]{:S(2)}) %all-to-all-start.4) | async-done | bytes 786464 | tf_op jit(solution)/shard_map/all_to_all | solution.py:24
  123.7 12.3 %all_to_all.46 = bf16[4,8,3072]{2,1,0:T(8,128)(2,1)S(1)} all-to-all(bf16[4,8,3072]{2,1,0:T(8,128)(2,1)S(1)} %bitcast.53), channel_id=1, replica_groups=mesh['zq'=2,'za'=4,'x'=4,'c'=2,'zh'=2,'y'=4] {'za'}, dimensions={0} | all-to-all | bytes 393216 | tf_op jit(solution)/shard_map/all_to_all | solution.py:24
  136.0 1.9 collective-permute-start.6
  137.9 5.0 %collective-permute-start.8 = (bf16[768,512]{1,0:T(8,128)(2,1)}, bf16[768,512]{1,0:T(8,128)(2,1)S(1)}, u32[]{:S(2)}, u32[]{:S(2)}) collective-permute-start(bf16[768,512]{1,0:T(8,128)(2,1)} %bitcast.14), channel_id=1, source_target_pairs={{0,8},{8,0},{1,9},{9,1},{2,10},{10,2},{3,11},{11,3},{4,12},{12,4},... | collective-permute-start | bytes 2359304 | tf_op jit(solution)/shard_map/ppermute | solution.py:37
  142.9 3.4 %collective-permute-done.6 = bf16[8,3072]{1,0:T(8,128)(2,1)S(1)} collective-permute-done((bf16[8,3072]{1,0:T(8,128)(2,1)S(1)}, bf16[8,3072]{1,0:T(8,128)(2,1)S(1)}, u32[]{:S(2)}, u32[]{:S(2)}) %collective-permute-start.6) | collective-permute-done | bytes 49184 | tf_op jit(solution)/shard_map/ppermute | solution.py:37
  146.3 8.0 %all_to_all.47 = bf16[4,8,3072]{2,1,0:T(8,128)(2,1)S(1)} all-to-all(bf16[4,8,3072]{2,1,0:T(8,128)(2,1)S(1)} %broadcast_in_dim.34), channel_id=1, replica_groups=mesh['zq'=2,'za'=4,'x'=4,'c'=2,'zh'=2,'y'=4] {'za'}, dimensions={0} | all-to-all | bytes 393216 | tf_op jit(solution)/shard_map/all_to_all | solution.py:24
  155.3 3.5 %all-to-all-start.7 = ((bf16[4,4,8,3072]{3,2,1,0:T(8,128)(2,1)}), bf16[4,4,8,3072]{3,2,1,0:T(8,128)(2,1)S(1)}, u32[]{:S(2)}, u32[]{:S(2)}) async-start(bf16[4,4,8,3072]{3,2,1,0:T(8,128)(2,1)} %broadcast_in_dim.35), calls=%async_computation.7 | async-start | bytes 1572864 | tf_op jit(solution)/shard_map/all_to_all | solution.py:24
  158.8 5.1 %collective-permute-start.11 = (bf16[128,512]{1,0:T(8,128)(2,1)S(1)}, bf16[128,512]{1,0:T(8,128)(2,1)}, u32[]{:S(2)}, u32[]{:S(2)}) collective-permute-start(bf16[128,512]{1,0:T(8,128)(2,1)S(1)} %multiply_convert_fusion.1), channel_id=1, source_target_pairs={{0,3},{1,0},{2,1},{3,2},{4,7},{5,4},{6,5},{7,6},{8,11},{9,8},{10,9... | collective-permute-start | bytes 393224 | tf_op jit(solution)/shard_map/ppermute | solution.py:37
  163.9 2.7 %collective-permute-start.10 = (bf16[128,512]{1,0:T(8,128)(2,1)S(1)}, bf16[128,512]{1,0:T(8,128)(2,1)}, u32[]{:S(2)}, u32[]{:S(2)}) collective-permute-start(bf16[128,512]{1,0:T(8,128)(2,1)S(1)} %multiply_convert_fusion.1), channel_id=1, source_target_pairs={{0,2},{1,3},{2,0},{3,1},{4,6},{5,7},{6,4},{7,5},{8,10},{9,11},{10,... | collective-permute-start | bytes 393224 | tf_op jit(solution)/shard_map/ppermute | solution.py:37
  166.6 2.5 %collective-permute-start.9 = (bf16[128,512]{1,0:T(8,128)(2,1)S(1)}, bf16[128,512]{1,0:T(8,128)(2,1)}, u32[]{:S(2)}, u32[]{:S(2)}) collective-permute-start(bf16[128,512]{1,0:T(8,128)(2,1)S(1)} %multiply_convert_fusion.1), channel_id=1, source_target_pairs={{0,1},{1,2},{2,3},{3,0},{4,5},{5,6},{6,7},{7,4},{8,9},{9,10},{10,1... | collective-permute-start | bytes 393224 | tf_op jit(solution)/shard_map/ppermute | solution.py:37
  174.0 8.6 %collective-permute-start.7 = (bf16[128,512]{1,0:T(8,128)(2,1)S(1)}, bf16[128,512]{1,0:T(8,128)(2,1)S(1)}, u32[]{:S(2)}, u32[]{:S(2)}) collective-permute-start(bf16[128,512]{1,0:T(8,128)(2,1)S(1)} %convert_element_type.95), channel_id=1, source_target_pairs={{0,4},{4,0},{1,5},{5,1},{2,6},{6,2},{3,7},{7,3},{8,12},{12,8},{9,1... | collective-permute-start | bytes 393224 | tf_op jit(solution)/shard_map/ppermute | solution.py:37
  183.3 4.0 %collective-permute-start.14 = (bf16[128,768]{1,0:T(8,128)(2,1)S(1)}, bf16[128,768]{1,0:T(8,128)(2,1)}, u32[]{:S(2)}, u32[]{:S(2)}) collective-permute-start(bf16[128,768]{1,0:T(8,128)(2,1)S(1)} %get-tuple-element.51), channel_id=1, source_target_pairs={{0,3},{1,0},{2,1},{3,2},{4,7},{5,4},{6,5},{7,6},{8,11},{9,8},{10,9... | collective-permute-start | bytes 589832 | tf_op jit(solution)/shard_map/ppermute | solution.py:37
  188.4 3.6 %collective-permute-start.13 = (bf16[128,768]{1,0:T(8,128)(2,1)S(1)}, bf16[128,768]{1,0:T(8,128)(2,1)}, u32[]{:S(2)}, u32[]{:S(2)}) collective-permute-start(bf16[128,768]{1,0:T(8,128)(2,1)S(1)} %get-tuple-element.52), channel_id=1, source_target_pairs={{0,2},{1,3},{2,0},{3,1},{4,6},{5,7},{6,4},{7,5},{8,10},{9,11},{10,... | collective-permute-start | bytes 589832 | tf_op jit(solution)/shard_map/ppermute | solution.py:37
  192.2 2.9 %collective-permute-start.12 = (bf16[128,768]{1,0:T(8,128)(2,1)S(1)}, bf16[128,768]{1,0:T(8,128)(2,1)S(1)}, u32[]{:S(2)}, u32[]{:S(2)}) collective-permute-start(bf16[128,768]{1,0:T(8,128)(2,1)S(1)} %get-tuple-element.53), channel_id=1, source_target_pairs={{0,1},{1,2},{2,3},{3,0},{4,5},{5,6},{6,7},{7,4},{8,9},{9,10},{10,1... | collective-permute-start | bytes 589832 | tf_op jit(solution)/shard_map/ppermute | solution.py:37
  196.0 15.5 %all-to-all-start.8 = ((bf16[8,128,256]{2,1,0:T(8,128)(2,1)}), bf16[8,128,256]{2,1,0:T(8,128)(2,1)S(1)}, u32[]{:S(2)}, u32[]{:S(2)}) async-start(bf16[8,128,256]{2,1,0:T(8,128)(2,1)} %bitcast.19), calls=%async_computation.8 | async-start | bytes 1048576 | tf_op jit(solution)/shard_map/all_to_all | solution.py:24
  213.3 2.5 %fusion.3 = bf16[256,768]{1,0:T(8,128)(2,1)} fusion(bf16[512,512]{1,0:T(8,128)(2,1)S(1)} %pad_maximum_fusion.4, bf16[128,768]{1,0:T(8,128)(2,1)} %collective-permute-done.14, bf16[128,768]{1,0:T(8,128)(2,1)} %collective-permute-done.13, bf16[128,768]{1,0:T(8,128)(2,1)} %copy-done.21, bf16[128,768]{1,0:T(8,128)(2,1)} %get-tuple-element.50), kind=kOutput, calls=%fused_computation.10 | convolution fusion | flops 204865536 | bytes 1441792 | tf_op jit(solution)/shard_map/tf,td->fd/dot_general | solution.py:155
  217.7 3.0 %all-to-all-done.8 = bf16[8,128,256]{2,1,0:T(8,128)(2,1)S(1)} async-done(((bf16[8,128,256]{2,1,0:T(8,128)(2,1)}), bf16[8,128,256]{2,1,0:T(8,128)(2,1)S(1)}, u32[]{:S(2)}, u32[]{:S(2)}) %all-to-all-start.8) | async-done | bytes 524320 | tf_op jit(solution)/shard_map/all_to_all | solution.py:24
  222.5 2.7 %multiply_add_fusion = (f32[256,768]{1,0:T(8,128)}, bf16[256,768]{1,0:T(8,128)(2,1)}) fusion(bf16[256,768]{1,0:T(8,128)(2,1)S(1)} %copy-done.13, f32[256,768]{1,0:T(8,128)S(1)} %copy-done.20, bf16[256,768]{1,0:T(8,128)(2,1)} %collective-permute-done.15, bf16[128,768]{1,0:T(8,128)(2,1)} %collective-permute-done.14, ...), kind=kOutput, calls=%fused_computation.16 | convolution fusion | flops 206438400 | bytes 3801088 | tf_op jit(solution)/shard_map/tf,td->fd/dot_general | solution.py:155
  (104 shorter events, 28.9 us)
Async XLA Ops:
  25.2 6.0 %copy-start.5 = (bf16[768,256]{1,0:T(8,128)(2,1)S(1)}, bf16[768,256]{1,0:T(8,128)(2,1)}, u32[]{:S(2)}) copy-start(bf16[768,256]{1,0:T(8,128)(2,1)} %param.9) | copy-start | bytes 1179652
  25.2 12.9 %copy-start.12 = (bf16[256,768]{1,0:T(8,128)(2,1)S(1)}, bf16[256,768]{1,0:T(8,128)(2,1)}, u32[]{:S(2)}) copy-start(bf16[256,768]{1,0:T(8,128)(2,1)} %param.10) | copy-start | bytes 1179652
  25.2 19.5 %copy-start.16 = (bf16[16,768]{1,0:T(8,128)(2,1)S(1)}, bf16[16,768]{1,0:T(8,128)(2,1)}, u32[]{:S(2)}) copy-start(bf16[16,768]{1,0:T(8,128)(2,1)} %param.7) | copy-start | bytes 73732
  25.2 20.2 %copy-start.19 = (bf16[16,768]{1,0:T(8,128)(2,1)S(1)}, bf16[16,768]{1,0:T(8,128)(2,1)}, u32[]{:S(2)}) copy-start(bf16[16,768]{1,0:T(8,128)(2,1)} %param.8) | copy-start | bytes 73732
  27.2 37.5 %all-to-all-start.1 = ((bf16[4,128,768]{2,1,0:T(8,128)(2,1)}), bf16[4,128,768]{2,1,0:T(8,128)(2,1)S(1)}, u32[]{:S(2)}, u32[]{:S(2)}) async-start(bf16[4,128,768]{2,1,0:T(8,128)(2,1)} %broadcast_in_dim.31), calls=%async_computation.1 | async-start | bytes 1572864 | tf_op jit(solution)/shard_map/all_to_all | solution.py:24
  31.2 18.3 %collective-permute-start = (bf16[768,256]{1,0:T(8,128)(2,1)S(1)}, bf16[768,256]{1,0:T(8,128)(2,1)S(1)}, u32[]{:S(2)}, u32[]{:S(2)}) collective-permute-start(bf16[768,256]{1,0:T(8,128)(2,1)S(1)} %copy-done.5), channel_id=1, source_target_pairs={{0,8},{8,0},{1,9},{9,1},{2,10},{10,2},{3,11},{11,3},{4,12},{12,4},... | collective-permute-start | bytes 1179656 | tf_op jit(solution)/shard_map/ppermute | solution.py:37
  38.2 13.1 %collective-permute-start.1 = (bf16[256,768]{1,0:T(8,128)(2,1)S(1)}, bf16[256,768]{1,0:T(8,128)(2,1)S(1)}, u32[]{:S(2)}, u32[]{:S(2)}) collective-permute-start(bf16[256,768]{1,0:T(8,128)(2,1)S(1)} %copy-done.12), channel_id=1, source_target_pairs={{0,3},{1,0},{2,1},{3,2},{4,7},{5,4},{6,5},{7,6},{8,11},{9,8},{10,9... | collective-permute-start | bytes 1179656 | tf_op jit(solution)/shard_map/ppermute | solution.py:37
  42.8 21.9 %collective-permute-start.2 = (bf16[256,768]{1,0:T(8,128)(2,1)S(1)}, bf16[256,768]{1,0:T(8,128)(2,1)S(1)}, u32[]{:S(2)}, u32[]{:S(2)}) collective-permute-start(bf16[256,768]{1,0:T(8,128)(2,1)S(1)} %copy-done.12), channel_id=1, source_target_pairs={{0,1},{1,2},{2,3},{3,0},{4,5},{5,6},{6,7},{7,4},{8,9},{9,10},{10,1... | collective-permute-start | bytes 1179656 | tf_op jit(solution)/shard_map/ppermute | solution.py:37
  46.0 24.3 %collective-permute-start.3 = (bf16[256,768]{1,0:T(8,128)(2,1)S(1)}, bf16[256,768]{1,0:T(8,128)(2,1)}, u32[]{:S(2)}, u32[]{:S(2)}) collective-permute-start(bf16[256,768]{1,0:T(8,128)(2,1)S(1)} %copy-done.12), channel_id=1, source_target_pairs={{0,2},{1,3},{2,0},{3,1},{4,6},{5,7},{6,4},{7,5},{8,10},{9,11},{10,... | collective-permute-start | bytes 1179656 | tf_op jit(solution)/shard_map/ppermute | solution.py:37
  66.2 11.6 %all-to-all-start.2 = ((bf16[4,128,512]{2,1,0:T(8,128)(2,1)}), bf16[4,128,512]{2,1,0:T(8,128)(2,1)S(1)}, u32[]{:S(2)}, u32[]{:S(2)}) async-start(bf16[4,128,512]{2,1,0:T(8,128)(2,1)} %bitcast.5), calls=%async_computation.2 | async-start | bytes 1048576 | tf_op jit(solution)/shard_map/all_to_all | solution.py:24
  77.8 7.6 %all-to-all-start.3 = ((bf16[4,2,4,768]{3,2,1,0:T(4,128)(2,1)}), bf16[4,2,4,768]{3,2,1,0:T(4,128)(2,1)S(1)}, u32[]{:S(2)}, u32[]{:S(2)}) async-start(bf16[4,2,4,768]{3,2,1,0:T(4,128)(2,1)} %pad_maximum_fusion.8), calls=%async_computation.3 | async-start | bytes 98304 | tf_op jit(solution)/shard_map/all_to_all | solution.py:24
  81.1 26.2 %collective-permute-start.5 = (bf16[256,3072]{1,0:T(8,128)(2,1)S(1)}, bf16[256,3072]{1,0:T(8,128)(2,1)S(1)}, u32[]{:S(2)}, u32[]{:S(2)}) collective-permute-start(bf16[256,3072]{1,0:T(8,128)(2,1)S(1)} %pad_maximum_fusion), channel_id=1, source_target_pairs={{0,8},{8,0},{1,9},{9,1},{2,10},{10,2},{3,11},{11,3},{4,12},{12,4},... | collective-permute-start | bytes 4718600 | tf_op jit(solution)/shard_map/ppermute | solution.py:37
  85.5 20.7 %collective-permute-start.4 = (bf16[128,512]{1,0:T(8,128)(2,1)S(1)}, bf16[128,512]{1,0:T(8,128)(2,1)S(1)}, u32[]{:S(2)}, u32[]{:S(2)}) collective-permute-start(bf16[128,512]{1,0:T(8,128)(2,1)S(1)} %convert_element_type.83), channel_id=1, source_target_pairs={{0,4},{4,0},{1,5},{5,1},{2,6},{6,2},{3,7},{7,3},{8,12},{12,8},{9,1... | collective-permute-start | bytes 393224 | tf_op jit(solution)/shard_map/ppermute | solution.py:37
  108.8 4.6 %copy-start.4 = (bf16[4,128,768]{2,1,0:T(8,128)(2,1)S(1)}, bf16[4,128,768]{2,1,0:T(8,128)(2,1)}, u32[]{:S(2)}) copy-start(bf16[4,128,768]{2,1,0:T(8,128)(2,1)} %copy-done.3) | copy-start | bytes 2359300
  108.8 13.7 %all-to-all-start.4 = ((bf16[4,32,3072]{2,1,0:T(8,128)(2,1)}), bf16[4,32,3072]{2,1,0:T(8,128)(2,1)}, u32[]{:S(2)}, u32[]{:S(2)}) async-start(bf16[4,32,3072]{2,1,0:T(8,128)(2,1)} %bitcast.50), calls=%async_computation.4 | async-start | bytes 1572864 | tf_op jit(solution)/shard_map/all_to_all | solution.py:24
  113.4 22.5 %copy-start.14 = (f32[8,3072]{1,0:T(8,128)S(1)}, f32[8,3072]{1,0:T(8,128)}, u32[]{:S(2)}) copy-start(f32[8,3072]{1,0:T(8,128)} %maximum_select_fusion) | copy-start | bytes 294916
  136.0 10.3 %collective-permute-start.6 = (bf16[8,3072]{1,0:T(8,128)(2,1)S(1)}, bf16[8,3072]{1,0:T(8,128)(2,1)S(1)}, u32[]{:S(2)}, u32[]{:S(2)}) collective-permute-start(bf16[8,3072]{1,0:T(8,128)(2,1)S(1)} %get-tuple-element.42), channel_id=1, source_target_pairs={{0,256},{256,0},{1,257},{257,1},{2,258},{258,2},{3,259},{259,3},{4... | collective-permute-start | bytes 147464 | tf_op jit(solution)/shard_map/ppermute | solution.py:37
  137.9 31.3 %collective-permute-start.8 = (bf16[768,512]{1,0:T(8,128)(2,1)}, bf16[768,512]{1,0:T(8,128)(2,1)S(1)}, u32[]{:S(2)}, u32[]{:S(2)}) collective-permute-start(bf16[768,512]{1,0:T(8,128)(2,1)} %bitcast.14), channel_id=1, source_target_pairs={{0,8},{8,0},{1,9},{9,1},{2,10},{10,2},{3,11},{11,3},{4,12},{12,4},... | collective-permute-start | bytes 2359304 | tf_op jit(solution)/shard_map/ppermute | solution.py:37
  155.3 16.5 %all-to-all-start.7 = ((bf16[4,4,8,3072]{3,2,1,0:T(8,128)(2,1)}), bf16[4,4,8,3072]{3,2,1,0:T(8,128)(2,1)S(1)}, u32[]{:S(2)}, u32[]{:S(2)}) async-start(bf16[4,4,8,3072]{3,2,1,0:T(8,128)(2,1)} %broadcast_in_dim.35), calls=%async_computation.7 | async-start | bytes 1572864 | tf_op jit(solution)/shard_map/all_to_all | solution.py:24
  158.8 33.4 %collective-permute-start.11 = (bf16[128,512]{1,0:T(8,128)(2,1)S(1)}, bf16[128,512]{1,0:T(8,128)(2,1)}, u32[]{:S(2)}, u32[]{:S(2)}) collective-permute-start(bf16[128,512]{1,0:T(8,128)(2,1)S(1)} %multiply_convert_fusion.1), channel_id=1, source_target_pairs={{0,3},{1,0},{2,1},{3,2},{4,7},{5,4},{6,5},{7,6},{8,11},{9,8},{10,9... | collective-permute-start | bytes 393224 | tf_op jit(solution)/shard_map/ppermute | solution.py:37
  163.9 47.5 %collective-permute-start.10 = (bf16[128,512]{1,0:T(8,128)(2,1)S(1)}, bf16[128,512]{1,0:T(8,128)(2,1)}, u32[]{:S(2)}, u32[]{:S(2)}) collective-permute-start(bf16[128,512]{1,0:T(8,128)(2,1)S(1)} %multiply_convert_fusion.1), channel_id=1, source_target_pairs={{0,2},{1,3},{2,0},{3,1},{4,6},{5,7},{6,4},{7,5},{8,10},{9,11},{10,... | collective-permute-start | bytes 393224 | tf_op jit(solution)/shard_map/ppermute | solution.py:37
  166.6 44.8 %collective-permute-start.9 = (bf16[128,512]{1,0:T(8,128)(2,1)S(1)}, bf16[128,512]{1,0:T(8,128)(2,1)}, u32[]{:S(2)}, u32[]{:S(2)}) collective-permute-start(bf16[128,512]{1,0:T(8,128)(2,1)S(1)} %multiply_convert_fusion.1), channel_id=1, source_target_pairs={{0,1},{1,2},{2,3},{3,0},{4,5},{5,6},{6,7},{7,4},{8,9},{9,10},{10,1... | collective-permute-start | bytes 393224 | tf_op jit(solution)/shard_map/ppermute | solution.py:37
  173.9 18.1 %copy-start.11 = (bf16[128,512]{1,0:T(8,128)(2,1)S(1)}, bf16[128,512]{1,0:T(8,128)(2,1)}, u32[]{:S(2)}) copy-start(bf16[128,512]{1,0:T(8,128)(2,1)} %copy-done.10) | copy-start | bytes 393220
  174.0 14.5 %collective-permute-start.7 = (bf16[128,512]{1,0:T(8,128)(2,1)S(1)}, bf16[128,512]{1,0:T(8,128)(2,1)S(1)}, u32[]{:S(2)}, u32[]{:S(2)}) collective-permute-start(bf16[128,512]{1,0:T(8,128)(2,1)S(1)} %convert_element_type.95), channel_id=1, source_target_pairs={{0,4},{4,0},{1,5},{5,1},{2,6},{6,2},{3,7},{7,3},{8,12},{12,8},{9,1... | collective-permute-start | bytes 393224 | tf_op jit(solution)/shard_map/ppermute | solution.py:37
  183.3 29.3 %collective-permute-start.14 = (bf16[128,768]{1,0:T(8,128)(2,1)S(1)}, bf16[128,768]{1,0:T(8,128)(2,1)}, u32[]{:S(2)}, u32[]{:S(2)}) collective-permute-start(bf16[128,768]{1,0:T(8,128)(2,1)S(1)} %get-tuple-element.51), channel_id=1, source_target_pairs={{0,3},{1,0},{2,1},{3,2},{4,7},{5,4},{6,5},{7,6},{8,11},{9,8},{10,9... | collective-permute-start | bytes 589832 | tf_op jit(solution)/shard_map/ppermute | solution.py:37
  188.4 24.1 %collective-permute-start.13 = (bf16[128,768]{1,0:T(8,128)(2,1)S(1)}, bf16[128,768]{1,0:T(8,128)(2,1)}, u32[]{:S(2)}, u32[]{:S(2)}) collective-permute-start(bf16[128,768]{1,0:T(8,128)(2,1)S(1)} %get-tuple-element.52), channel_id=1, source_target_pairs={{0,2},{1,3},{2,0},{3,1},{4,6},{5,7},{6,4},{7,5},{8,10},{9,11},{10,... | collective-permute-start | bytes 589832 | tf_op jit(solution)/shard_map/ppermute | solution.py:37
  192.2 20.3 %collective-permute-start.12 = (bf16[128,768]{1,0:T(8,128)(2,1)S(1)}, bf16[128,768]{1,0:T(8,128)(2,1)S(1)}, u32[]{:S(2)}, u32[]{:S(2)}) collective-permute-start(bf16[128,768]{1,0:T(8,128)(2,1)S(1)} %get-tuple-element.53), channel_id=1, source_target_pairs={{0,1},{1,2},{2,3},{3,0},{4,5},{5,6},{6,7},{7,4},{8,9},{9,10},{10,1... | collective-permute-start | bytes 589832 | tf_op jit(solution)/shard_map/ppermute | solution.py:37
  196.0 24.8 %all-to-all-start.8 = ((bf16[8,128,256]{2,1,0:T(8,128)(2,1)}), bf16[8,128,256]{2,1,0:T(8,128)(2,1)S(1)}, u32[]{:S(2)}, u32[]{:S(2)}) async-start(bf16[8,128,256]{2,1,0:T(8,128)(2,1)} %bitcast.19), calls=%async_computation.8 | async-start | bytes 1048576 | tf_op jit(solution)/shard_map/all_to_all | solution.py:24
  213.3 7.5 %copy-start = (bf16[768,1024]{1,0:T(8,128)(2,1)S(1)}, bf16[768,1024]{1,0:T(8,128)(2,1)}, u32[]{:S(2)}) copy-start(bf16[768,1024]{1,0:T(8,128)(2,1)} %pad_maximum_fusion.1) | copy-start | bytes 4718596
  213.3 7.5 %copy-start.6 = (bf16[768,256]{1,0:T(8,128)(2,1)S(1)}, bf16[768,256]{1,0:T(8,128)(2,1)}, u32[]{:S(2)}) copy-start(bf16[768,256]{1,0:T(8,128)(2,1)} %param.9) | copy-start | bytes 1179652
  213.3 7.5 %copy-start.7 = (f32[768,256]{1,0:T(8,128)S(1)}, f32[768,256]{1,0:T(8,128)}, u32[]{:S(2)}) copy-start(f32[768,256]{1,0:T(8,128)} %param.11) | copy-start | bytes 2359300
  215.8 6.7 %collective-permute-start.15 = (bf16[256,768]{1,0:T(8,128)(2,1)}, bf16[256,768]{1,0:T(8,128)(2,1)}, u32[]{:S(2)}, u32[]{:S(2)}) collective-permute-start(bf16[256,768]{1,0:T(8,128)(2,1)} %fusion.3), channel_id=1, source_target_pairs={{0,8},{8,0},{1,9},{9,1},{2,10},{10,2},{3,11},{11,3},{4,12},{12,4},... | collective-permute-start | bytes 1179656 | tf_op jit(solution)/shard_map/ppermute | solution.py:37
  (13 other events, 26.1 us)

commit v7 on v6

--- a/solution.py
+++ b/solution.py
@@ -90,8 +90,10 @@
     partial_pre = (dot(arrived.reshape(tokens, d), w_both) * in_scale).astype(BF)
     partial_pre = partial_pre.reshape(nx, ny, part // nx, 2 * f).swapaxes(0, 1)
     sums = scatter(partial_pre.reshape(ny, part, 2 * f), "y")
+    gathered_t = arrived.reshape(nx, ny, part // nx, d).swapaxes(0, 1).reshape(tokens, d).T
+    gathered_t = with_layout_constraint(gathered_t, Layout((0, 1)))
 
-    sums, w_ring = tie(sums, w_ring)
+    sums, w_ring, gathered_t = tie(sums, w_ring, gathered_t)
     other = shift(sums.astype(BF), "zh", 1)
     w_ring_theirs = shift(w_ring, "c", 1)
 
@@ -114,18 +116,14 @@
         hiddens.append(shift(hidden, "y", k))
 
     partial_out = (dot(hidden[:, :f], w_ring) + dot(hidden[:, f:], w_ring_theirs)) * out_scale
-    partial_out, arrived = tie(partial_out, arrived)
     sums = scatter(partial_out.reshape(nx, part // nx, ny * d), "x")
-    gathered_t = arrived.reshape(nx, ny, part // nx, d).swapaxes(0, 1).reshape(tokens, d).T
-    gathered_t = with_layout_constraint(gathered_t, Layout((0, 1)))
-    sums, gathered_t = tie(sums, gathered_t)
     sums = scatter(sums.reshape(na, nq * few, ny * d), "za")
     sums = sums + own
     other = shift(sums.astype(BF), "zq", 1)
     turned = shift(gathered_t, "c", 1)
     slope = (sums + other.astype(F32)).astype(BF)
     slopes = gather(slope, "za")
-    slopes = gather(slopes, "x")
+    slopes = lax.all_gather(slopes, "x")
     slopes = slopes.reshape(part, ny * d)
 
     slope_part = out_scale * jnp.concatenate(
@@ -156,7 +154,8 @@
 
     theirs = grad_of(hiddens[:, f:]).astype(BF)
     theirs = shift(theirs, "c", 1).astype(F32)
-    grad_out = grad_of(hiddens[:, :f]) + theirs
+    theirs, ours = tie(theirs, grad_of(hiddens[:, :f]))
+    grad_out = ours + theirs
     new_out = ema(teach_out, w_out, grad_out)
 
     grad_in = dot(turned, pre_slopes) * in_scale

time: 227 us -> 227 us (level)
  blocking collectives: 44.1 us -> 61 us
  waiting for transfers between devices: 48.9 us -> 38 us
  starting transfers between devices: 102 us -> 95.9 us
    all_gather x0 -> x1, blocking collectives: none -> 11.4 us  [shards(): slopes = lax.all_gather(slopes, 'x')]
    all_to_all x6 -> x5, waiting for transfers between devices: 17.1 us -> 8.11 us  [exchange(): return lax.all_to_all(pieces, axis, split_axis=0, concat_axis=0, tiled=True)]
    all_to_all x3, blocking collectives: 44.1 us -> 49.6 us  [exchange(): return lax.all_to_all(pieces, axis, split_axis=0, concat_axis=0, tiled=True)]
    all_to_all x6 -> x5, starting transfers between devices: 34.3 us -> 29.7 us  [exchange(): return lax.all_to_all(pieces, axis, split_axis=0, concat_axis=0, tiled=True)]
  transfers between devices with their start and end apart: 22 -> 21, of which waited for: 8 -> 7; matrix products, arithmetic and copies ran while one was open for 8% -> 8% of each run, Pallas kernels for 0% -> 0%
where the time goes in v7:
time: 227 us; the launch traced here: 226 us
  starting transfers between devices  95.9 us (42%)
  blocking collectives  61 us (27%)
  waiting for transfers between devices  38 us (17%)
  matrix products  11.3 us (5%)
  other arithmetic  10.3 us (5%)
  local copies, waits for them, and re-layouts  8.42 us (4%)
    ppermute x16, starting transfers between devices, shift(): return lax.ppermute(value, axis, [(i, (i + by) % n) for i in range(n)])  66.2 us
    all_to_all x3, blocking collectives, exchange(): return lax.all_to_all(pieces, axis, split_axis=0, concat_axis=0, tiled=True)  49.6 us
    ppermute x16, waiting for transfers between devices, shift(): return lax.ppermute(value, axis, [(i, (i + by) % n) for i in range(n)])  29.9 us
    all_to_all x5, starting transfers between devices, exchange(): return lax.all_to_all(pieces, axis, split_axis=0, concat_axis=0, tiled=True)  29.7 us
    all_gather x1, blocking collectives, shards(): slopes = lax.all_gather(slopes, 'x')  11.4 us
    all_to_all x5, waiting for transfers between devices, exchange(): return lax.all_to_all(pieces, axis, split_axis=0, concat_axis=0, tiled=True)  8.11 us
    dot_general x5, matrix products, dot(): return jnp.dot(a, b, preferred_element_type=F32)  5.23 us
    dot_general x2, matrix products, grad_of(): jnp.einsum('tf,td->fd', units, own_slopes, preferred_element_type=F32)  4.75 us
  transfers between devices with their start and end apart: 21, of which 7 were waited for; matrix products, arithmetic and copies ran while one was open for 8% of the time, Pallas kernels for 0%

profile of v7, /device:TPU:1, one launch (start us, length us, event | category | flops | bytes accessed | tf_op | source)
XLA Modules:
  0.0 226.0 jit_solution(5169054292405303372)
XLA Ops:
  1.4 23.8 %all_to_all.40 = bf16[8,16,768]{2,1,0:T(8,128)(2,1)S(1)} all-to-all(bf16[8,16,768]{2,1,0:T(8,128)(2,1)S(1)} %broadcast_in_dim.27), channel_id=1, replica_groups=mesh['zq'=2,'za'=4,'x'=4,'c'=2,'zh'=2,'y'=4] {'za','zq'}, dimensions={0} | all-to-all | bytes 393216 | tf_op jit(solution)/shard_map/all_to_all | solution.py:24
  27.2 4.0 %all-to-all-start.1 = ((bf16[4,128,768]{2,1,0:T(8,128)(2,1)}), bf16[4,128,768]{2,1,0:T(8,128)(2,1)S(1)}, u32[]{:S(2)}, u32[]{:S(2)}) async-start(bf16[4,128,768]{2,1,0:T(8,128)(2,1)} %broadcast_in_dim.28), calls=%async_computation.1 | async-start | bytes 1572864 | tf_op jit(solution)/shard_map/all_to_all | solution.py:24
  31.2 6.9 %collective-permute-start = (bf16[768,256]{1,0:T(8,128)(2,1)S(1)}, bf16[768,256]{1,0:T(8,128)(2,1)}, u32[]{:S(2)}, u32[]{:S(2)}) collective-permute-start(bf16[768,256]{1,0:T(8,128)(2,1)S(1)} %copy-done.3), channel_id=1, source_target_pairs={{0,8},{8,0},{1,9},{9,1},{2,10},{10,2},{3,11},{11,3},{4,12},{12,4},... | collective-permute-start | bytes 1179656 | tf_op jit(solution)/shard_map/ppermute | solution.py:37
  38.2 4.6 %collective-permute-start.1 = (bf16[256,768]{1,0:T(8,128)(2,1)S(1)}, bf16[256,768]{1,0:T(8,128)(2,1)S(1)}, u32[]{:S(2)}, u32[]{:S(2)}) collective-permute-start(bf16[256,768]{1,0:T(8,128)(2,1)S(1)} %copy-done.5), channel_id=1, source_target_pairs={{0,3},{1,0},{2,1},{3,2},{4,7},{5,4},{6,5},{7,6},{8,11},{9,8},{10,9... | collective-permute-start | bytes 1179656 | tf_op jit(solution)/shard_map/ppermute | solution.py:37
  44.8 3.5 %collective-permute-start.3 = (bf16[256,768]{1,0:T(8,128)(2,1)S(1)}, bf16[256,768]{1,0:T(8,128)(2,1)}, u32[]{:S(2)}, u32[]{:S(2)}) collective-permute-start(bf16[256,768]{1,0:T(8,128)(2,1)S(1)} %copy-done.5), channel_id=1, source_target_pairs={{0,2},{1,3},{2,0},{3,1},{4,6},{5,7},{6,4},{7,5},{8,10},{9,11},{10,... | collective-permute-start | bytes 1179656 | tf_op jit(solution)/shard_map/ppermute | solution.py:37
  49.4 10.1 %collective-permute-done.1 = bf16[256,768]{1,0:T(8,128)(2,1)S(1)} collective-permute-done((bf16[256,768]{1,0:T(8,128)(2,1)S(1)}, bf16[256,768]{1,0:T(8,128)(2,1)S(1)}, u32[]{:S(2)}, u32[]{:S(2)}) %collective-permute-start.1) | collective-permute-done | bytes 393248 | tf_op jit(solution)/shard_map/ppermute | solution.py:37
  59.6 5.2 %collective-permute-done.2 = bf16[256,768]{1,0:T(8,128)(2,1)S(1)} collective-permute-done((bf16[256,768]{1,0:T(8,128)(2,1)S(1)}, bf16[256,768]{1,0:T(8,128)(2,1)S(1)}, u32[]{:S(2)}, u32[]{:S(2)}) %collective-permute-start.2) | collective-permute-done | bytes 393248 | tf_op jit(solution)/shard_map/ppermute | solution.py:37
  66.9 3.5 %all-to-all-start.2 = ((bf16[4,128,512]{2,1,0:T(8,128)(2,1)}), bf16[4,128,512]{2,1,0:T(8,128)(2,1)S(1)}, u32[]{:S(2)}, u32[]{:S(2)}) async-start(bf16[4,128,512]{2,1,0:T(8,128)(2,1)} %bitcast.5), calls=%async_computation.2 | async-start | bytes 1048576 | tf_op jit(solution)/shard_map/all_to_all | solution.py:24
  73.5 5.0 %all-to-all-done.2 = bf16[4,128,512]{2,1,0:T(8,128)(2,1)S(1)} async-done(((bf16[4,128,512]{2,1,0:T(8,128)(2,1)}), bf16[4,128,512]{2,1,0:T(8,128)(2,1)S(1)}, u32[]{:S(2)}, u32[]{:S(2)}) %all-to-all-start.2) | async-done | bytes 524320 | tf_op jit(solution)/shard_map/all_to_all | solution.py:24
  78.5 3.3 %all-to-all-start.3 = ((bf16[4,2,4,768]{3,2,1,0:T(4,128)(2,1)}), bf16[4,2,4,768]{3,2,1,0:T(4,128)(2,1)S(1)}, u32[]{:S(2)}, u32[]{:S(2)}) async-start(bf16[4,2,4,768]{3,2,1,0:T(4,128)(2,1)} %pad_maximum_fusion.8), calls=%async_computation.3 | async-start | bytes 98304 | tf_op jit(solution)/shard_map/all_to_all | solution.py:24
  81.8 4.2 %collective-permute-start.5 = (bf16[256,3072]{1,0:T(8,128)(2,1)S(1)}, bf16[256,3072]{1,0:T(8,128)(2,1)S(1)}, u32[]{:S(2)}, u32[]{:S(2)}) collective-permute-start(bf16[256,3072]{1,0:T(8,128)(2,1)S(1)} %pad_maximum_fusion), channel_id=1, source_target_pairs={{0,8},{8,0},{1,9},{9,1},{2,10},{10,2},{3,11},{11,3},{4,12},{12,4},... | collective-permute-start | bytes 4718600 | tf_op jit(solution)/shard_map/ppermute | solution.py:37
  86.2 7.9 %collective-permute-start.4 = (bf16[128,512]{1,0:T(8,128)(2,1)S(1)}, bf16[128,512]{1,0:T(8,128)(2,1)S(1)}, u32[]{:S(2)}, u32[]{:S(2)}) collective-permute-start(bf16[128,512]{1,0:T(8,128)(2,1)S(1)} %convert_element_type.79), channel_id=1, source_target_pairs={{0,4},{4,0},{1,5},{5,1},{2,6},{6,2},{3,7},{7,3},{8,12},{12,8},{9,1... | collective-permute-start | bytes 393224 | tf_op jit(solution)/shard_map/ppermute | solution.py:37
  94.9 12.0 %collective-permute-done.4 = bf16[128,512]{1,0:T(8,128)(2,1)S(1)} collective-permute-done((bf16[128,512]{1,0:T(8,128)(2,1)S(1)}, bf16[128,512]{1,0:T(8,128)(2,1)S(1)}, u32[]{:S(2)}, u32[]{:S(2)}) %collective-permute-start.4) | collective-permute-done | bytes 131104 | tf_op jit(solution)/shard_map/ppermute | solution.py:37
  109.2 13.7 %all_to_all.41 = bf16[4,32,3072]{2,1,0:T(8,128)(2,1)S(1)} all-to-all(bf16[4,32,3072]{2,1,0:T(8,128)(2,1)S(1)} %bitcast.50), channel_id=1, replica_groups=mesh['zq'=2,'za'=4,'x'=4,'c'=2,'zh'=2,'y'=4] {'x'}, dimensions={0} | all-to-all | bytes 1572864 | tf_op jit(solution)/shard_map/all_to_all | solution.py:24
  123.7 12.1 %all_to_all.42 = bf16[4,8,3072]{2,1,0:T(8,128)(2,1)S(1)} all-to-all(bf16[4,8,3072]{2,1,0:T(8,128)(2,1)} %bitcast.52), channel_id=1, replica_groups=mesh['zq'=2,'za'=4,'x'=4,'c'=2,'zh'=2,'y'=4] {'za'}, dimensions={0} | all-to-all | bytes 393216 | tf_op jit(solution)/shard_map/all_to_all | solution.py:24
  138.7 5.1 %collective-permute-start.8 = (bf16[768,512]{1,0:T(8,128)(2,1)S(1)}, bf16[768,512]{1,0:T(8,128)(2,1)S(1)}, u32[]{:S(2)}, u32[]{:S(2)}) collective-permute-start(bf16[768,512]{1,0:T(8,128)(2,1)S(1)} %bitcast.48), channel_id=1, source_target_pairs={{0,8},{8,0},{1,9},{9,1},{2,10},{10,2},{3,11},{11,3},{4,12},{12,4},... | collective-permute-start | bytes 2359304 | tf_op jit(solution)/shard_map/ppermute | solution.py:37
  143.8 6.1 %collective-permute-start.11 = (bf16[128,512]{1,0:T(8,128)(2,1)S(1)}, bf16[128,512]{1,0:T(8,128)(2,1)}, u32[]{:S(2)}, u32[]{:S(2)}) collective-permute-start(bf16[128,512]{1,0:T(8,128)(2,1)S(1)} %multiply_convert_fusion.1), channel_id=1, source_target_pairs={{0,3},{1,0},{2,1},{3,2},{4,7},{5,4},{6,5},{7,6},{8,11},{9,8},{10,9... | collective-permute-start | bytes 393224 | tf_op jit(solution)/shard_map/ppermute | solution.py:37
  149.9 1.9 collective-permute-start.10
  151.8 2.5 %collective-permute-start.9 = (bf16[128,512]{1,0:T(8,128)(2,1)S(1)}, bf16[128,512]{1,0:T(8,128)(2,1)}, u32[]{:S(2)}, u32[]{:S(2)}) collective-permute-start(bf16[128,512]{1,0:T(8,128)(2,1)S(1)} %multiply_convert_fusion.1), channel_id=1, source_target_pairs={{0,1},{1,2},{2,3},{3,0},{4,5},{5,6},{6,7},{7,4},{8,9},{9,10},{10,1... | collective-permute-start | bytes 393224 | tf_op jit(solution)/shard_map/ppermute | solution.py:37
  155.1 4.0 %all-to-all-start.6 = ((bf16[4,8,3072]{2,1,0:T(8,128)(2,1)}), bf16[4,8,3072]{2,1,0:T(8,128)(2,1)}, u32[]{:S(2)}, u32[]{:S(2)}) async-start(bf16[4,8,3072]{2,1,0:T(8,128)(2,1)} %broadcast_in_dim.31), calls=%async_computation.6 | async-start | bytes 393216 | tf_op jit(solution)/shard_map/all_to_all | solution.py:24
  159.1 2.5 %collective-permute-done.9 = bf16[128,512]{1,0:T(8,128)(2,1)} collective-permute-done((bf16[128,512]{1,0:T(8,128)(2,1)S(1)}, bf16[128,512]{1,0:T(8,128)(2,1)}, u32[]{:S(2)}, u32[]{:S(2)}) %collective-permute-start.9) | collective-permute-done | bytes 131104 | tf_op jit(solution)/shard_map/ppermute | solution.py:37
  164.3 11.4 %all-gather = bf16[16,8,3072]{2,1,0:T(8,128)(2,1)S(1)} all-gather(bf16[4,8,3072]{2,1,0:T(8,128)(2,1)} %all-to-all-done.6), channel_id=2, replica_groups=mesh['zq'=2,'za'=4,'x'=4,'c'=2,'zh'=2,'y'=4] {'x'}, dimensions={0}, use_global_device_ids=true | all-gather | bytes 983040 | tf_op jit(solution)/shard_map/all_gather | solution.py:126
  177.1 8.2 %collective-permute-start.7 = (bf16[128,512]{1,0:T(8,128)(2,1)S(1)}, bf16[128,512]{1,0:T(8,128)(2,1)S(1)}, u32[]{:S(2)}, u32[]{:S(2)}) collective-permute-start(bf16[128,512]{1,0:T(8,128)(2,1)S(1)} %convert_element_type.89), channel_id=1, source_target_pairs={{0,4},{4,0},{1,5},{5,1},{2,6},{6,2},{3,7},{7,3},{8,12},{12,8},{9,1... | collective-permute-start | bytes 393224 | tf_op jit(solution)/shard_map/ppermute | solution.py:37
  186.1 4.0 %collective-permute-start.14 = (bf16[128,768]{1,0:T(8,128)(2,1)}, bf16[128,768]{1,0:T(8,128)(2,1)}, u32[]{:S(2)}, u32[]{:S(2)}) collective-permute-start(bf16[128,768]{1,0:T(8,128)(2,1)} %get-tuple-element.49), channel_id=1, source_target_pairs={{0,3},{1,0},{2,1},{3,2},{4,7},{5,4},{6,5},{7,6},{8,11},{9,8},{10,9... | collective-permute-start | bytes 589832 | tf_op jit(solution)/shard_map/ppermute | solution.py:37
  190.1 3.1 %collective-permute-start.13 = (bf16[128,768]{1,0:T(8,128)(2,1)}, bf16[128,768]{1,0:T(8,128)(2,1)}, u32[]{:S(2)}, u32[]{:S(2)}) collective-permute-start(bf16[128,768]{1,0:T(8,128)(2,1)} %get-tuple-element.50), channel_id=1, source_target_pairs={{0,2},{1,3},{2,0},{3,1},{4,6},{5,7},{6,4},{7,5},{8,10},{9,11},{10,... | collective-permute-start | bytes 589832 | tf_op jit(solution)/shard_map/ppermute | solution.py:37
  193.3 2.1 collective-permute-start.12
  196.4 14.9 %all-to-all-start.7 = ((bf16[8,128,256]{2,1,0:T(8,128)(2,1)}), bf16[8,128,256]{2,1,0:T(8,128)(2,1)S(1)}, u32[]{:S(2)}, u32[]{:S(2)}) async-start(bf16[8,128,256]{2,1,0:T(8,128)(2,1)} %bitcast.19), calls=%async_computation.7 | async-start | bytes 1048576 | tf_op jit(solution)/shard_map/all_to_all | solution.py:24
  211.4 2.3 fusion.3
  213.6 2.0 collective-permute-start.15
  215.7 2.5 %convolution_multiply_fusion.1 = f32[256,768]{1,0:T(8,128)} fusion(bf16[512,512]{1,0:T(8,128)(2,1)S(1)} %copy-done.9, bf16[128,768]{1,0:T(8,128)(2,1)} %collective-permute-done.14, bf16[128,768]{1,0:T(8,128)(2,1)} %collective-permute-done.13, bf16[128,768]{1,0:T(8,128)(2,1)} %collective-permute-done.12, bf16[128,768]{1,0:T(8,128)(2,1)} %copy-done.14), kind=kOutput, calls=%fused_computation.7 | convolution fusion | flops 204668928 | bytes 1835008 | tf_op jit(solution)/shard_map/tf,td->fd/dot_general | solution.py:153
  218.2 2.5 %all-to-all-done.7 = bf16[8,128,256]{2,1,0:T(8,128)(2,1)S(1)} async-done(((bf16[8,128,256]{2,1,0:T(8,128)(2,1)}), bf16[8,128,256]{2,1,0:T(8,128)(2,1)S(1)}, u32[]{:S(2)}, u32[]{:S(2)}) %all-to-all-start.7) | async-done | bytes 524320 | tf_op jit(solution)/shard_map/all_to_all | solution.py:24
  220.7 2.9 %multiply_add_fusion.1 = (f32[768,256]{1,0:T(8,128)}, bf16[768,256]{1,0:T(8,128)(2,1)}) fusion(bf16[768,256]{1,0:T(8,128)(2,1)S(1)} %copy-done.4, f32[768,256]{1,0:T(8,128)} %param.11, bf16[768,1024]{1,0:T(8,128)(2,1)S(1)} %pad_maximum_fusion.1, bf16[1024,256]{1,0:T(8,128)(2,1)S(1)} %bitcast.51), kind=kOutput, calls=%fused_computation.16 | convolution fusion | flops 404226048 | bytes 4456448 | tf_op jit(solution)/shard_map/dot_general | solution.py:58
  (92 shorter events, 26.8 us)
Async XLA Ops:
  25.2 6.0 %copy-start.3 = (bf16[768,256]{1,0:T(8,128)(2,1)S(1)}, bf16[768,256]{1,0:T(8,128)(2,1)}, u32[]{:S(2)}) copy-start(bf16[768,256]{1,0:T(8,128)(2,1)} %param.9) | copy-start | bytes 1179652
  25.2 12.9 %copy-start.5 = (bf16[256,768]{1,0:T(8,128)(2,1)S(1)}, bf16[256,768]{1,0:T(8,128)(2,1)}, u32[]{:S(2)}) copy-start(bf16[256,768]{1,0:T(8,128)(2,1)} %param.10) | copy-start | bytes 1179652
  25.2 19.5 %copy-start.15 = (bf16[16,768]{1,0:T(8,128)(2,1)S(1)}, bf16[16,768]{1,0:T(8,128)(2,1)}, u32[]{:S(2)}) copy-start(bf16[16,768]{1,0:T(8,128)(2,1)} %param.7) | copy-start | bytes 73732
  25.2 19.6 %copy-start.16 = (bf16[16,768]{1,0:T(8,128)(2,1)S(1)}, bf16[16,768]{1,0:T(8,128)(2,1)}, u32[]{:S(2)}) copy-start(bf16[16,768]{1,0:T(8,128)(2,1)} %param.8) | copy-start | bytes 73732
  27.2 37.5 %all-to-all-start.1 = ((bf16[4,128,768]{2,1,0:T(8,128)(2,1)}), bf16[4,128,768]{2,1,0:T(8,128)(2,1)S(1)}, u32[]{:S(2)}, u32[]{:S(2)}) async-start(bf16[4,128,768]{2,1,0:T(8,128)(2,1)} %broadcast_in_dim.28), calls=%async_computation.1 | async-start | bytes 1572864 | tf_op jit(solution)/shard_map/all_to_all | solution.py:24
  31.2 17.2 %collective-permute-start = (bf16[768,256]{1,0:T(8,128)(2,1)S(1)}, bf16[768,256]{1,0:T(8,128)(2,1)}, u32[]{:S(2)}, u32[]{:S(2)}) collective-permute-start(bf16[768,256]{1,0:T(8,128)(2,1)S(1)} %copy-done.3), channel_id=1, source_target_pairs={{0,8},{8,0},{1,9},{9,1},{2,10},{10,2},{3,11},{11,3},{4,12},{12,4},... | collective-permute-start | bytes 1179656 | tf_op jit(solution)/shard_map/ppermute | solution.py:37
  38.2 21.4 %collective-permute-start.1 = (bf16[256,768]{1,0:T(8,128)(2,1)S(1)}, bf16[256,768]{1,0:T(8,128)(2,1)S(1)}, u32[]{:S(2)}, u32[]{:S(2)}) collective-permute-start(bf16[256,768]{1,0:T(8,128)(2,1)S(1)} %copy-done.5), channel_id=1, source_target_pairs={{0,3},{1,0},{2,1},{3,2},{4,7},{5,4},{6,5},{7,6},{8,11},{9,8},{10,9... | collective-permute-start | bytes 1179656 | tf_op jit(solution)/shard_map/ppermute | solution.py:37
  42.8 21.9 %collective-permute-start.2 = (bf16[256,768]{1,0:T(8,128)(2,1)S(1)}, bf16[256,768]{1,0:T(8,128)(2,1)S(1)}, u32[]{:S(2)}, u32[]{:S(2)}) collective-permute-start(bf16[256,768]{1,0:T(8,128)(2,1)S(1)} %copy-done.5), channel_id=1, source_target_pairs={{0,1},{1,2},{2,3},{3,0},{4,5},{5,6},{6,7},{7,4},{8,9},{9,10},{10,1... | collective-permute-start | bytes 1179656 | tf_op jit(solution)/shard_map/ppermute | solution.py:37
  44.8 27.4 %collective-permute-start.3 = (bf16[256,768]{1,0:T(8,128)(2,1)S(1)}, bf16[256,768]{1,0:T(8,128)(2,1)}, u32[]{:S(2)}, u32[]{:S(2)}) collective-permute-start(bf16[256,768]{1,0:T(8,128)(2,1)S(1)} %copy-done.5), channel_id=1, source_target_pairs={{0,2},{1,3},{2,0},{3,1},{4,6},{5,7},{6,4},{7,5},{8,10},{9,11},{10,... | collective-permute-start | bytes 1179656 | tf_op jit(solution)/shard_map/ppermute | solution.py:37
  66.9 11.6 %all-to-all-start.2 = ((bf16[4,128,512]{2,1,0:T(8,128)(2,1)}), bf16[4,128,512]{2,1,0:T(8,128)(2,1)S(1)}, u32[]{:S(2)}, u32[]{:S(2)}) async-start(bf16[4,128,512]{2,1,0:T(8,128)(2,1)} %bitcast.5), calls=%async_computation.2 | async-start | bytes 1048576 | tf_op jit(solution)/shard_map/all_to_all | solution.py:24
  78.5 7.6 %all-to-all-start.3 = ((bf16[4,2,4,768]{3,2,1,0:T(4,128)(2,1)}), bf16[4,2,4,768]{3,2,1,0:T(4,128)(2,1)S(1)}, u32[]{:S(2)}, u32[]{:S(2)}) async-start(bf16[4,2,4,768]{3,2,1,0:T(4,128)(2,1)} %pad_maximum_fusion.8), calls=%async_computation.3 | async-start | bytes 98304 | tf_op jit(solution)/shard_map/all_to_all | solution.py:24
  81.8 26.2 %collective-permute-start.5 = (bf16[256,3072]{1,0:T(8,128)(2,1)S(1)}, bf16[256,3072]{1,0:T(8,128)(2,1)S(1)}, u32[]{:S(2)}, u32[]{:S(2)}) collective-permute-start(bf16[256,3072]{1,0:T(8,128)(2,1)S(1)} %pad_maximum_fusion), channel_id=1, source_target_pairs={{0,8},{8,0},{1,9},{9,1},{2,10},{10,2},{3,11},{11,3},{4,12},{12,4},... | collective-permute-start | bytes 4718600 | tf_op jit(solution)/shard_map/ppermute | solution.py:37
  86.2 20.7 %collective-permute-start.4 = (bf16[128,512]{1,0:T(8,128)(2,1)S(1)}, bf16[128,512]{1,0:T(8,128)(2,1)S(1)}, u32[]{:S(2)}, u32[]{:S(2)}) collective-permute-start(bf16[128,512]{1,0:T(8,128)(2,1)S(1)} %convert_element_type.79), channel_id=1, source_target_pairs={{0,4},{4,0},{1,5},{5,1},{2,6},{6,2},{3,7},{7,3},{8,12},{12,8},{9,1... | collective-permute-start | bytes 393224 | tf_op jit(solution)/shard_map/ppermute | solution.py:37
  109.2 29.4 %copy-start.2 = (bf16[512,768]{0,1:T(8,128)(2,1)S(1)}, bf16[512,768]{0,1:T(8,128)(2,1)}, u32[]{:S(2)}) copy-start(bf16[512,768]{0,1:T(8,128)(2,1)} %copy.19) | copy-start | bytes 2359300
  136.7 17.6 %collective-permute-start.6 = (bf16[8,3072]{1,0:T(8,128)(2,1)S(1)}, bf16[8,3072]{1,0:T(8,128)(2,1)S(1)}, u32[]{:S(2)}, u32[]{:S(2)}) collective-permute-start(bf16[8,3072]{1,0:T(8,128)(2,1)S(1)} %get-tuple-element.40), channel_id=1, source_target_pairs={{0,256},{256,0},{1,257},{257,1},{2,258},{258,2},{3,259},{259,3},{4... | collective-permute-start | bytes 147464 | tf_op jit(solution)/shard_map/ppermute | solution.py:37
  138.7 24.8 %collective-permute-start.8 = (bf16[768,512]{1,0:T(8,128)(2,1)S(1)}, bf16[768,512]{1,0:T(8,128)(2,1)S(1)}, u32[]{:S(2)}, u32[]{:S(2)}) collective-permute-start(bf16[768,512]{1,0:T(8,128)(2,1)S(1)} %bitcast.48), channel_id=1, source_target_pairs={{0,8},{8,0},{1,9},{9,1},{2,10},{10,2},{3,11},{11,3},{4,12},{12,4},... | collective-permute-start | bytes 2359304 | tf_op jit(solution)/shard_map/ppermute | solution.py:37
  143.8 15.3 %collective-permute-start.11 = (bf16[128,512]{1,0:T(8,128)(2,1)S(1)}, bf16[128,512]{1,0:T(8,128)(2,1)}, u32[]{:S(2)}, u32[]{:S(2)}) collective-permute-start(bf16[128,512]{1,0:T(8,128)(2,1)S(1)} %multiply_convert_fusion.1), channel_id=1, source_target_pairs={{0,3},{1,0},{2,1},{3,2},{4,7},{5,4},{6,5},{7,6},{8,11},{9,8},{10,9... | collective-permute-start | bytes 393224 | tf_op jit(solution)/shard_map/ppermute | solution.py:37
  149.9 9.2 %collective-permute-start.10 = (bf16[128,512]{1,0:T(8,128)(2,1)S(1)}, bf16[128,512]{1,0:T(8,128)(2,1)}, u32[]{:S(2)}, u32[]{:S(2)}) collective-permute-start(bf16[128,512]{1,0:T(8,128)(2,1)S(1)} %multiply_convert_fusion.1), channel_id=1, source_target_pairs={{0,2},{1,3},{2,0},{3,1},{4,6},{5,7},{6,4},{7,5},{8,10},{9,11},{10,... | collective-permute-start | bytes 393224 | tf_op jit(solution)/shard_map/ppermute | solution.py:37
  151.8 9.7 %collective-permute-start.9 = (bf16[128,512]{1,0:T(8,128)(2,1)S(1)}, bf16[128,512]{1,0:T(8,128)(2,1)}, u32[]{:S(2)}, u32[]{:S(2)}) collective-permute-start(bf16[128,512]{1,0:T(8,128)(2,1)S(1)} %multiply_convert_fusion.1), channel_id=1, source_target_pairs={{0,1},{1,2},{2,3},{3,0},{4,5},{5,6},{6,7},{7,4},{8,9},{9,10},{10,1... | collective-permute-start | bytes 393224 | tf_op jit(solution)/shard_map/ppermute | solution.py:37
  155.1 9.3 %all-to-all-start.6 = ((bf16[4,8,3072]{2,1,0:T(8,128)(2,1)}), bf16[4,8,3072]{2,1,0:T(8,128)(2,1)}, u32[]{:S(2)}, u32[]{:S(2)}) async-start(bf16[4,8,3072]{2,1,0:T(8,128)(2,1)} %broadcast_in_dim.31), calls=%async_computation.6 | async-start | bytes 393216 | tf_op jit(solution)/shard_map/all_to_all | solution.py:24
  164.3 12.0 %copy-start.1 = (bf16[256,3072]{1,0:T(8,128)(2,1)S(1)}, bf16[256,3072]{1,0:T(8,128)(2,1)}, u32[]{:S(2)}) copy-start(bf16[256,3072]{1,0:T(8,128)(2,1)} %copy-done) | copy-start | bytes 4718596
  177.0 18.3 %copy-start.11 = (bf16[128,512]{1,0:T(8,128)(2,1)S(1)}, bf16[128,512]{1,0:T(8,128)(2,1)}, u32[]{:S(2)}) copy-start(bf16[128,512]{1,0:T(8,128)(2,1)} %copy-done.10) | copy-start | bytes 393220
  177.1 18.2 %collective-permute-start.7 = (bf16[128,512]{1,0:T(8,128)(2,1)S(1)}, bf16[128,512]{1,0:T(8,128)(2,1)S(1)}, u32[]{:S(2)}, u32[]{:S(2)}) collective-permute-start(bf16[128,512]{1,0:T(8,128)(2,1)S(1)} %convert_element_type.89), channel_id=1, source_target_pairs={{0,4},{4,0},{1,5},{5,1},{2,6},{6,2},{3,7},{7,3},{8,12},{12,8},{9,1... | collective-permute-start | bytes 393224 | tf_op jit(solution)/shard_map/ppermute | solution.py:37
  186.1 25.2 %copy-start.14 = (bf16[128,768]{1,0:T(8,128)(2,1)}, bf16[128,768]{1,0:T(8,128)(2,1)S(1)}, u32[]{:S(2)}) copy-start(bf16[128,768]{1,0:T(8,128)(2,1)S(1)} %get-tuple-element.48) | copy-start | bytes 589828
  186.1 25.2 %collective-permute-start.14 = (bf16[128,768]{1,0:T(8,128)(2,1)}, bf16[128,768]{1,0:T(8,128)(2,1)}, u32[]{:S(2)}, u32[]{:S(2)}) collective-permute-start(bf16[128,768]{1,0:T(8,128)(2,1)} %get-tuple-element.49), channel_id=1, source_target_pairs={{0,3},{1,0},{2,1},{3,2},{4,7},{5,4},{6,5},{7,6},{8,11},{9,8},{10,9... | collective-permute-start | bytes 589832 | tf_op jit(solution)/shard_map/ppermute | solution.py:37
  190.1 21.2 %collective-permute-start.13 = (bf16[128,768]{1,0:T(8,128)(2,1)}, bf16[128,768]{1,0:T(8,128)(2,1)}, u32[]{:S(2)}, u32[]{:S(2)}) collective-permute-start(bf16[128,768]{1,0:T(8,128)(2,1)} %get-tuple-element.50), channel_id=1, source_target_pairs={{0,2},{1,3},{2,0},{3,1},{4,6},{5,7},{6,4},{7,5},{8,10},{9,11},{10,... | collective-permute-start | bytes 589832 | tf_op jit(solution)/shard_map/ppermute | solution.py:37
  193.2 18.1 %copy-start.9 = (bf16[512,512]{1,0:T(8,128)(2,1)S(1)}, bf16[512,512]{1,0:T(8,128)(2,1)}, u32[]{:S(2)}) copy-start(bf16[512,512]{1,0:T(8,128)(2,1)} %pad_maximum_fusion.4) | copy-start | bytes 1572868
  193.3 18.1 %collective-permute-start.12 = (bf16[128,768]{1,0:T(8,128)(2,1)S(1)}, bf16[128,768]{1,0:T(8,128)(2,1)}, u32[]{:S(2)}, u32[]{:S(2)}) collective-permute-start(bf16[128,768]{1,0:T(8,128)(2,1)S(1)} %get-tuple-element.51), channel_id=1, source_target_pairs={{0,1},{1,2},{2,3},{3,0},{4,5},{5,6},{6,7},{7,4},{8,9},{9,10},{10,1... | collective-permute-start | bytes 589832 | tf_op jit(solution)/shard_map/ppermute | solution.py:37
  196.4 24.3 %all-to-all-start.7 = ((bf16[8,128,256]{2,1,0:T(8,128)(2,1)}), bf16[8,128,256]{2,1,0:T(8,128)(2,1)S(1)}, u32[]{:S(2)}, u32[]{:S(2)}) async-start(bf16[8,128,256]{2,1,0:T(8,128)(2,1)} %bitcast.19), calls=%async_computation.7 | async-start | bytes 1048576 | tf_op jit(solution)/shard_map/all_to_all | solution.py:24
  213.6 7.0 %copy-start.4 = (bf16[768,256]{1,0:T(8,128)(2,1)S(1)}, bf16[768,256]{1,0:T(8,128)(2,1)}, u32[]{:S(2)}) copy-start(bf16[768,256]{1,0:T(8,128)(2,1)} %param.9) | copy-start | bytes 1179652
  213.6 9.9 %collective-permute-start.15 = (bf16[256,768]{1,0:T(8,128)(2,1)}, bf16[256,768]{1,0:T(8,128)(2,1)}, u32[]{:S(2)}, u32[]{:S(2)}) collective-permute-start(bf16[256,768]{1,0:T(8,128)(2,1)} %fusion.3), channel_id=1, source_target_pairs={{0,8},{8,0},{1,9},{9,1},{2,10},{10,2},{3,11},{11,3},{4,12},{12,4},... | collective-permute-start | bytes 1179656 | tf_op jit(solution)/shard_map/ppermute | solution.py:37
  220.7 4.0 %copy-start.8 = (f32[256,768]{1,0:T(8,128)S(1)}, f32[256,768]{1,0:T(8,128)}, u32[]{:S(2)}) copy-start(f32[256,768]{1,0:T(8,128)} %convolution_multiply_fusion.1) | copy-start | bytes 2359300
  (6 other events, 9.1 us)
